TPU v7x, 128 devices: a whole 4x4x4 slice. The times are simulated.
128 devices in a mesh: seq: 64 (over y_lo, x, z, core), ch: 2 (over y_hi).
Axes of the slice: x: 4, y: 4 (y_hi: 2, y_lo: 2; y = y_hi * 2 + y_lo), z: 4, core: 2. Of those that a mesh axis runs over, the one named last changes fastest.
Arguments:
- out_grad: bfloat16 [8192, 4096], P('seq', 'ch'), may hold values from -6 to 6
- out_weight: bfloat16 [4096, 4096], P(('seq', 'ch')), may hold values from -0.09375 to 0.09375
- outer_gate: bfloat16 [8192, 4096], P('seq', 'ch'), may hold values from -6 to 6
- long_out: bfloat16 [8192, 4096], P('seq', 'ch'), may hold values from -6 to 6
- inner_gate: bfloat16 [8192, 4096], P('seq', 'ch'), may hold values from -6 to 6
- conv_input: bfloat16 [8192, 4096], P('seq', 'ch'), may hold values from -6 to 6
- short_out: bfloat16 [8192, 4096], P('seq', 'ch'), may hold values from -6 to 6
- medium_out: bfloat16 [8192, 4096], P('seq', 'ch'), may hold values from -6 to 6
- long_filter: bfloat16 [8192, 4096], P('seq', 'ch'), may hold values from -6 to 6
- taps_short: bfloat16 [7, 4096], P(None, 'ch'), may hold values from -2 to 2
- taps_medium: bfloat16 [128, 4096], P(None, 'ch'), may hold values from -0.5 to 0.5
Outputs:
- grad_outer: bfloat16 [8192, 4096], P('seq', 'ch')
- grad_inner: bfloat16 [8192, 4096], P('seq', 'ch')
- grad_input: bfloat16 [8192, 4096], P('seq', 'ch')
- grad_filter: float32 [8192, 4096], P('seq', 'ch')
- grad_short: float32 [7, 4096], P(None, 'ch')
- grad_medium: float32 [128, 4096], P(None, 'ch')
All inputs are finite; a program needn't handle non-finite values.
Results may differ from a plain program's by a relative error of at most 0.0065.
Values may be sent and summed in bfloat16 or wider, within the bound.
A program may use at most 128 MiB of HBM per device.

v0:
```python
import math

import jax
import jax.numpy as jnp
from jax import lax
from jax.sharding import PartitionSpec as P

SHORT = 7
MEDIUM = 128


ACCURATE = lax.Precision.HIGH


def from_behind(value, axis, steps):
    count = lax.axis_size(axis)
    leading, last = (max(0, -steps), min(count, count - steps))
    return lax.ppermute(value, axis, [(source, source + steps) for source in range(leading, last)])


def in_order(parts, dim):
    parts = jnp.moveaxis(parts, 0, dim)
    shape = parts.shape
    return parts.reshape(*shape[:dim], shape[dim] * shape[dim + 1], *shape[dim + 2 :])


def sent_to_all(x, axis):
    size = lax.axis_size(axis)
    return lax.all_to_all(jnp.broadcast_to(x[None], (size, *x.shape)), axis, 0, 0, tiled=True)


def gathered_copies(x, axis, dim):
    return in_order(sent_to_all(x, axis), dim)


def side_by_side(arrays, axis, split_dim, concat_dim, along):
    ends, at = ([], 0)
    for a in arrays[:-1]:
        at += a.shape[along]
        ends.append(at)
    both = jnp.concatenate(arrays, axis=along)
    return tuple(
        jnp.split(
            lax.all_to_all(both, axis, split_axis=split_dim, concat_axis=concat_dim, tiled=True),
            ends,
            axis=along,
        )
    )


def padded_to(lines, size):
    spare = -lines.shape[0] % size
    if not spare:
        return lines
    return jnp.concatenate([lines, jnp.zeros((spare, *lines.shape[1:]), lines.dtype)])


def cut_along(x, dim, size):
    before, after = (x.shape[:dim], x.shape[dim + 1 :])
    return jnp.moveaxis(x.reshape(*before, size, -1, *after), dim, 0)


def summed_on_arrival(x, axis, dim):
    size = lax.axis_size(axis)
    parts = lax.all_to_all(cut_along(x, dim, size), axis, 0, 0, tiled=True)
    return jnp.sum(parts.astype(jnp.float32), axis=0)


def total_of(x, axes):
    lines = x.reshape(-1)
    padded = padded_to(lines, lax.axis_size(axes))
    whole = gathered_copies(summed_on_arrival(padded, axes, 0).astype(jnp.bfloat16), axes, 0)
    return lax.slice_in_dim(whole, 0, len(lines)).reshape(x.shape).astype(jnp.float32)


def rotation(numer, denom):
    angles = 2.0 * math.pi / denom * numer.astype(jnp.float32)
    return (jnp.cos(angles), jnp.sin(angles))


def dft_table(length, orient):
    indices = lax.iota(jnp.int32, length)
    cosine, sine_part = rotation(indices[:, None] * indices[None, :] % length, length)
    return (cosine, orient * sine_part)


def apply_table(table, real_part, imag_part, pattern):

    def multiply(left, right):
        return jnp.einsum(pattern, left, right, precision=ACCURATE)

    if imag_part is None:
        return (multiply(table[0], real_part), multiply(table[1], real_part))
    return (
        multiply(table[0], real_part) - multiply(table[1], imag_part),
        multiply(table[0], imag_part) + multiply(table[1], real_part),
    )


def real_table(table, real_part, imag_part, pattern):
    return jnp.einsum(pattern, table[0], real_part, precision=ACCURATE) - jnp.einsum(
        pattern, table[1], imag_part, precision=ACCURATE
    )


def twist(real_part, imag_part, cosine, sine_part):
    return (real_part * cosine - imag_part * sine_part, real_part * sine_part + imag_part * cosine)


def outer_forward(signal, time_pos, row_pos, freq_pos, total):
    table = dft_table(signal.shape[0], -1.0)
    cosine, sine_part = rotation(time_pos, 2 * total)
    shift_real, shift_imag = rotation(row_pos * freq_pos % total, total)
    outputs = []
    for parity in range(2):
        if parity == 0:
            real_part, imag_part = apply_table(table, signal, None, "ca,am->cm")
        else:
            real_part, imag_part = apply_table(
                table, signal * cosine, -signal * sine_part, "ca,am->cm"
            )
        outputs += list(twist(real_part, imag_part, shift_real, -shift_imag))
    return outputs


def inner_forward(parts):
    table = dft_table(parts[0].shape[0], -1.0)
    outputs = []
    for place in range(0, len(parts), 2):
        outputs += list(apply_table(table, parts[place], parts[place + 1], "br,rn->bn"))
    return outputs


def inner_inverse(parts, narrow, total):
    table = dft_table(parts[0].shape[0], 1.0)
    row_pos = lax.iota(jnp.int32, parts[0].shape[0])[:, None]
    freq_pos = lax.iota(jnp.int32, parts[0].shape[1])[None, :] // narrow
    shift_real, shift_imag = rotation(row_pos * freq_pos % total, total)
    outputs = []
    for place in range(0, len(parts), 2):
        real_part, imag_part = apply_table(table, parts[place], parts[place + 1], "rb,bn->rn")
        outputs += list(twist(real_part, imag_part, shift_real, shift_imag))
    return outputs


def outer_inverse(parts, time_pos, total):
    table = dft_table(parts[0].shape[0], 1.0)
    cosine, sine_part = rotation(time_pos, 2 * total)
    outputs = []
    for place in range(0, len(parts), 4):
        high_real, high_imag = apply_table(table, parts[place + 2], parts[place + 3], "ac,cm->am")
        high_real, high_imag = twist(high_real, high_imag, cosine, sine_part)
        outputs.append(real_table(table, parts[place], parts[place + 1], "ac,cm->am") + high_real)
    return outputs


def conj_times(left_real, left_imag, right_real, right_imag):
    return (
        left_real * right_real + left_imag * right_imag,
        left_real * right_imag - left_imag * right_real,
    )


def spectral_terms(spectra):
    first, second = ([], [])
    for parity in range(2):
        grad_real, grad_imag = (spectra[4 + 2 * parity], spectra[5 + 2 * parity])
        point_real, point_imag = conj_times(
            spectra[8 + 2 * parity], spectra[9 + 2 * parity], grad_real, grad_imag
        )
        filt_real, filt_imag = conj_times(
            spectra[2 * parity], spectra[2 * parity + 1], grad_real, grad_imag
        )
        first += [point_real, point_imag]
        second += [filt_real, filt_imag]
    return first + second


def depthwise(signal, kernel):
    channels = signal.shape[1]
    result = lax.conv_general_dilated(
        signal.astype(jnp.float32)[None],
        kernel.astype(jnp.float32)[:, None, :],
        (1,),
        "VALID",
        dimension_numbers=("NWC", "WIO", "NWC"),
        feature_group_count=channels,
        precision=lax.Precision.HIGHEST,
    )
    return result[0]


def adjoint_taps(extended, taps):
    return depthwise(extended, taps)


def tap_products(grads, extended):
    return depthwise(extended, grads)[::-1]


def per_device(
    out_grad,
    out_weight,
    outer_gate,
    long_out,
    inner_gate,
    conv_input,
    short_out,
    medium_out,
    long_filter,
    taps_short,
    taps_medium,
):
    height = out_grad.shape[0]
    channels = outer_gate.shape[1]
    devices = lax.axis_size("seq")
    total = height * devices
    earlier_short, earlier_input = from_behind(
        (short_out[height - (MEDIUM - 1) :], conv_input[height - (SHORT - 1) :]), "seq", 1
    )
    features = gathered_copies(out_grad, "ch", 1)
    aligned = lax.all_to_all(out_weight, "ch", split_axis=1, concat_axis=0, tiled=True)
    hidden = jnp.dot(
        features,
        lax.all_gather(aligned, "seq", axis=0, tiled=True),
        preferred_element_type=jnp.float32,
    )
    grad_outer = (hidden * long_out.astype(jnp.float32)).astype(jnp.bfloat16)
    long_grad = (hidden * outer_gate.astype(jnp.float32)).astype(jnp.bfloat16)
    product = (inner_gate.astype(jnp.float32) * medium_out.astype(jnp.float32)).astype(jnp.bfloat16)
    narrow = channels // devices
    lane_span = height * narrow

    def to_blocks(signal):
        return (
            signal.reshape(height, devices, narrow).transpose(1, 0, 2).reshape(devices, lane_span)
        )

    def to_inner(signal):
        return (
            signal.reshape(devices, height, narrow)
            .transpose(1, 0, 2)
            .reshape(height, devices * narrow)
        )

    arrived = side_by_side(
        (to_blocks(product), to_blocks(long_grad), to_blocks(long_filter)), "seq", 0, 0, 1
    )
    row_pos = lax.iota(jnp.int32, lane_span)[None, :] // narrow
    source = lax.iota(jnp.int32, devices)[:, None]
    time_pos = source * height + row_pos
    spread = []
    for signal in arrived:
        spread += outer_forward(signal.astype(jnp.float32), time_pos, row_pos, source, total)
    spectra = inner_forward([to_inner(piece) for piece in spread])
    terms = inner_inverse(spectral_terms(spectra), narrow, total)
    results = outer_inverse([to_blocks(piece) for piece in terms], time_pos, total)
    result = lax.all_to_all(jnp.stack(results), "seq", split_axis=1, concat_axis=1, tiled=True)
    result = (
        result.reshape(2, devices, height, narrow)
        .transpose(0, 2, 1, 3)
        .reshape(2, height, channels)
    )
    scale = total ** (-0.5) / (2.0 * total)
    point_grad = result[0] * scale
    grad_filter = result[1] * scale
    medium_grad = (point_grad * inner_gate.astype(jnp.float32)).astype(jnp.bfloat16)
    grad_inner = (point_grad * medium_out.astype(jnp.float32)).astype(jnp.bfloat16)
    later_medium = from_behind(medium_grad[: MEDIUM - 1], "seq", -1)
    short_grad = adjoint_taps(jnp.concatenate([medium_grad, later_medium]), taps_medium).astype(
        jnp.bfloat16
    )
    later_short = from_behind(short_grad[: SHORT - 1], "seq", -1)
    grad_input = adjoint_taps(jnp.concatenate([short_grad, later_short]), taps_short).astype(
        jnp.bfloat16
    )
    partial_medium = tap_products(medium_grad, jnp.concatenate([earlier_short, short_out]))
    partial_short = tap_products(short_grad, jnp.concatenate([earlier_input, conv_input]))
    sum_medium, sum_short = (
        total_of(partial_medium.astype(jnp.bfloat16), "seq"),
        total_of(partial_short.astype(jnp.bfloat16), "seq"),
    )
    factor = total ** (-0.5)
    return (
        grad_outer,
        grad_inner,
        grad_input,
        grad_filter,
        sum_short * factor,
        sum_medium * factor,
    )


def solution(mesh):
    return jax.shard_map(
        per_device,
        mesh=mesh,
        in_specs=(
            P("seq", "ch"),
            P(("seq", "ch"), None),
            P("seq", "ch"),
            P("seq", "ch"),
            P("seq", "ch"),
            P("seq", "ch"),
            P("seq", "ch"),
            P("seq", "ch"),
            P("seq", "ch"),
            P(None, "ch"),
            P(None, "ch"),
        ),
        out_specs=(
            P("seq", "ch"),
            P("seq", "ch"),
            P("seq", "ch"),
            P("seq", "ch"),
            P(None, "ch"),
            P(None, "ch"),
        ),
        check_vma=False,
    )
```

profile of v0, /device:TPU:1, one launch (start us, length us, event | category | flops | bytes accessed | tf_op | source)
XLA Modules:
  0.0 697.4 jit_solution(6125251082649983839)
XLA Ops:
  8.2 10.4 %all_to_all.73 = bf16[32,2,2048]{2,0,1:T(8,128)(2,1)} all-to-all(bf16[32,2,2048]{2,0,1:T(8,128)(2,1)S(1)} %bitcast.295), channel_id=1, replica_groups=mesh['seq'=64,'ch'=2] {'ch'}, dimensions={1} | all-to-all | bytes 524288 | tf_op jit(solution)/shard_map/all_to_all | solution.py:222
  21.1 3.6 all-to-all-start
  32.0 5.8 all-to-all-done
  37.8 109.5 %all-gather.2.cloned.1.call-done = bf16[4096,2048]{1,0:T(8,128)(2,1)} async-done(((bf16[64,2048]{1,0:T(8,128)(2,1)}), bf16[4096,2048]{1,0:T(8,128)(2,1)}) %all-gather.2.cloned.1.call-update) | async-done | bytes 16777232 | tf_op jit(solution)/shard_map/all_gather | solution.py:225
  147.2 9.3 %multiply_convert_fusion = (bf16[128,2048]{1,0:T(8,128)(2,1)}, bf16[128,2048]{1,0:T(8,128)(2,1)}) fusion(bf16[128,2048]{1,0:T(8,128)(2,1)} %param.13, bf16[128,2048]{1,0:T(8,128)(2,1)} %param.14, bf16[128,4096]{0,1:T(8,128)(2,1)S(1)} %bitcast.274, bf16[4096,2048]{1,0:T(8,128)(2,1)} %all-gather.2.cloned.1.call-done), kind=kOutput, calls=%fused_computation.128 | convolution fusion | flops 2149056512 | bytes 19922944 | tf_op jit(solution)/shard_map/dot_general | solution.py:223
  158.8 3.7 copy.307
  162.5 13.1 %maximum_bitcast_fusion = bf16[64,1,12288]{0,2,1:T(8,128)(2,1)} fusion(bf16[64,4096]{0,1:T(8,128)(2,1)S(1)} %bitcast.286, bf16[64,4096]{0,1:T(8,128)(2,1)} %bitcast.288, bf16[64,4096]{0,1:T(8,128)(2,1)S(1)} %bitcast.287), kind=kLoop, calls=%fused_computation.22 | loop fusion | flops 4718592 | bytes 3145728 | tf_op jit(solution)/shard_map/all_to_all | solution.py:44
  176.1 5.6 reduce.8
  181.7 3.1 copy.397
  186.9 6.5 all-to-all-start.2
  193.4 22.6 %all-to-all-done.2 = bf16[64,2,6144]{2,1,0:T(2,128)(2,1)S(1)} async-done(((bf16[64,2,6144]{2,1,0:T(2,128)(2,1)}), bf16[64,2,6144]{2,1,0:T(2,128)(2,1)S(1)}, u32[]{:S(2)}, u32[]{:S(2)}) %all-to-all-start.2) | async-done | bytes 1572896 | tf_op jit(solution)/shard_map/all_to_all | solution.py:44
  216.1 4.1 reshape.351
  220.2 3.6 copy.391
  225.4 4.2 fusion.47
  229.6 4.4 fusion.32
  234.0 4.2 fusion.44
  238.3 4.2 fusion.33
  243.5 4.6 fusion.41
  248.2 4.2 fusion.34
  252.3 4.2 convolution_add_fusion.4
  256.5 4.4 convolution_subtract_fusion.5
  260.9 4.2 convolution_add_fusion.3
  265.1 4.2 convolution_subtract_fusion.4
  269.4 4.4 convolution_add_fusion.1
  273.8 4.2 convolution_subtract_fusion.1
  278.0 8.8 %multiply_subtract_fusion.13 = (f32[64,4096]{1,0:T(8,128)}, f32[64,4096]{1,0:T(8,128)}, f32[64,4096]{1,0:T(8,128)S(1)}, f32[64,4096]{1,0:T(8,128)S(1)}, f32[64,4...) fusion(f32[64,4096]{1,0:T(8,128)S(1)} %fusion.118, ...), kind=kOutput, calls=%fused_computation.124 | convolution fusion | flops 114094080 | bytes 24657920 | tf_op jit(solution)/shard_map/ca,am->cm/dot_general | solution.py:90
  302.4 3.2 copy.311
  310.4 3.2 copy.313
  324.2 3.1 copy.338
  347.3 3.3 copy.330
  361.1 3.2 copy.323
  369.1 3.2 copy.325
  382.8 3.6 copy.346
  410.6 7.7 %multiply_add_fusion.10 = (f32[128,2048]{1,0:T(8,128)}, f32[128,2048]{1,0:T(8,128)}, f32[128,2048]{1,0:T(8,128)}, f32[128,2048]{1,0:T(8,128)}, f32[128,2048]{1,0...) fusion(f32[128,2048]{1,0:T(8,128)S(1)} %copy-done.17, ...), kind=kOutput, calls=%fused_computation.115 | convolution fusion | flops 211779584 | bytes 17833984 | tf_op jit(solution)/shard_map/rb,bn->rn/dot_general | solution.py:90
  419.7 3.0 copy.350
  427.6 3.0 copy.348
  433.0 6.6 fusion
  442.1 3.0 copy.340
  453.4 3.0 copy.334
  461.4 3.0 copy.332
  466.8 6.3 fusion.4
  475.7 3.0 copy.320
  483.6 4.3 copy.322
  487.9 7.4 %fusion.9 = f32[64,4096]{1,0:T(8,128)S(1)} fusion(f32[64,4096]{1,0:T(8,128)} %fusion, f32[64,4096]{1,0:T(8,128)} %fusion.207, f32[64,4096]{0,1:T(8,128)S(1)} %bitcast.229, s32[64]{0:T(128)S(1)} %iota_multiply_fusion, s32[4096]{0:T(1024)S(1)} %add_select_fusion.4), kind=kOutput, calls=%fused_computation.21 | convolution fusion | flops 102293504 | bytes 4210944 | tf_op jit(solution)/shard_map/ac,cm->am/dot_general | solution.py:90
  495.4 4.6 fusion.8
  506.3 5.5 all-to-all-start.3
  513.0 3.5 collective-permute-start.3
  516.6 24.1 %collective-permute-done.3 = bf16[127,2048]{1,0:T(8,128)(2,1)S(1)} collective-permute-done((bf16[127,2048]{1,0:T(8,128)(2,1)S(1)}, bf16[127,2048]{1,0:T(8,128)(2,1)S(1)}, u32[]{:S(2)}, u32[]{:S(2)}) %collective-permute-start.3) | collective-permute-done | bytes 520224 | tf_op jit(solution)/shard_map/ppermute | solution.py:18
  542.9 3.6 copy.352
  546.5 4.5 copy.353
  556.1 16.4 %fusion.11 = bf16[1,128,2048]{2,0,1:T(2,128)(2,1)S(1)} fusion(bf16[128,1,2048]{2,1,0:T(2,128)(2,1)S(1)} %copy.365, bf16[1,255,2048]{2,1,0:T(8,128)(2,1)} %maximum_bitcast_fusion.2), kind=kOutput, calls=%fused_computation.47 | convolution fusion | flops 67108864 | bytes 2093056 | tf_op jit(solution)/shard_map/conv_general_dilated | solution.py:181
  574.4 3.9 reduce.9
  579.4 10.4 %all-to-all-start.6 = ((bf16[64,2,2048]{2,1,0:T(2,128)(2,1)}), bf16[64,2,2048]{2,1,0:T(2,128)(2,1)S(1)}, u32[]{:S(2)}, u32[]{:S(2)}) async-start(bf16[64,2,2048]{2,1,0:T(2,128)(2,1)} %reshape.352), calls=%async_computation.6 | async-start | bytes 1048576 | tf_op jit(solution)/shard_map/all_to_all | solution.py:65
  590.6 3.5 collective-permute-start.2
  604.5 3.8 reduce.10
  610.7 4.0 copy.355
  614.7 17.4 %convolution_convert_fusion = bf16[1,128,2048]{2,0,1:T(2,128)(2,1)S(1)} fusion(bf16[1,255,2048]{2,0,1:T(2,128)(2,1)} %copy.355, bf16[128,1,2048]{2,0,1:T(8,128)(2,1)S(1)} %bitcast.205), kind=kOutput, calls=%fused_computation.44 | convolution fusion | flops 67371008 | bytes 2093056 | tf_op jit(solution)/shard_map/conv_general_dilated | solution.py:181
  638.6 8.3 %all-to-all-start.4 = ((bf16[64,1,224]{2,1,0:T(2,128)(2,1)}), bf16[64,1,224]{2,1,0:T(2,128)(2,1)S(1)}, u32[]{:S(2)}, u32[]{:S(2)}) async-start(bf16[64,1,224]{2,1,0:T(2,128)(2,1)} %all_to_all.63), calls=%async_computation.4 | async-start | bytes 131072 | tf_op jit(solution)/shard_map/all_to_all | solution.py:65
  647.6 7.5 %all-to-all-done.4 = bf16[64,1,224]{2,1,0:T(2,128)(2,1)S(1)} async-done(((bf16[64,1,224]{2,1,0:T(2,128)(2,1)}), bf16[64,1,224]{2,1,0:T(2,128)(2,1)S(1)}, u32[]{:S(2)}, u32[]{:S(2)}) %all-to-all-start.4) | async-done | bytes 28704 | tf_op jit(solution)/shard_map/all_to_all | solution.py:65
  655.9 4.4 all-to-all-start.5
  661.7 7.0 all-to-all-done.5
  668.6 4.7 all-to-all-start.7
  675.1 10.3 %all-to-all-done.7 = bf16[64,2,2048]{2,1,0:T(2,128)(2,1)S(1)} async-done(((bf16[64,2,2048]{2,1,0:T(2,128)(2,1)}), bf16[64,2,2048]{2,1,0:T(2,128)(2,1)S(1)}, u32[]{:S(2)}, u32[]{:S(2)}) %all-to-all-start.7) | async-done | bytes 524320 | tf_op jit(solution)/shard_map/all_to_all | solution.py:29
  685.9 3.3 multiply_reduce_fusion
  (258 shorter events, 196.8 us)
Async XLA Ops:
  7.2 607.5 %copy-start = (bf16[128,2048]{1,0:T(8,128)(2,1)S(1)}, bf16[128,2048]{1,0:T(8,128)(2,1)}, u32[]{:S(2)}) copy-start(bf16[128,2048]{1,0:T(8,128)(2,1)} %param.21) | copy-start | bytes 1572868
  7.2 140.0 %all-gather.2.cloned.1.call-start = ((), (), s32[]{:S(2)}) async-start(), calls=%async_computation.8 | async-start | bytes 17039360 | tf_op jit(solution)/shard_map/all_gather | solution.py:225
  20.0 4.7 copy-start.53
  20.0 4.9 copy-start.54
  21.1 16.7 %all-to-all-start = ((bf16[2,128,2048]{1,2,0:T(8,128)(2,1)}), bf16[2,128,2048]{1,2,0:T(8,128)(2,1)S(1)}, u32[]{:S(2)}, u32[]{:S(2)}) async-start(bf16[2,128,2048]{1,2,0:T(8,128)(2,1)} %broadcast_in_dim.20), calls=%async_computation | async-start | bytes 2097152 | tf_op jit(solution)/shard_map/all_to_all | solution.py:29
  29.2 127.4 %copy-start.15 = (bf16[128,2048]{0,1:T(8,128)(2,1)}, bf16[128,2048]{0,1:T(8,128)(2,1)S(1)}, u32[]{:S(2)}) copy-start(bf16[128,2048]{0,1:T(8,128)(2,1)S(1)} %copy.304) | copy-start | bytes 1572868
  156.6 5.9 copy-start.35
  156.6 5.9 copy-start.36
  186.9 29.2 %all-to-all-start.2 = ((bf16[64,2,6144]{2,1,0:T(2,128)(2,1)}), bf16[64,2,6144]{2,1,0:T(2,128)(2,1)S(1)}, u32[]{:S(2)}, u32[]{:S(2)}) async-start(bf16[64,2,6144]{2,1,0:T(2,128)(2,1)} %reshape.350), calls=%async_computation.2 | async-start | bytes 3145728 | tf_op jit(solution)/shard_map/all_to_all | solution.py:44
  298.7 1.8 copy-start.27
  308.6 5.0 copy-start.11
  316.6 1.8 copy-start.28
  318.5 1.8 copy-start.24
  320.2 2.0 copy-start.50
  324.2 4.9 copy-start.49
  335.3 1.8 copy-start.42
  335.3 1.8 copy-start.44
  336.2 1.4 copy-start.12
  336.2 1.7 copy-start.38
  336.2 2.0 copy-start.40
  340.8 2.7 copy-start.5
  343.5 1.9 copy-start.48
  347.3 5.2 copy-start.47
  357.5 1.8 copy-start.30
  367.3 5.0 copy-start.9
  375.3 1.9 copy-start.31
  377.2 1.8 copy-start.25
  379.1 1.8 copy-start.46
  382.8 5.4 copy-start.45
  394.4 1.8 copy-start.41
  394.4 1.8 copy-start.43
  395.3 1.4 copy-start.10
  395.3 1.7 copy-start.37
  395.3 2.0 copy-start.39
  401.3 2.0 copy-start.8
  408.7 1.5 copy-start.17
  408.7 1.8 copy-start.22
  422.7 4.9 copy-start.1
  430.6 2.3 copy-start.20
  449.0 3.0 copy-start.23
  456.4 5.0 copy-start.3
  464.5 2.4 copy-start.21
  483.6 4.3 copy-start.2
  487.9 7.4 %copy-start.4 = (f32[64,128,32]{0,2,1:T(8,128)S(1)}, f32[64,128,32]{0,2,1:T(8,128)}, u32[]{:S(2)}) copy-start(f32[64,128,32]{0,2,1:T(8,128)} %copy-done.3) | copy-start | bytes 3145732
  487.9 7.4 %copy-start.32 = (f32[64,4096]{1,0:T(8,128)S(1)}, f32[64,4096]{1,0:T(8,128)}, u32[]{:S(2)}) copy-start(f32[64,4096]{1,0:T(8,128)} %fusion.216) | copy-start | bytes 3145732
  487.9 7.4 %copy-start.33 = (f32[64,4096]{1,0:T(8,128)S(1)}, f32[64,4096]{1,0:T(8,128)}, u32[]{:S(2)}) copy-start(f32[64,4096]{1,0:T(8,128)} %fusion.4) | copy-start | bytes 3145732
  495.3 4.6 copy-start.13
  495.3 4.6 copy-start.18
  500.0 1.6 copy-start.14
  500.0 1.8 copy-start.19
  506.3 36.5 %all-to-all-start.3 = ((f32[2,64,4096]{2,0,1:T(2,128)}), f32[2,64,4096]{2,0,1:T(2,128)S(1)}, u32[]{:S(2)}, u32[]{:S(2)}) async-start(f32[2,64,4096]{2,0,1:T(2,128)} %copy.351), calls=%async_computation.3 | async-start | bytes 4194304 | tf_op jit(solution)/shard_map/all_to_all | solution.py:258
  513.0 27.6 %collective-permute-start.3 = (bf16[127,2048]{1,0:T(8,128)(2,1)S(1)}, bf16[127,2048]{1,0:T(8,128)(2,1)S(1)}, u32[]{:S(2)}, u32[]{:S(2)}) collective-permute-start(bf16[127,2048]{1,0:T(8,128)(2,1)S(1)} %slice.29), channel_id=1, source_target_pairs={{0,2},{2,4},{4,6},{6,8},{8,10},{10,12},{12,14},{14,16},{16,18},{18... | collective-permute-start | bytes 1560584 | tf_op jit(solution)/shard_map/ppermute | solution.py:18
  553.2 56.2 %collective-permute-start = (bf16[127,2048]{0,1:T(8,128)(2,1)S(1)}, bf16[127,2048]{0,1:T(8,128)(2,1)}, u32[]{:S(2)}, u32[]{:S(2)}) collective-permute-start(bf16[127,2048]{0,1:T(8,128)(2,1)S(1)} %bitcast.275), channel_id=1, source_target_pairs={{2,0},{4,2},{6,4},{8,6},{10,8},{12,10},{14,12},{16,14},{18,16},{20... | collective-permute-start | bytes 1560584 | tf_op jit(solution)/shard_map/ppermute | solution.py:18
  574.3 23.3 %copy-start.51 = (bf16[128,2048]{0,1:T(8,128)(2,1)S(1)}, bf16[128,2048]{0,1:T(8,128)(2,1)}, u32[]{:S(2)}) copy-start(bf16[128,2048]{0,1:T(8,128)(2,1)} %get-tuple-element.71) | copy-start | bytes 1572868
  578.2 20.4 %copy-start.34 = (f32[1,128,64,32]{1,3,2,0:T(8,128)S(1)}, f32[1,128,64,32]{1,3,2,0:T(8,128)}, u32[]{:S(2)}) copy-start(f32[1,128,64,32]{1,3,2,0:T(8,128)} %get-tuple-element.64) | copy-start | bytes 3145732
  579.4 22.3 %all-to-all-start.6 = ((bf16[64,2,2048]{2,1,0:T(2,128)(2,1)}), bf16[64,2,2048]{2,1,0:T(2,128)(2,1)S(1)}, u32[]{:S(2)}, u32[]{:S(2)}) async-start(bf16[64,2,2048]{2,1,0:T(2,128)(2,1)} %reshape.352), calls=%async_computation.6 | async-start | bytes 1048576 | tf_op jit(solution)/shard_map/all_to_all | solution.py:65
  590.6 5.1 collective-permute-start.2
  614.7 19.9 %copy-start.52 = (bf16[1,134,2048]{2,1,0:T(8,128)(2,1)S(1)}, bf16[1,134,2048]{2,1,0:T(8,128)(2,1)}, u32[]{:S(2)}) copy-start(bf16[1,134,2048]{2,1,0:T(8,128)(2,1)} %maximum_bitcast_fusion.4) | copy-start | bytes 1646596
  632.2 14.7 %collective-permute-start.1 = (bf16[6,2048]{1,0:T(8,128)(2,1)S(1)}, bf16[6,2048]{1,0:T(8,128)(2,1)S(1)}, u32[]{:S(2)}, u32[]{:S(2)}) collective-permute-start(bf16[6,2048]{1,0:T(8,128)(2,1)S(1)} %bitcast.298), channel_id=1, source_target_pairs={{2,0},{4,2},{6,4},{8,6},{10,8},{12,10},{14,12},{16,14},{18,16},{20... | collective-permute-start | bytes 73736 | tf_op jit(solution)/shard_map/ppermute | solution.py:18
  638.6 16.5 %all-to-all-start.4 = ((bf16[64,1,224]{2,1,0:T(2,128)(2,1)}), bf16[64,1,224]{2,1,0:T(2,128)(2,1)S(1)}, u32[]{:S(2)}, u32[]{:S(2)}) async-start(bf16[64,1,224]{2,1,0:T(2,128)(2,1)} %all_to_all.63), calls=%async_computation.4 | async-start | bytes 131072 | tf_op jit(solution)/shard_map/all_to_all | solution.py:65
  647.0 13.4 %copy-start.55 = (bf16[7,2048]{1,0:T(8,128)(2,1)S(1)}, bf16[7,2048]{1,0:T(8,128)(2,1)}, u32[]{:S(2)}) copy-start(bf16[7,2048]{1,0:T(8,128)(2,1)} %param.20) | copy-start | bytes 86020
  647.0 13.4 %copy-start.56 = (pred[8,17]{0,1:T(8,128)(4,1)S(1)}, pred[8,17]{0,1:T(8,128)(4,1)}, u32[]{:S(2)}) copy-start(pred[8,17]{0,1:T(8,128)(4,1)} %constant.132) | copy-start | bytes 412
  655.9 12.8 %all-to-all-start.5 = ((bf16[64,1,224]{2,1,0:T(2,128)(2,1)}), bf16[64,1,224]{2,1,0:T(2,128)(2,1)S(1)}, u32[]{:S(2)}, u32[]{:S(2)}) async-start(bf16[64,1,224]{2,1,0:T(2,128)(2,1)} %broadcast_in_dim.26), calls=%async_computation.5 | async-start | bytes 131072 | tf_op jit(solution)/shard_map/all_to_all | solution.py:29
  668.6 16.8 %all-to-all-start.7 = ((bf16[64,2,2048]{2,1,0:T(2,128)(2,1)}), bf16[64,2,2048]{2,1,0:T(2,128)(2,1)S(1)}, u32[]{:S(2)}, u32[]{:S(2)}) async-start(bf16[64,2,2048]{2,1,0:T(2,128)(2,1)} %reshape.354), calls=%async_computation.7 | async-start | bytes 1048576 | tf_op jit(solution)/shard_map/all_to_all | solution.py:29
  (5 other events, 6.1 us)
Sparse Core Ops, SparseCore 0:
  18.8 128.3 all-gather.1
where the time goes:
time: 706 us; the launch traced here: 697 us
  matrix products  212 us (30%)
  waiting for transfers between devices  190 us (27%)
  local copies, waits for them, and re-layouts  175 us (25%)
  starting transfers between devices  54.8 us (8%)
  other arithmetic  39 us (6%)
  between operations  15.6 us (2%)
  blocking collectives  10.4 us (1%)
    dot_general x66, matrix products, multiply(): return jnp.einsum(pattern, left, right, precision=ACCURATE)  158 us
    all_gather x1, waiting for transfers between devices, per_device(): lax.all_gather(aligned, 'seq', axis=0, tiled=True)  109 us
    transpose x12, local copies, waits for them, and re-layouts, to_inner(): return signal.reshape(devices, height, narrow).transpose(1, 0, 2).reshape...  37.1 us
    conv_general_dilated x4, matrix products, depthwise(): lax.conv_general_dilated(signal.astype(jnp.float32)[None], kernel.astype(...  37.1 us
    transpose x11, local copies, waits for them, and re-layouts, to_blocks(): signal.reshape(height, devices, narrow).transpose(1, 0, 2)  34.3 us
    unnamed x132, local copies, waits for them, and re-layouts  27.5 us
    ppermute x4, waiting for transfers between devices, from_behind(): lax.ppermute(value, axis, [(source, source + steps) for source in range(l...  25.6 us
    sub x10, local copies, waits for them, and re-layouts, twist(): real_part * cosine - imag_part * sine_part  24.4 us
  transfers between devices with their start and end apart: 12, of which 9 were waited for; matrix products, arithmetic and copies ran while one was open for 8% of the time, Pallas kernels for 0%

commit v1 on v0

v1 whole, which is shorter than its diff:
```python
import math

import jax
import jax.numpy as jnp
import numpy as np
from jax import lax
from jax.experimental import pallas as pl
from jax.experimental.pallas import tpu as pltpu
from jax.sharding import PartitionSpec as P

SHORT = 7
MEDIUM = 128
LANES = 128
F32 = jnp.float32
BF16 = jnp.bfloat16
VMEM_LIMIT = 60 * 1024 * 1024


def split_np(table):
    high = table.astype(np.float32).astype(jnp.bfloat16)
    low = (table - high.astype(np.float64)).astype(np.float32).astype(jnp.bfloat16)
    return high, low


def tables(rows):
    total = 2 * rows * LANES
    freq = np.arange(rows)[:, None] + 0.5
    place = np.arange(rows)[None, :]
    angle = 2.0 * np.pi * freq * place / (2 * rows)
    first = np.concatenate([np.cos(angle), -np.sin(angle)], 0)
    first = np.concatenate(split_np(first), 1)
    twist = 2.0 * np.pi * freq * np.arange(LANES)[None, :] / total
    inner = 2.0 * np.pi * np.outer(np.arange(LANES), np.arange(LANES)) / LANES
    cosine, sine = np.cos(inner), np.sin(inner)
    forward = np.block([[cosine, -sine], [sine, cosine]])
    inverse = np.block([[cosine, sine], [-sine, cosine]])
    scale = (rows * LANES) ** -0.5 * 2.0 / total
    last = np.concatenate([np.cos(angle.T), -np.sin(angle.T)], 1) * scale
    twists = np.concatenate([np.cos(twist), np.sin(twist)], 1).astype(np.float32)
    flip = np.eye(LANES)[::-1].astype(jnp.bfloat16)
    return (
        first,
        twists,
        np.concatenate(split_np(forward), 0),
        np.concatenate(split_np(inverse), 0),
        np.concatenate(split_np(last), 0),
        flip,
    )


def dot(a, b):
    return jnp.dot(a, b, preferred_element_type=F32)


def dot_t(a, b):
    return lax.dot_general(a, b, (((1,), (1,)), ((), ())), preferred_element_type=F32)


def split(x):
    high = x.astype(BF16)
    return high, (x - high.astype(F32)).astype(BF16)


def dot3(high, low, table):
    size = table.shape[0] // 2
    return dot(high, table[:size]) + dot(high, table[size:]) + dot(low, table[:size])


def outer_stage(pair, first, twists):
    rows = pair.shape[0]
    spread = dot(first, jnp.concatenate([pair, pair], 0))
    cosine = jnp.concatenate([twists[:, :LANES]] * 2, 1)
    sine = jnp.concatenate([twists[:, LANES:]] * 2, 1)
    real, imag = spread[:rows], spread[rows:]
    new_real = real * cosine + imag * sine
    new_imag = imag * cosine - real * sine
    return (
        jnp.concatenate([new_real[:, :LANES], new_imag[:, :LANES]], 1),
        jnp.concatenate([new_real[:, LANES:], new_imag[:, LANES:]], 1),
    )


def toeplitz(line):
    row = jnp.concatenate([line, jnp.zeros_like(line)], 1)
    block = jnp.broadcast_to(row, (LANES, 2 * LANES))
    return pltpu.roll(block, 0, 1, stride=1, stride_axis=0)


def prepare_kernel(
    early_ref, taps_ref, first_ref, twists_ref, forward_ref, flip_ref,
    spec_ref, gates_ref, bands_ref, turned_ref,
    lines, zh, zl,
):
    rows, width = early_ref.shape[0], early_ref.shape[2]

    @pl.loop(0, rows)
    def _(i):
        at = pl.ds(pl.multiple_of(i * width, width), width)
        for k in range(5):
            lines[k, at, :] = early_ref[i, k].astype(F32)

    @pl.loop(0, width)
    def _(c):
        pick = pl.ds(c, rows, stride=width)
        inner, medium = lines[0, pick, :], lines[1, pick, :]
        mine = pl.ds(pl.multiple_of(c * rows, rows), rows)
        gates_ref[0, mine, :] = inner
        gates_ref[1, mine, :] = medium
        product = (inner * medium).astype(BF16)
        pair = jnp.concatenate([product, lines[4, pick, :].astype(BF16)], 1)
        for k, part in enumerate(outer_stage(pair, first_ref[...], twists_ref[...])):
            high, low = split(part)
            there = pl.ds(pl.multiple_of(k * rows * width + c * rows, rows), rows)
            zh[there, :] = high
            zl[there, :] = low
        wide = pl.ds(pl.multiple_of(c * LANES, LANES), LANES)
        for k in range(2):
            bands_ref[k, wide, :] = toeplitz(taps_ref[k, pl.ds(c, 1), :]).astype(BF16)
            saved = lines[2 + k, pick, :].astype(BF16)
            turned_ref[k, wide, :] = dot_t(flip_ref[...], saved).astype(BF16)

    step = 512

    @pl.loop(0, 2 * rows * width // step)
    def _(b):
        at = pl.ds(pl.multiple_of(b * step, step), step)
        spec_ref[at, :] = dot3(zh[at, :], zl[at, :], forward_ref[...])


def finish_kernel(
    late_ref, spec_ref, gates_ref, bands_ref, turned_ref,
    first_ref, twists_ref, forward_ref, inverse_ref, last_ref,
    out_ref, taps_ref,
    lines, zh, zl, ch, cl, results,
):
    rows, width = late_ref.shape[0], late_ref.shape[1]
    high_row = rows - 1

    @pl.loop(0, rows)
    def _(i):
        at = pl.ds(pl.multiple_of(i * width, width), width)
        lines[at, :] = late_ref[i].astype(F32)

    @pl.loop(0, width // 2)
    def _(c):
        pair = jnp.concatenate(
            [lines[pl.ds(2 * c + k, rows, stride=width), :] for k in range(2)], 1
        ).astype(BF16)
        for k, part in enumerate(outer_stage(pair, first_ref[...], twists_ref[...])):
            high, low = split(part)
            there = pl.ds(pl.multiple_of((2 * c + k) * rows, rows), rows)
            zh[there, :] = high
            zl[there, :] = low

    many = 4
    step = many * rows

    @pl.loop(0, width // many)
    def _(b):
        at = pl.ds(pl.multiple_of(b * step, step), step)
        grad = dot3(zh[at, :], zl[at, :], forward_ref[...])
        grad_real, grad_imag = grad[:, :LANES], grad[:, LANES:]
        cosine = jnp.concatenate([twists_ref[:, :LANES]] * many, 0)
        sine = jnp.concatenate([twists_ref[:, LANES:]] * many, 0)
        reals, imags = [], []
        for k in range(2):
            source = 1 - k
            other = spec_ref[
                pl.ds(pl.multiple_of(source * rows * width + b * step, step), step), :
            ]
            real, imag = other[:, :LANES], other[:, LANES:]
            term = jnp.concatenate(
                [real * grad_real + imag * grad_imag, real * grad_imag - imag * grad_real], 1
            )
            back = dot3(*split(term), inverse_ref[...])
            real, imag = back[:, :LANES], back[:, LANES:]
            reals.append(real * cosine - imag * sine)
            imags.append(real * sine + imag * cosine)
        real, imag = jnp.concatenate(reals, 1), jnp.concatenate(imags, 1)
        for k in range(many):
            both = jnp.concatenate(
                [real[k * rows : (k + 1) * rows], imag[k * rows : (k + 1) * rows]], 0
            )
            high, low = split(both)
            there = pl.ds(
                pl.multiple_of((b * many + k) * 2 * rows, 2 * rows), 2 * rows
            )
            ch[there, :] = high
            cl[there, :] = low

    row = lax.broadcasted_iota(jnp.int32, (rows, LANES), 0)

    def with_next(x):
        following = jnp.where(row == high_row, 0.0, pltpu.roll(x, high_row, 0))
        return jnp.concatenate([x, following], 1).astype(BF16)

    def diagonals(c, k, both):
        wide = pl.ds(pl.multiple_of(c * LANES, LANES), LANES)
        products = dot(turned_ref[k, wide, :], both)
        slid = pltpu.roll(products, 0, 1, stride=1, stride_axis=0)
        return jnp.sum(slid, axis=0, keepdims=True)

    def channel(c):
        there = pl.ds(pl.multiple_of(c * 2 * rows, 2 * rows), 2 * rows)
        mine = pl.ds(pl.multiple_of(c * rows, rows), rows)
        wide = pl.ds(pl.multiple_of(c * LANES, LANES), LANES)
        high, low = ch[there, :], cl[there, :]
        point = dot(last_ref[:rows], high) + dot(last_ref[:rows], low) + dot(last_ref[rows:], high)
        point, filt = point[:, :LANES], point[:, LANES:]
        medium_grad = (point * gates_ref[0, mine, :]).astype(BF16).astype(F32)
        both = with_next(medium_grad)
        short_grad = dot_t(both, bands_ref[0, wide, :]).astype(BF16).astype(F32)
        pair = with_next(short_grad)
        grad_input = dot_t(pair, bands_ref[1, wide, :])
        pick = pl.ds(c, rows, stride=width)
        results[0, pick, :] = point * gates_ref[1, mine, :]
        results[1, pick, :] = grad_input
        results[2, pick, :] = filt
        taps_ref[0, pl.ds(c, 1), :] = diagonals(c, 0, both)
        taps_ref[1, pl.ds(c, 1), :] = diagonals(c, 1, pair)

    unroll = 4

    @pl.loop(0, width // unroll)
    def _(b):
        for k in range(unroll):
            channel(b * unroll + k)

    @pl.loop(0, rows)
    def _(i):
        at = pl.ds(pl.multiple_of(i * width, width), width)
        for k in range(3):
            out_ref[i, k] = results[k, at, :].astype(BF16)


def whole(n):
    return [pl.BlockSpec(memory_space=pltpu.VMEM)] * n


def prepare(early, taps, first, twists, forward, flip):
    rows, _, width, _ = early.shape
    area = rows * width
    return pl.pallas_call(
        prepare_kernel,
        out_shape=(
            jax.ShapeDtypeStruct((2 * area, 2 * LANES), F32),
            jax.ShapeDtypeStruct((2, area, LANES), F32),
            jax.ShapeDtypeStruct((2, width * LANES, 2 * LANES), BF16),
            jax.ShapeDtypeStruct((2, width * LANES, rows), BF16),
        ),
        in_specs=whole(6),
        out_specs=whole(4),
        scratch_shapes=[
            pltpu.VMEM((5, area, LANES), F32),
            pltpu.VMEM((2 * area, 2 * LANES), BF16),
            pltpu.VMEM((2 * area, 2 * LANES), BF16),
        ],
        compiler_params=pltpu.CompilerParams(vmem_limit_bytes=VMEM_LIMIT),
        cost_estimate=pl.CostEstimate(flops=4 * 10**9, bytes_accessed=20 * 2**20, transcendentals=0),
        name="prepare",
    )(early, taps, first, twists, forward, flip)


def finish(late, spec, gates, bands, turned, first, twists, forward, inverse, last):
    rows, width, _ = late.shape
    area = rows * width
    return pl.pallas_call(
        finish_kernel,
        out_shape=(
            jax.ShapeDtypeStruct((rows, 3, width, LANES), BF16),
            jax.ShapeDtypeStruct((2, width, 2 * LANES), F32),
        ),
        in_specs=whole(10),
        out_specs=whole(2),
        scratch_shapes=[
            pltpu.VMEM((area, LANES), F32),
            pltpu.VMEM((area, 2 * LANES), BF16),
            pltpu.VMEM((area, 2 * LANES), BF16),
            pltpu.VMEM((2 * area, 2 * LANES), BF16),
            pltpu.VMEM((2 * area, 2 * LANES), BF16),
            pltpu.VMEM((3, area, LANES), F32),
        ],
        compiler_params=pltpu.CompilerParams(vmem_limit_bytes=VMEM_LIMIT),
        cost_estimate=pl.CostEstimate(flops=8 * 10**9, bytes_accessed=20 * 2**20, transcendentals=0),
        name="finish",
    )(late, spec, gates, bands, turned, first, twists, forward, inverse, last)


def turn_kernel(*refs):
    *ins, out = refs
    blocks, _, width, _ = out.shape
    for k, ref in enumerate(ins):
        out[:, k] = ref[...].astype(F32).T.astype(BF16).reshape(blocks, width, LANES)


def to_blocks(arrays, devices):
    height, channels = arrays[0].shape
    width = channels // devices
    span = 8
    return pl.pallas_call(
        turn_kernel,
        grid=(devices // span,),
        out_shape=jax.ShapeDtypeStruct((devices, len(arrays), width, height), BF16),
        in_specs=[pl.BlockSpec((height, span * width), lambda i: (0, i))] * len(arrays),
        out_specs=pl.BlockSpec((span, len(arrays), width, height), lambda i: (i, 0, 0, 0)),
        cost_estimate=pl.CostEstimate(
            flops=0, bytes_accessed=4 * len(arrays) * height * channels, transcendentals=0
        ),
        name="to_blocks",
    )(*arrays)


def unturn_kernel(in_ref, *outs):
    blocks, _, width, height = in_ref.shape
    for k, out in enumerate(outs):
        block = in_ref[:, k].astype(F32).reshape(blocks * width, height)
        out[...] = block.T.astype(out.dtype)


def from_blocks(block, dtypes):
    devices, count, width, height = block.shape
    span = 8
    return pl.pallas_call(
        unturn_kernel,
        grid=(devices // span,),
        out_shape=[jax.ShapeDtypeStruct((height, devices * width), t) for t in dtypes],
        in_specs=[pl.BlockSpec((span, count, width, height), lambda i: (i, 0, 0, 0))],
        out_specs=[pl.BlockSpec((height, span * width), lambda i: (0, i))] * count,
        cost_estimate=pl.CostEstimate(
            flops=0, bytes_accessed=8 * count * height * devices * width, transcendentals=0
        ),
        name="from_blocks",
    )(block)


def per_device(
    out_grad, out_weight, outer_gate, long_out, inner_gate, conv_input,
    short_out, medium_out, long_filter, taps_short, taps_medium,
):
    height = out_grad.shape[0]
    channels = outer_gate.shape[1]
    devices = lax.axis_size("seq")
    width = channels // devices
    first, twists, forward, inverse, last, flip = tables(devices)

    both = jnp.broadcast_to(out_grad[None], (2, *out_grad.shape))
    features = lax.all_to_all(both, "ch", 0, 0, tiled=True)
    aligned = lax.all_to_all(out_weight, "ch", split_axis=1, concat_axis=0, tiled=True)
    weight = lax.all_gather(aligned, "seq", axis=0, tiled=True)

    early = to_blocks((inner_gate, medium_out, short_out, conv_input, long_filter), devices)
    early = lax.all_to_all(early, "seq", 0, 0, tiled=True)
    at = lax.axis_index("seq") * width
    own = [lax.dynamic_slice_in_dim(t, at, width, 1) for t in (taps_medium, taps_short)]
    own[1] = jnp.pad(own[1], ((0, MEDIUM - SHORT), (0, 0)))
    taps = jnp.stack([t.astype(F32).T for t in own])
    spec, gates, bands, turned = prepare(early, taps, first, twists, forward, flip)

    half = features.shape[2]
    hidden = jnp.dot(
        jnp.concatenate([features[0], features[1]], 1), weight, preferred_element_type=F32
    )
    grad_outer = (hidden * long_out.astype(F32)).astype(BF16)
    long_grad = (hidden * outer_gate.astype(F32)).astype(BF16)
    late = lax.all_to_all(to_blocks((long_grad,), devices), "seq", 0, 0, tiled=True)
    late = late.reshape(devices, width, height)
    results, sums = finish(
        late, spec, gates, bands, turned, first, twists, forward, inverse, last
    )
    results = lax.all_to_all(results, "seq", 0, 0, tiled=True)
    grad_inner, grad_input, grad_filter = from_blocks(results, (BF16, BF16, F32))
    factor = (height * devices) ** -0.5
    lags = jnp.concatenate(
        [sums[0, :, MEDIUM - 1 : 2 * MEDIUM - 1], sums[1, :, MEDIUM - 1 : MEDIUM - 1 + 8]], 1
    )
    lags = lax.all_gather(lags.T * factor, "seq", axis=1, tiled=True)
    return grad_outer, grad_inner, grad_input, grad_filter, lags[MEDIUM : MEDIUM + SHORT], lags[:MEDIUM]


def solution(mesh):
    rows = P("seq", "ch")
    return jax.shard_map(
        per_device,
        mesh=mesh,
        in_specs=(rows, P(("seq", "ch"), None)) + (rows,) * 7 + (P(None, "ch"),) * 2,
        out_specs=(rows,) * 4 + (P(None, "ch"),) * 2,
        check_vma=False,
    )
```

time: 706 us -> 370 us (0.52)
  matrix products: 212 us -> 9.25 us
  local copies, waits for them, and re-layouts: 175 us -> 10.2 us
  Pallas kernels: 0 us -> 63.9 us
  other arithmetic: 39 us -> 1.27 us
  blocking collectives: 10.4 us -> 43.3 us
  starting transfers between devices: 54.8 us -> 31.9 us
    dot_general x71 -> x1, matrix products: 175 us -> 9.25 us  [per_device(): jnp.dot(jnp.concatenate([features[0], features[1]], 1), weight, preferred...]
    all_gather x1 -> x2, waiting for transfers between devices: 109 us -> 186 us  [the longest x1 112 us: per_device(): weight = lax.all_gather(aligned, 'seq', axis=0, tiled=True)]
    transpose x23 -> x0, local copies, waits for them, and re-layouts: 71.4 us -> none  [the longest x12 37.1 us: to_inner(): return signal.reshape(devices, height, narrow).transpose(1, 0, 2).reshape...]
    pallas_call x0 -> x5, Pallas kernels: none -> 63.9 us  [the longest x1 26.4 us: finish(): pl.pallas_call(finish_kernel, out_shape=(jax.ShapeDtypeStruct((rows, 3, w...]
    all_to_all x7 -> x3, waiting for transfers between devices: 55 us -> 6.54 us  [the longest x1 6.53 us: per_device(): features = lax.all_to_all(both, 'ch', 0, 0, tiled=True)]
    conv_general_dilated x4 -> x0, matrix products: 37.1 us -> none  [depthwise(): lax.conv_general_dilated(signal.astype(jnp.float32)[None], kernel.astype(...]
    all_to_all x0 -> x1, blocking collectives: none -> 32.8 us  [per_device(): results = lax.all_to_all(results, 'seq', 0, 0, tiled=True)]
    ppermute x4 -> x0, waiting for transfers between devices: 25.6 us -> none  [from_behind(): lax.ppermute(value, axis, [(source, source + steps) for source in range(l...]
  transfers between devices with their start and end apart: 12 -> 5, of which waited for: 9 -> 3; matrix products, arithmetic and copies ran while one was open for 8% -> 4% of each run, Pallas kernels for 0% -> 10%
where the time goes in v1:
time: 370 us; the launch traced here: 367 us
  waiting for transfers between devices  193 us (52%)
  Pallas kernels  63.9 us (17%)
  blocking collectives  43.3 us (12%)
  starting transfers between devices  31.9 us (9%)
  between operations  14.1 us (4%)
  local copies, waits for them, and re-layouts  10.2 us (3%)
  matrix products  9.25 us (2%)
    all_gather x1, waiting for transfers between devices, per_device(): weight = lax.all_gather(aligned, 'seq', axis=0, tiled=True)  112 us
    all_gather x1, waiting for transfers between devices, per_device(): lags = lax.all_gather(lags.T * factor, 'seq', axis=1, tiled=True)  74.2 us
    all_to_all x1, blocking collectives, per_device(): results = lax.all_to_all(results, 'seq', 0, 0, tiled=True)  32.8 us
    pallas_call x1, Pallas kernels, finish(): pl.pallas_call(finish_kernel, out_shape=(jax.ShapeDtypeStruct((rows, 3, w...  26.4 us
    all_to_all x1, starting transfers between devices, per_device(): early = lax.all_to_all(early, 'seq', 0, 0, tiled=True)  22.1 us
    pallas_call x1, Pallas kernels, prepare(): pl.pallas_call(prepare_kernel, out_shape=(jax.ShapeDtypeStruct((2 * area,...  20 us
    pallas_call x2, Pallas kernels, to_blocks(): pl.pallas_call(turn_kernel, grid=(devices // span,), out_shape=jax.ShapeD...  11.7 us
    all_to_all x1, blocking collectives, per_device(): lax.all_to_all(out_weight, 'ch', split_axis=1, concat_axis=0, tiled=True)  10.4 us
  transfers between devices with their start and end apart: 5, of which 3 were waited for; matrix products, arithmetic and copies ran while one was open for 4% of the time, Pallas kernels for 10%

profile of v1, /device:TPU:1, one launch (start us, length us, event | category | flops | bytes accessed | tf_op | source)
XLA Modules:
  0.0 366.9 jit_solution(13059031695776699909)
XLA Ops:
  7.2 0.0 copy-start
  7.2 0.0 all-gather.3.cloned.1.call-start
  7.2 1.0 copy.48
  8.2 10.4 %all_to_all.39 = bf16[32,2,2048]{2,0,1:T(8,128)(2,1)} all-to-all(bf16[32,2,2048]{2,0,1:T(8,128)(2,1)S(1)} %bitcast.27), channel_id=1, replica_groups=mesh['seq'=64,'ch'=2] {'ch'}, dimensions={1} | all-to-all | bytes 524288 | tf_op jit(solution)/shard_map/all_to_all | solution.py:348
  18.7 0.0 all-gather.3.cloned.1.call-update
  18.7 2.1 broadcast_in_dim.2
  20.8 3.6 all-to-all-start
  24.4 6.5 %to_blocks.3 = bf16[64,5,32,128]{3,2,1,0:T(8,128)(2,1)} custom-call(bf16[128,2048]{1,0:T(8,128)(2,1)} %refs_0_.1, bf16[128,2048]{1,0:T(8,128)(2,1)} %refs_1_.1, bf16[128,2048]{1,0:T(8,128)(2,1)} %refs_2_.1, bf16[128,2048]{1,0:T(8,128)(2,1)} %refs_3_.1, bf16[128,2048]{1,0:T(8,128)(2,1)} %refs_4_.1), custom_call_target="tpu_custom_call" | custom-call | bytes 5242880 | tf_op jit(solution)/shard_map/to_blocks/pallas_call | solution.py:300
  31.0 0.0 copy-start.1
  31.0 6.5 %all-to-all-done = bf16[2,128,2048]{2,1,0:T(8,128)(2,1)S(1)} async-done(((bf16[2,128,2048]{2,1,0:T(8,128)(2,1)}), bf16[2,128,2048]{2,1,0:T(8,128)(2,1)S(1)}, u32[]{:S(2)}, u32[]{:S(2)}) %all-to-all-start) | async-done | bytes 1048608 | tf_op jit(solution)/shard_map/all_to_all | solution.py:347
  37.5 22.1 %all-to-all-start.3 = ((bf16[64,5,32,128]{3,2,1,0:T(8,128)(2,1)}), bf16[64,5,32,128]{3,2,1,0:T(8,128)(2,1)}, u32[]{:S(2)}, u32[]{:S(2)}) async-start(bf16[64,5,32,128]{3,2,1,0:T(8,128)(2,1)} %to_blocks.3), calls=%async_computation.3 | async-start | bytes 5242880 | tf_op jit(solution)/shard_map/all_to_all | solution.py:352
  59.7 0.8 constant_dynamic-slice_fusion
  60.4 0.1 copy.45
  60.5 0.0 copy-done
  60.5 0.1 constant_dynamic-slice_fusion.1
  60.6 0.1 slice_bitcast_fusion.1
  60.7 112.2 %all-gather.3.cloned.1.call-done = bf16[4096,2048]{1,0:T(8,128)(2,1)} async-done(((bf16[64,2048]{1,0:T(8,128)(2,1)}), bf16[4096,2048]{1,0:T(8,128)(2,1)}) %all-gather.3.cloned.1.call-update) | async-done | bytes 16777232 | tf_op jit(solution)/shard_map/all_gather | solution.py:349
  172.9 0.0 copy-done.1
  172.9 9.2 %multiply_convert_fusion = (bf16[128,2048]{1,0:T(8,128)(2,1)}, bf16[128,2048]{1,0:T(8,128)(2,1)}) fusion(bf16[128,2048]{1,0:T(8,128)(2,1)S(1)} %copy-done.1, bf16[128,2048]{1,0:T(8,128)(2,1)} %param.20, bf16[4096,2048]{1,0:T(8,128)(2,1)} %all-gather.3.cloned.1.call-done, bf16[128,2048]{1,0:T(8,128)(2,1)S(1)} %get-tuple-element.51, ...), kind=kOutput, calls=%fused_computation.4 | convolution fusion | flops 2151153664 | bytes 19922944 | tf_op jit(solution)/shard_map/dot_general | solution.py:360
  182.2 5.1 %to_blocks.2 = bf16[64,1,32,128]{3,2,1,0:T(8,128)(2,1)} custom-call(bf16[128,2048]{1,0:T(8,128)(2,1)} %get-tuple-element.48.refs_0_), custom_call_target="tpu_custom_call" | custom-call | bytes 1048576 | tf_op jit(solution)/shard_map/to_blocks/pallas_call | solution.py:300
  187.3 0.0 all-to-all-done.3.early_ref
  187.3 6.1 %all-to-all-start.2 = ((bf16[64,1,32,128]{3,2,1,0:T(8,128)(2,1)}), bf16[64,1,32,128]{3,2,1,0:T(8,128)(2,1)S(1)}, u32[]{:S(2)}, u32[]{:S(2)}) async-start(bf16[64,1,32,128]{3,2,1,0:T(8,128)(2,1)} %to_blocks.2), calls=%async_computation.2 | async-start | bytes 1048576 | tf_op jit(solution)/shard_map/all_to_all | solution.py:365
  193.4 0.0 all-gather.5.cloned.1.call-start
  193.5 0.1 copy.44
  193.5 0.6 maximum_convert_fusion.taps_ref
  194.2 20.0 %prepare.1 = (f32[4096,256]{1,0:T(8,128)}, f32[2,2048,128]{2,1,0:T(8,128)}, bf16[2,4096,256]{2,1,0:T(8,128)(2,1)}, bf16[2,4096,64]{2,1,0:T(8,128)(2,1)}) custom-call(bf16[64,5,32,128]{3,2,1,0:T(8,128)(2,1)} %all-to-all-done.3.early_ref, f32[2,32,128]{2,1,0:T(8,128)} %maximum_convert_fusion.taps_ref, bf16[128,128]{1,0:T(8,128)(2,1)} %constant.28.clone.first_ref, ...), custom_call_target="tpu_custom_call" | custom-call | flops 4000000000 | bytes 20971520 | tf_op jit(solution)/shard_map/prepare/pallas_call | solution.py:243
  214.2 0.0 all-to-all-done.2
  214.2 0.0 copy-start.2
  214.2 0.8 copy-done.2
  215.0 26.4 %finish.1 = (bf16[64,3,32,128]{3,2,1,0:T(8,128)(2,1)}, f32[2,32,256]{2,1,0:T(8,128)}) custom-call(bf16[64,32,128]{2,1,0:T(8,128)(2,1)} %bitcast.28, f32[4096,256]{1,0:T(8,128)} %get-tuple-element.15.spec_ref, f32[2,2048,128]{2,1,0:T(8,128)} %get-tuple-element.16.gates_ref, bf16[2,4096,256]{2,1,0:T(8,128)(2,1)} %get-tuple-element.17.bands_ref, ...), custom_call_target="tpu_custom_call" | custom-call | flops 8000000000 | bytes 20971520 | tf_op jit(solution)/shard_map/finish/pallas_call | solution.py:267
  241.4 0.8 slice_bitcast_fusion.2
  242.2 0.8 slice_bitcast_fusion.3
  243.0 0.6 fusion.4
  243.7 0.0 all-gather.5.cloned.1.call-update
  243.7 32.8 %all_to_all.40.in_ref = bf16[64,3,32,128]{3,2,1,0:T(8,128)(2,1)} all-to-all(bf16[64,3,32,128]{3,2,1,0:T(8,128)(2,1)} %get-tuple-element.19), channel_id=1, replica_groups=mesh['seq'=64,'ch'=2] {'seq'}, dimensions={0} | all-to-all | bytes 3145728 | tf_op jit(solution)/shard_map/all_to_all | solution.py:370
  276.5 5.9 %from_blocks.1 = (bf16[128,2048]{1,0:T(8,128)(2,1)}, bf16[128,2048]{1,0:T(8,128)(2,1)}, f32[128,2048]{1,0:T(8,128)}) custom-call(bf16[64,3,32,128]{3,2,1,0:T(8,128)(2,1)} %all_to_all.40.in_ref), custom_call_target="tpu_custom_call" | custom-call | bytes 6291456 | tf_op jit(solution)/shard_map/from_blocks/pallas_call | solution.py:323
  282.4 74.2 %all-gather.5.cloned.1.call-done = f32[136,2048]{0,1:T(8,128)} async-done(((f32[136,32]{0,1:T(8,128)}), f32[136,2048]{0,1:T(8,128)}) %all-gather.5.cloned.1.call-update) | async-done | bytes 1114128 | tf_op jit(solution)/shard_map/all_gather | solution.py:376
  356.6 0.0 slice-start
  356.6 0.0 slice-start.1
  356.6 1.2 slice-done
  357.8 1.0 copy.42
  358.7 0.0 slice-done.1
  358.7 1.3 copy.43
  (1 shorter events, 0.0 us)
Async XLA Ops:
  7.2 53.4 %copy-start = (bf16[128,2048]{1,0:T(8,128)(2,1)S(1)}, bf16[128,2048]{1,0:T(8,128)(2,1)}, u32[]{:S(2)}) copy-start(bf16[128,2048]{1,0:T(8,128)(2,1)} %param.27) | copy-start | bytes 1572868
  7.2 165.8 %all-gather.3.cloned.1.call-start = ((), (), s32[]{:S(2)}) async-start(), calls=%async_computation.5 | async-start | bytes 17039360 | tf_op jit(solution)/shard_map/all_gather | solution.py:349
  20.8 16.7 %all-to-all-start = ((bf16[2,128,2048]{2,1,0:T(8,128)(2,1)}), bf16[2,128,2048]{2,1,0:T(8,128)(2,1)S(1)}, u32[]{:S(2)}, u32[]{:S(2)}) async-start(bf16[2,128,2048]{2,1,0:T(8,128)(2,1)} %broadcast_in_dim.2), calls=%async_computation | async-start | bytes 2097152 | tf_op jit(solution)/shard_map/all_to_all | solution.py:347
  31.0 142.0 %copy-start.1 = (bf16[128,2048]{1,0:T(8,128)(2,1)S(1)}, bf16[128,2048]{1,0:T(8,128)(2,1)}, u32[]{:S(2)}) copy-start(bf16[128,2048]{1,0:T(8,128)(2,1)} %param.19) | copy-start | bytes 1572868
  37.5 149.8 %all-to-all-start.3 = ((bf16[64,5,32,128]{3,2,1,0:T(8,128)(2,1)}), bf16[64,5,32,128]{3,2,1,0:T(8,128)(2,1)}, u32[]{:S(2)}, u32[]{:S(2)}) async-start(bf16[64,5,32,128]{3,2,1,0:T(8,128)(2,1)} %to_blocks.3), calls=%async_computation.3 | async-start | bytes 5242880 | tf_op jit(solution)/shard_map/all_to_all | solution.py:352
  187.3 26.9 %all-to-all-start.2 = ((bf16[64,1,32,128]{3,2,1,0:T(8,128)(2,1)}), bf16[64,1,32,128]{3,2,1,0:T(8,128)(2,1)S(1)}, u32[]{:S(2)}, u32[]{:S(2)}) async-start(bf16[64,1,32,128]{3,2,1,0:T(8,128)(2,1)} %to_blocks.2), calls=%async_computation.2 | async-start | bytes 1048576 | tf_op jit(solution)/shard_map/all_to_all | solution.py:365
  193.4 163.1 %all-gather.5.cloned.1.call-start = ((), (), s32[]{:S(2)}) async-start(), calls=%async_computation.6 | async-start | bytes 2129920 | tf_op jit(solution)/shard_map/all_gather | solution.py:376
  214.2 0.8 copy-start.2
  356.6 1.2 slice-start
  356.6 2.2 slice-start.1
Sparse Core Ops, SparseCore 0:
  18.8 154.0 all-gather.2
  243.8 112.7 all-gather.4

commit v2 on v1

--- a/solution.py
+++ b/solution.py
@@ -14,6 +14,10 @@
 F32 = jnp.float32
 BF16 = jnp.bfloat16
 VMEM_LIMIT = 60 * 1024 * 1024
+PAD = 16
+SIDE = 4
+PLANE = SIDE * SIDE
+MESH = pl.DeviceIdType.MESH
 
 
 def split_np(table):
@@ -130,8 +134,8 @@
 def finish_kernel(
     late_ref, spec_ref, gates_ref, bands_ref, turned_ref,
     first_ref, twists_ref, forward_ref, inverse_ref, last_ref,
-    out_ref, taps_ref,
-    lines, zh, zl, ch, cl, results,
+    out_ref,
+    lines, zh, zl, ch, cl, results, sums,
 ):
     rows, width = late_ref.shape[0], late_ref.shape[1]
     high_row = rows - 1
@@ -216,8 +220,8 @@
         results[0, pick, :] = point * gates_ref[1, mine, :]
         results[1, pick, :] = grad_input
         results[2, pick, :] = filt
-        taps_ref[0, pl.ds(c, 1), :] = diagonals(c, 0, both)
-        taps_ref[1, pl.ds(c, 1), :] = diagonals(c, 1, pair)
+        sums[0, pl.ds(c, 1), :] = diagonals(c, 0, both)
+        sums[1, pl.ds(c, 1), :] = diagonals(c, 1, pair)
 
     unroll = 4
 
@@ -226,11 +230,19 @@
         for k in range(unroll):
             channel(b * unroll + k)
 
+    factor = (rows * LANES) ** -0.5
+    lags = [pltpu.roll(sums[k], LANES + 1, 1)[:, :LANES] * factor for k in range(2)]
+    medium = lags[0].astype(BF16)
+    square = jnp.concatenate([lags[1], jnp.zeros((LANES - width, LANES), F32)], 0)
+    short = square.T[:PAD].astype(BF16)
+
     @pl.loop(0, rows)
     def _(i):
         at = pl.ds(pl.multiple_of(i * width, width), width)
         for k in range(3):
-            out_ref[i, k] = results[k, at, :].astype(BF16)
+            out_ref[i, k * width : (k + 1) * width] = results[k, at, :].astype(BF16)
+        out_ref[i, 3 * width : 4 * width] = medium
+        out_ref[i, 4 * width :] = short
 
 
 def whole(n):
@@ -266,12 +278,9 @@
     area = rows * width
     return pl.pallas_call(
         finish_kernel,
-        out_shape=(
-            jax.ShapeDtypeStruct((rows, 3, width, LANES), BF16),
-            jax.ShapeDtypeStruct((2, width, 2 * LANES), F32),
-        ),
+        out_shape=jax.ShapeDtypeStruct((rows, 4 * width + PAD, LANES), BF16),
         in_specs=whole(10),
-        out_specs=whole(2),
+        out_specs=whole(1)[0],
         scratch_shapes=[
             pltpu.VMEM((area, LANES), F32),
             pltpu.VMEM((area, 2 * LANES), BF16),
@@ -279,6 +288,7 @@
             pltpu.VMEM((2 * area, 2 * LANES), BF16),
             pltpu.VMEM((2 * area, 2 * LANES), BF16),
             pltpu.VMEM((3, area, LANES), F32),
+            pltpu.VMEM((2, width, 2 * LANES), F32),
         ],
         compiler_params=pltpu.CompilerParams(vmem_limit_bytes=VMEM_LIMIT),
         cost_estimate=pl.CostEstimate(flops=8 * 10**9, bytes_accessed=20 * 2**20, transcendentals=0),
@@ -288,93 +298,401 @@
 
 def turn_kernel(*refs):
     *ins, out = refs
-    blocks, _, width, _ = out.shape
+    _, blocks, _, _, width, _ = out.shape
     for k, ref in enumerate(ins):
-        out[:, k] = ref[...].astype(F32).T.astype(BF16).reshape(blocks, width, LANES)
+        out[0, :, 0, k] = ref[...].astype(F32).T.astype(BF16).reshape(blocks, width, LANES)
+
+
+def block_place(i):
+    return i // 4, i % 2, (i // 2) % 2
 
 
 def to_blocks(arrays, devices):
     height, channels = arrays[0].shape
     width = channels // devices
-    span = 8
-    return pl.pallas_call(
+    span = PLANE // 2
+    count = len(arrays)
+    out = pl.pallas_call(
         turn_kernel,
         grid=(devices // span,),
-        out_shape=jax.ShapeDtypeStruct((devices, len(arrays), width, height), BF16),
-        in_specs=[pl.BlockSpec((height, span * width), lambda i: (0, i))] * len(arrays),
-        out_specs=pl.BlockSpec((span, len(arrays), width, height), lambda i: (i, 0, 0, 0)),
+        out_shape=jax.ShapeDtypeStruct((2, PLANE, 2, count, width, height), BF16),
+        in_specs=[pl.BlockSpec((height, span * width), lambda i: (0, i))] * count,
+        out_specs=pl.BlockSpec(
+            (1, span, 1, count, width, height), lambda i: (*block_place(i), 0, 0, 0)
+        ),
         cost_estimate=pl.CostEstimate(
-            flops=0, bytes_accessed=4 * len(arrays) * height * channels, transcendentals=0
+            flops=0, bytes_accessed=4 * count * height * channels, transcendentals=0
         ),
         name="to_blocks",
     )(*arrays)
+    return out.reshape(devices, count, width, height)
 
 
 def unturn_kernel(in_ref, *outs):
-    blocks, _, width, height = in_ref.shape
+    blocks, height = in_ref.shape[1], in_ref.shape[4]
+    width = outs[0].shape[1] // blocks
     for k, out in enumerate(outs):
-        block = in_ref[:, k].astype(F32).reshape(blocks * width, height)
-        out[...] = block.T.astype(out.dtype)
-
-
-def from_blocks(block, dtypes):
-    devices, count, width, height = block.shape
-    span = 8
+        block = in_ref[0, :, 0, k * width : (k + 1) * width].astype(F32)
+        out[...] = block.reshape(blocks * width, height).T.astype(out.dtype)
+
+
+def from_blocks(block, width, dtypes):
+    devices, lines, height = block.shape
+    span = PLANE // 2
+    count = len(dtypes)
     return pl.pallas_call(
         unturn_kernel,
         grid=(devices // span,),
         out_shape=[jax.ShapeDtypeStruct((height, devices * width), t) for t in dtypes],
-        in_specs=[pl.BlockSpec((span, count, width, height), lambda i: (i, 0, 0, 0))],
+        in_specs=[
+            pl.BlockSpec((1, span, 1, lines, height), lambda i: (*block_place(i), 0, 0))
+        ],
         out_specs=[pl.BlockSpec((height, span * width), lambda i: (0, i))] * count,
         cost_estimate=pl.CostEstimate(
             flops=0, bytes_accessed=8 * count * height * devices * width, transcendentals=0
         ),
         name="from_blocks",
-    )(block)
+    )(block.reshape(2, PLANE, 2, lines, height))
+
+
+def wrap(i):
+    return lax.rem(i + SIDE, SIDE)
+
+
+class Here:
+    def __init__(self):
+        seq = lax.axis_index("seq")
+        self.y_hi = lax.axis_index("ch")
+        self.core = seq % 2
+        self.z = (seq // 2) % SIDE
+        self.x = (seq // (2 * SIDE)) % SIDE
+        self.y_lo = seq // (2 * PLANE)
+        self.y = self.y_hi * 2 + self.y_lo
+
+    def at(self, x=None, y=None, z=None, core=None):
+        x = self.x if x is None else x
+        y = self.y if y is None else y
+        z = self.z if z is None else z
+        core = self.core if core is None else core
+        seq = (((y % 2) * SIDE + x) * SIDE + z) * 2 + core
+        return {"seq": seq, "ch": y // 2}
+
+
+def send(source, target, sends, recvs, device):
+    copy = pltpu.make_async_remote_copy(
+        src_ref=source,
+        dst_ref=target,
+        send_sem=sends,
+        recv_sem=recvs,
+        device_id=device,
+        device_id_type=MESH,
+    )
+    copy.start()
+
+
+def await_bytes(ref, sem):
+    pltpu.make_async_copy(ref, ref, sem).wait()
+
+
+class Ring:
+    def __init__(self, here, axis, item, half, sends, recvs, source=None):
+        self.at = lambda p: here.at(**{axis: p})
+        self.place = getattr(here, axis)
+        self.item, self.half = item, half
+        self.sends, self.recvs = sends, recvs
+        self.source = item(self.place) if source is None else source
+
+    def step(self, i, source, target, to):
+        send(source, target, self.sends.at[i], self.recvs.at[i], self.at(wrap(self.place + to)))
+
+    def start(self):
+        self.step(0, self.source, self.item(self.place), 1)
+        self.step(1, self.source, self.item(self.place), -1)
+
+    def relay(self):
+        for i, to in ((0, 1), (1, -1)):
+            other = wrap(self.place - to)
+            await_bytes(self.item(other), self.recvs.at[i])
+            half = self.half(self.item(other), i)
+            self.step(2 + i, half, half, to)
+
+    def finish(self):
+        opposite = self.item(wrap(self.place + 2))
+        for i in range(2):
+            await_bytes(self.half(opposite, i), self.recvs.at[2 + i])
+
+    def drain(self):
+        opposite = self.item(wrap(self.place + 2))
+        for i in range(2):
+            await_bytes(self.item(self.place), self.sends.at[i])
+            await_bytes(self.half(opposite, i), self.sends.at[2 + i])
+
+
+def project_kernel(
+    grad_ref, weight_ref, gate_ref, long_ref,
+    outer_ref, late_ref,
+    feats, weights, gates, total, turned, hidden, arrived,
+    local, spread_s, spread_r, gate_s, gate_r, feat_s, feat_r, pass_s, pass_r,
+    ring_s, ring_r, late_s, late_r, back_s, back_r,
+):
+    here = Here()
+    me = here.y_lo * 2 + here.core
+    cell = here.x * SIDE + here.z
+    columns = gates.shape[2]
+    height = grad_ref.shape[0]
+
+    def column_peers():
+        for dy in range(SIDE):
+            for dc in range(2):
+                if dy or dc:
+                    yield dy * 2 + dc - 1, wrap(here.y + dy), (here.core + dc) % 2
+
+    def plane_peers():
+        for dx in range(SIDE):
+            for dz in range(SIDE):
+                if dx or dz:
+                    yield dx * SIDE + dz - 1, wrap(here.x + dx), wrap(here.z + dz)
+
+    barrier = pltpu.get_barrier_semaphore()
+    for _, y, core in column_peers():
+        pl.semaphore_signal(barrier, 1, device_id=here.at(y=y, core=core), device_id_type=MESH)
+    for _, x, z in plane_peers():
+        pl.semaphore_signal(barrier, 1, device_id=here.at(x=x, z=z), device_id_type=MESH)
+    pl.semaphore_wait(barrier, 22)
+
+    def weight_columns(y, core):
+        return weight_ref.at[:, pl.ds(pl.multiple_of((y * 2 + core) * columns, columns), columns)]
+
+    def gate_columns(index):
+        return gate_ref.at[:, pl.ds(pl.multiple_of(index * columns, columns), columns)]
+
+    row_block = here.core * 2 + here.y_hi
+    own_rows = weights.at[here.y_lo, here.x, here.z, row_block]
+    for i, y, core in column_peers():
+        send(weight_columns(y, core), own_rows, spread_s.at[i], spread_r.at[i], here.at(y=y, core=core))
+    copies = [
+        pltpu.make_async_copy(weight_columns(here.y, here.core), own_rows, local.at[0]),
+        pltpu.make_async_copy(grad_ref, feats.at[here.y_hi, me], local.at[1]),
+        pltpu.make_async_copy(gate_columns(me), gates.at[me], local.at[2]),
+    ]
+    for copy in copies:
+        copy.start()
+
+    def half_tokens(ref, i):
+        return ref.at[pl.ds(i * (height // 2), height // 2)]
+
+    features = Ring(
+        here, "y", lambda y: feats.at[y // 2, (y % 2) * 2 + here.core], half_tokens,
+        feat_s, feat_r, source=grad_ref,
+    )
+    features.start()
+    partner = here.at(core=1 - here.core)
+
+    def feat(y, core):
+        return feats.at[y // 2, (y % 2) * 2 + core]
+
+    def pass_on(i, y):
+        send(grad_ref if i == 0 else feat(y, here.core), feat(y, here.core), pass_s.at[i], pass_r.at[i], partner)
+
+    pass_on(0, here.y)
+    share = [(0, 1), (1, 0), (1, 1)]
+    for i, (dy, dc) in enumerate(share):
+        y_lo, core = (here.y_lo + dy) % 2, (here.core + dc) % 2
+        send(
+            gate_columns(y_lo * 2 + core), gates.at[me], gate_s.at[i], gate_r.at[i],
+            here.at(y=here.y_hi * 2 + y_lo, core=core),
+        )
+
+    for i, y, core in column_peers():
+        source_y, source_core = wrap(2 * here.y - y + SIDE), core
+        await_bytes(
+            weights.at[source_y % 2, here.x, here.z, source_core * 2 + source_y // 2],
+            spread_r.at[i],
+        )
+    copies[0].wait()
+
+    def half_block(ref, i):
+        return ref.at[pl.ds(i * 2, 2)]
+
+    def block_ring(k, axis, item):
+        return Ring(here, axis, item, half_block, ring_s.at[k], ring_r.at[k])
+
+    first = [
+        block_ring(0, "x", lambda x: weights.at[0, x, here.z]),
+        block_ring(1, "z", lambda z: weights.at[1, here.x, z]),
+    ]
+    order = (0, 3, 1, 2)
+    second = []
+    for j, d in enumerate(order):
+        second.append((
+            block_ring(2 + 2 * j, "z", lambda z, d=d: weights.at[0, wrap(here.x + d), z]),
+            block_ring(3 + 2 * j, "x", lambda x, d=d: weights.at[1, x, wrap(here.z + d)]),
+        ))
+    for ring in first:
+        ring.start()
+    for ring in second[0]:
+        ring.start()
+    for ring in first:
+        ring.relay()
+    for pair in second[1:3]:
+        for ring in pair:
+            ring.start()
+    for ring in second[0]:
+        ring.relay()
+    for ring in first:
+        ring.finish()
+    for ring in second[3]:
+        ring.start()
+    features.relay()
+    pass_on(1, wrap(here.y - 1))
+    pass_on(2, wrap(here.y + 1))
+    for pair in second[1:]:
+        for ring in pair:
+            ring.relay()
+    features.finish()
+    pass_on(3, wrap(here.y + 2))
+    for pair in second:
+        for ring in pair:
+            ring.finish()
+    for i, d in enumerate((0, -1, 1, 2)):
+        await_bytes(feat(wrap(here.y + d), 1 - here.core), pass_r.at[i])
+    copies[1].wait()
+
+    depth = SIDE * weights.shape[3] * weights.shape[4]
+    for h in range(2):
+        @pl.loop(0, SIDE)
+        def _(x):
+            part = pl.ds(pl.multiple_of(x * depth, depth), depth)
+            left = feats[h, :, :, part].reshape(4 * height, depth)
+            term = dot(left, weights[h, x].reshape(depth, columns))
+            if h == 0:
+                @pl.when(x == 0)
+                def _():
+                    total[...] = term
+
+                @pl.when(x > 0)
+                def _():
+                    total[...] += term
+            else:
+                total[...] += term
+
+    copies[2].wait()
+    for i, (dy, dc) in enumerate(share):
+        source = ((here.y_lo + dy) % 2) * 2 + (here.core + dc) % 2
+        await_bytes(gates.at[source], gate_r.at[i])
+    width = late_ref.shape[3]
+    for g in range(4):
+        part = total[g * height : (g + 1) * height]
+        long_grad = (part * gates[g].astype(F32)).astype(BF16).astype(F32)
+        turned[:, g // 2, g % 2] = long_grad.T.astype(BF16).reshape(PLANE, width, height)
+        hidden[g] = part.astype(BF16)
+    keep = pltpu.make_async_copy(turned.at[cell], late_ref.at[:, cell], local.at[0])
+    keep.start()
+    for i, x, z in plane_peers():
+        send(turned.at[x * SIDE + z], late_ref.at[:, cell], late_s.at[i], late_r.at[i], here.at(x=x, z=z))
+    for i, (dy, dc) in enumerate(share):
+        y_lo, core = (here.y_lo + dy) % 2, (here.core + dc) % 2
+        send(
+            hidden.at[y_lo * 2 + core], arrived.at[me], back_s.at[i], back_r.at[i],
+            here.at(y=here.y_hi * 2 + y_lo, core=core),
+        )
+    own = pltpu.make_async_copy(hidden.at[me], arrived.at[me], local.at[1])
+    own.start()
+    own.wait()
+    for i, (dy, dc) in enumerate(share):
+        source = ((here.y_lo + dy) % 2) * 2 + (here.core + dc) % 2
+        await_bytes(arrived.at[source], back_r.at[i])
+    for g in range(4):
+        part = slice(g * columns, (g + 1) * columns)
+        outer_ref[:, part] = (arrived[g].astype(F32) * long_ref[:, part].astype(F32)).astype(BF16)
+    keep.wait()
+    for i, x, z in plane_peers():
+        source = wrap(2 * here.x - x + SIDE) * SIDE + wrap(2 * here.z - z + SIDE)
+        await_bytes(late_ref.at[:, source], late_r.at[i])
+
+    for i in range(7):
+        await_bytes(own_rows, spread_s.at[i])
+    for i in range(3):
+        await_bytes(gates.at[me], gate_s.at[i])
+        await_bytes(hidden.at[me], back_s.at[i])
+    for i in range(4):
+        await_bytes(feats.at[0, 0], pass_s.at[i])
+    for i in range(15):
+        await_bytes(turned.at[0], late_s.at[i])
+    features.drain()
+    for ring in first:
+        ring.drain()
+    for pair in second:
+        for ring in pair:
+            ring.drain()
+
+
+def project(out_grad, out_weight, outer_gate, long_out):
+    height, half = out_grad.shape
+    rows, model = out_weight.shape
+    columns = model // 8
+    width = columns // PLANE
+    dma = pltpu.SemaphoreType.DMA
+    anywhere = pl.BlockSpec(memory_space=pl.ANY)
+    in_vmem = pl.BlockSpec(memory_space=pltpu.VMEM)
+    outer, late = pl.pallas_call(
+        project_kernel,
+        out_shape=(
+            jax.ShapeDtypeStruct((height, half), BF16),
+            jax.ShapeDtypeStruct((2, PLANE, 2, width, height), BF16),
+        ),
+        in_specs=[anywhere, anywhere, anywhere, in_vmem],
+        out_specs=(in_vmem, in_vmem),
+        scratch_shapes=[
+            pltpu.VMEM((2, 4, height, half), BF16),
+            pltpu.VMEM((2, SIDE, SIDE, 4, rows, columns), BF16),
+            pltpu.VMEM((4, height, columns), BF16),
+            pltpu.VMEM((4 * height, columns), F32),
+            pltpu.VMEM((PLANE, 2, 2, width, height), BF16),
+            pltpu.VMEM((4, height, columns), BF16),
+            pltpu.VMEM((4, height, columns), BF16),
+            dma((3,)), dma((7,)), dma((7,)), dma((3,)), dma((3,)), dma((4,)), dma((4,)),
+            dma((4,)), dma((4,)), dma((10, 4)), dma((10, 4)), dma((15,)), dma((15,)),
+            dma((3,)), dma((3,)),
+        ],
+        compiler_params=pltpu.CompilerParams(
+            collective_id=0, has_side_effects=True, vmem_limit_bytes=40 * 1024 * 1024
+        ),
+        cost_estimate=pl.CostEstimate(
+            flops=2 * 4 * height * model * columns, bytes_accessed=16 * 2**20, transcendentals=0
+        ),
+        name="project",
+    )(out_grad, out_weight, outer_gate, long_out)
+    return outer, late.reshape(4 * PLANE, width, height)
 
 
 def per_device(
     out_grad, out_weight, outer_gate, long_out, inner_gate, conv_input,
     short_out, medium_out, long_filter, taps_short, taps_medium,
 ):
-    height = out_grad.shape[0]
-    channels = outer_gate.shape[1]
+    height, channels = outer_gate.shape
     devices = lax.axis_size("seq")
     width = channels // devices
     first, twists, forward, inverse, last, flip = tables(devices)
 
-    both = jnp.broadcast_to(out_grad[None], (2, *out_grad.shape))
-    features = lax.all_to_all(both, "ch", 0, 0, tiled=True)
-    aligned = lax.all_to_all(out_weight, "ch", split_axis=1, concat_axis=0, tiled=True)
-    weight = lax.all_gather(aligned, "seq", axis=0, tiled=True)
-
     early = to_blocks((inner_gate, medium_out, short_out, conv_input, long_filter), devices)
     early = lax.all_to_all(early, "seq", 0, 0, tiled=True)
-    at = lax.axis_index("seq") * width
+    here = Here()
+    at = (((here.y_lo * 2 + here.core) * SIDE + here.x) * SIDE + here.z) * width
     own = [lax.dynamic_slice_in_dim(t, at, width, 1) for t in (taps_medium, taps_short)]
     own[1] = jnp.pad(own[1], ((0, MEDIUM - SHORT), (0, 0)))
     taps = jnp.stack([t.astype(F32).T for t in own])
+    grad_outer, late = project(out_grad, out_weight, outer_gate, long_out)
     spec, gates, bands, turned = prepare(early, taps, first, twists, forward, flip)
-
-    half = features.shape[2]
-    hidden = jnp.dot(
-        jnp.concatenate([features[0], features[1]], 1), weight, preferred_element_type=F32
+    results = finish(late, spec, gates, bands, turned, first, twists, forward, inverse, last)
+    results = lax.all_to_all(results, "seq", 0, 0, tiled=True)
+    grad_inner, grad_input, grad_filter, grad_medium = from_blocks(
+        results, width, (BF16, BF16, F32, F32)
     )
-    grad_outer = (hidden * long_out.astype(F32)).astype(BF16)
-    long_grad = (hidden * outer_gate.astype(F32)).astype(BF16)
-    late = lax.all_to_all(to_blocks((long_grad,), devices), "seq", 0, 0, tiled=True)
-    late = late.reshape(devices, width, height)
-    results, sums = finish(
-        late, spec, gates, bands, turned, first, twists, forward, inverse, last
-    )
-    results = lax.all_to_all(results, "seq", 0, 0, tiled=True)
-    grad_inner, grad_input, grad_filter = from_blocks(results, (BF16, BF16, F32))
-    factor = (height * devices) ** -0.5
-    lags = jnp.concatenate(
-        [sums[0, :, MEDIUM - 1 : 2 * MEDIUM - 1], sums[1, :, MEDIUM - 1 : MEDIUM - 1 + 8]], 1
-    )
-    lags = lax.all_gather(lags.T * factor, "seq", axis=1, tiled=True)
-    return grad_outer, grad_inner, grad_input, grad_filter, lags[MEDIUM : MEDIUM + SHORT], lags[:MEDIUM]
+    short = results[:, 4 * width : 4 * width + SHORT, :width]
+    short = short.reshape(2, PLANE, 2, SHORT, width).transpose(3, 0, 2, 1, 4)
+    grad_short = short.reshape(SHORT, channels).astype(F32)
+    return grad_outer, grad_inner, grad_input, grad_filter, grad_short, grad_medium
 
 
 def solution(mesh):

time: 370 us -> 189 us (0.51)
  waiting for transfers between devices: 193 us -> 31.2 us
  Pallas kernels: 63.9 us -> 133 us
  blocking collectives: 43.3 us -> 0 us
  starting transfers between devices: 31.9 us -> 17.7 us
  between operations: 14.1 us -> 0.8 us
  matrix products: 9.25 us -> 0 us
  local copies, waits for them, and re-layouts: 10.2 us -> 4.41 us
    all_gather x2 -> x0, waiting for transfers between devices: 186 us -> none  [the longest x1 112 us: per_device(): weight = lax.all_gather(aligned, 'seq', axis=0, tiled=True)]
    pallas_call x1 -> x2, Pallas kernels: 26.4 us -> 100 us  [the longest x1 73.4 us: project(): pl.pallas_call(project_kernel, out_shape=(jax.ShapeDtypeStruct((height, h...]
    all_to_all x2 -> x0, blocking collectives: 43.3 us -> none  [the longest x1 32.8 us: per_device(): results = lax.all_to_all(results, 'seq', 0, 0, tiled=True)]
    all_to_all x2 -> x1, waiting for transfers between devices: 6.54 us -> 31.2 us  [per_device(): results = lax.all_to_all(results, 'seq', 0, 0, tiled=True)]
    all_to_all x1, starting transfers between devices: 22.1 us -> 11.1 us  [per_device(): early = lax.all_to_all(early, 'seq', 0, 0, tiled=True)]
    dot_general x1 -> x0, matrix products: 9.25 us -> none  [per_device(): jnp.dot(jnp.concatenate([features[0], features[1]], 1), weight, preferred...]
    pallas_call x2 -> x1, Pallas kernels: 11.7 us -> 6.58 us  [to_blocks(): pl.pallas_call(turn_kernel, grid=(devices // span,), out_shape=jax.ShapeD...]
    all_to_all x2 -> x1, starting transfers between devices: 9.67 us -> 6.56 us  [per_device(): results = lax.all_to_all(results, 'seq', 0, 0, tiled=True)]
  transfers between devices with their start and end apart: 5 -> 2, of which waited for: 3 -> 1; matrix products, arithmetic and copies ran while one was open for 4% -> 1% of each run, Pallas kernels for 10% -> 39%
where the time goes in v2:
time: 189 us; the launch traced here: 188 us
  Pallas kernels  133 us (70%)
  waiting for transfers between devices  31.2 us (17%)
  starting transfers between devices  17.7 us (9%)
  local copies, waits for them, and re-layouts  4.41 us (2%)
    pallas_call x1, Pallas kernels, project(): pl.pallas_call(project_kernel, out_shape=(jax.ShapeDtypeStruct((height, h...  73.4 us
    all_to_all x1, waiting for transfers between devices, per_device(): results = lax.all_to_all(results, 'seq', 0, 0, tiled=True)  31.2 us
    pallas_call x1, Pallas kernels, finish(): pl.pallas_call(finish_kernel, out_shape=jax.ShapeDtypeStruct((rows, 4 * w...  26.8 us
    pallas_call x1, Pallas kernels, prepare(): pl.pallas_call(prepare_kernel, out_shape=(jax.ShapeDtypeStruct((2 * area,...  20 us
    all_to_all x1, starting transfers between devices, per_device(): early = lax.all_to_all(early, 'seq', 0, 0, tiled=True)  11.1 us
    pallas_call x1, Pallas kernels, to_blocks(): pl.pallas_call(turn_kernel, grid=(devices // span,), out_shape=jax.ShapeD...  6.58 us
    all_to_all x1, starting transfers between devices, per_device(): results = lax.all_to_all(results, 'seq', 0, 0, tiled=True)  6.56 us
    pallas_call x1, Pallas kernels, from_blocks(): pl.pallas_call(unturn_kernel, grid=(devices // span,), out_shape=[jax.Sha...  6.2 us
  transfers between devices with their start and end apart: 2, of which 1 were waited for; matrix products, arithmetic and copies ran while one was open for 1% of the time, Pallas kernels for 39%

profile of v2, /device:TPU:1, one launch (start us, length us, event | category | flops | bytes accessed | tf_op | source)
XLA Modules:
  0.0 187.7 jit_solution(10940739928073274205)
XLA Ops:
  0.6 0.0 copy-start
  0.6 6.6 %to_blocks.1 = bf16[2,16,2,5,32,128]{5,4,3,2,1,0:T(8,128)(2,1)} custom-call(bf16[128,2048]{1,0:T(8,128)(2,1)} %refs_0_.1, bf16[128,2048]{1,0:T(8,128)(2,1)} %refs_1_.1, bf16[128,2048]{1,0:T(8,128)(2,1)} %refs_2_.1, bf16[128,2048]{1,0:T(8,128)(2,1)} %refs_3_.1, bf16[128,2048]{1,0:T(8,128)(2,1)} %refs_4_.1), custom_call_target="tpu_custom_call" | custom-call | bytes 5242880 | tf_op jit(solution)/shard_map/to_blocks/pallas_call | solution.py:315
  7.2 0.0 copy-start.1
  7.2 0.0 copy-start.2
  7.2 0.0 copy-start.3
  7.2 0.0 copy-start.4
  7.3 11.1 %all-to-all-start = ((bf16[64,5,32,128]{3,2,1,0:T(8,128)(2,1)}), bf16[64,5,32,128]{3,2,1,0:T(8,128)(2,1)}, u32[]{:S(2)}, u32[]{:S(2)}) async-start(bf16[64,5,32,128]{3,2,1,0:T(8,128)(2,1)} %bitcast.17), calls=%async_computation | async-start | bytes 5242880 | tf_op jit(solution)/shard_map/all_to_all | solution.py:679
  18.5 0.0 copy-done
  18.5 0.1 constant_dynamic-slice_fusion.1
  18.6 0.1 copy.26
  18.6 0.8 constant_dynamic-slice_fusion
  19.4 0.1 copy.27
  19.5 0.6 maximum_convert_fusion.taps_ref
  20.2 0.0 copy-done.1
  20.2 0.0 copy-done.2
  20.2 0.0 copy-done.3
  20.2 0.0 copy-done.4
  20.2 73.4 %project.1 = (bf16[128,2048]{1,0:T(8,128)(2,1)S(1)}, bf16[2,16,2,32,128]{4,3,2,1,0:T(8,128)(2,1)S(1)}) custom-call(bf16[128,2048]{1,0:T(8,128)(2,1)S(1)} %copy-done.1, bf16[32,4096]{1,0:T(8,128)(2,1)S(1)} %copy-done.4, bf16[128,2048]{1,0:T(8,128)(2,1)S(1)} %copy-done.2, bf16[128,2048]{1,0:T(8,128)(2,1)S(1)} %copy-done.3), custom_call_target="tpu_custom_call" | custom-call | flops 2147483648 | bytes 16777216 | tf_op jit(solution)/shard_map/project/pallas_call | solution.py:638
  93.6 0.0 copy-start.5
  93.6 0.8 copy-done.5
  94.4 0.0 all-to-all-done.early_ref
  94.4 20.0 %prepare.1 = (f32[4096,256]{1,0:T(8,128)}, f32[2,2048,128]{2,1,0:T(8,128)}, bf16[2,4096,256]{2,1,0:T(8,128)(2,1)}, bf16[2,4096,64]{2,1,0:T(8,128)(2,1)}) custom-call(bf16[64,5,32,128]{3,2,1,0:T(8,128)(2,1)} %all-to-all-done.early_ref, f32[2,32,128]{2,1,0:T(8,128)} %maximum_convert_fusion.taps_ref, bf16[128,128]{1,0:T(8,128)(2,1)} %constant.83.clone.first_ref, ...), custom_call_target="tpu_custom_call" | custom-call | flops 4000000000 | bytes 20971520 | tf_op jit(solution)/shard_map/prepare/pallas_call | solution.py:255
  114.4 26.8 %finish.1 = bf16[64,144,128]{2,1,0:T(8,128)(2,1)} custom-call(bf16[64,32,128]{2,1,0:T(8,128)(2,1)} %bitcast.16, f32[4096,256]{1,0:T(8,128)} %get-tuple-element.18.spec_ref, f32[2,2048,128]{2,1,0:T(8,128)} %get-tuple-element.19.gates_ref, bf16[2,4096,256]{2,1,0:T(8,128)(2,1)} %get-tuple-element.20.bands_ref, ...), custom_call_target="tpu_custom_call" | custom-call | flops 8000000000 | bytes 20971520 | tf_op jit(solution)/shard_map/finish/pallas_call | solution.py:279
  141.2 6.6 %all-to-all-start.1 = ((bf16[64,144,128]{2,1,0:T(8,128)(2,1)}), bf16[64,144,128]{2,1,0:T(8,128)(2,1)}, u32[]{:S(2)}, u32[]{:S(2)}) async-start(bf16[64,144,128]{2,1,0:T(8,128)(2,1)} %finish.1), calls=%async_computation.1 | async-start | bytes 4718592 | tf_op jit(solution)/shard_map/all_to_all | solution.py:688
  147.8 31.2 %all-to-all-done.1 = bf16[64,144,128]{2,1,0:T(8,128)(2,1)} async-done(((bf16[64,144,128]{2,1,0:T(8,128)(2,1)}), bf16[64,144,128]{2,1,0:T(8,128)(2,1)}, u32[]{:S(2)}, u32[]{:S(2)}) %all-to-all-start.1) | async-done | bytes 2359328 | tf_op jit(solution)/shard_map/all_to_all | solution.py:688
  178.9 6.2 %from_blocks.1 = (bf16[128,2048]{1,0:T(8,128)(2,1)}, bf16[128,2048]{1,0:T(8,128)(2,1)}, f32[128,2048]{1,0:T(8,128)}, f32[128,2048]{1,0:T(8,128)}) custom-call(bf16[2,16,2,144,128]{4,3,2,1,0:T(8,128)(2,1)} %bitcast.6.in_ref), custom_call_target="tpu_custom_call" | custom-call | bytes 8388608 | tf_op jit(solution)/shard_map/from_blocks/pallas_call | solution.py:343
  185.1 0.9 slice.4
  186.1 0.1 copy.25
  186.2 0.8 reshape.30
  186.9 0.8 copy.29
  (2 shorter events, 0.0 us)
Async XLA Ops:
  0.6 17.9 %copy-start = (bf16[128,2048]{1,0:T(8,128)(2,1)S(1)}, bf16[128,2048]{1,0:T(8,128)(2,1)}, u32[]{:S(2)}) copy-start(bf16[128,2048]{1,0:T(8,128)(2,1)} %param.27) | copy-start | bytes 1572868
  7.2 12.9 %copy-start.1 = (bf16[128,2048]{1,0:T(8,128)(2,1)S(1)}, bf16[128,2048]{1,0:T(8,128)(2,1)}, u32[]{:S(2)}) copy-start(bf16[128,2048]{1,0:T(8,128)(2,1)} %grad_ref.1) | copy-start | bytes 1572868
  7.2 12.9 %copy-start.2 = (bf16[128,2048]{1,0:T(8,128)(2,1)S(1)}, bf16[128,2048]{1,0:T(8,128)(2,1)}, u32[]{:S(2)}) copy-start(bf16[128,2048]{1,0:T(8,128)(2,1)} %gate_ref.1) | copy-start | bytes 1572868
  7.2 12.9 %copy-start.3 = (bf16[128,2048]{1,0:T(8,128)(2,1)S(1)}, bf16[128,2048]{1,0:T(8,128)(2,1)}, u32[]{:S(2)}) copy-start(bf16[128,2048]{1,0:T(8,128)(2,1)} %long_ref.1) | copy-start | bytes 1572868
  7.2 12.9 %copy-start.4 = (bf16[32,4096]{1,0:T(8,128)(2,1)S(1)}, bf16[32,4096]{1,0:T(8,128)(2,1)}, u32[]{:S(2)}) copy-start(bf16[32,4096]{1,0:T(8,128)(2,1)} %weight_ref.1) | copy-start | bytes 786436
  7.3 87.2 %all-to-all-start = ((bf16[64,5,32,128]{3,2,1,0:T(8,128)(2,1)}), bf16[64,5,32,128]{3,2,1,0:T(8,128)(2,1)}, u32[]{:S(2)}, u32[]{:S(2)}) async-start(bf16[64,5,32,128]{3,2,1,0:T(8,128)(2,1)} %bitcast.17), calls=%async_computation | async-start | bytes 5242880 | tf_op jit(solution)/shard_map/all_to_all | solution.py:679
  93.6 0.8 copy-start.5
  141.2 37.7 %all-to-all-start.1 = ((bf16[64,144,128]{2,1,0:T(8,128)(2,1)}), bf16[64,144,128]{2,1,0:T(8,128)(2,1)}, u32[]{:S(2)}, u32[]{:S(2)}) async-start(bf16[64,144,128]{2,1,0:T(8,128)(2,1)} %finish.1), calls=%async_computation.1 | async-start | bytes 4718592 | tf_op jit(solution)/shard_map/all_to_all | solution.py:688

commit v3 on v2

--- a/solution.py
+++ b/solution.py
@@ -134,78 +134,50 @@
 def finish_kernel(
     late_ref, spec_ref, gates_ref, bands_ref, turned_ref,
     first_ref, twists_ref, forward_ref, inverse_ref, last_ref,
-    out_ref,
-    lines, zh, zl, ch, cl, results, sums,
+    back_ref,
+    lines, zh, zl, ch, cl, results, sums, parcels,
+    local, sends, recvs,
 ):
     rows, width = late_ref.shape[0], late_ref.shape[1]
+    chunk = parcels.shape[3]
     high_row = rows - 1
+    here = Here()
+    me = here.seq
+
+    def target(i):
+        return here.token_peer(i)
+
+    def origin(i):
+        return here.token_peer(i, -1)
+
+    barrier = pltpu.get_barrier_semaphore()
+
+    @pl.loop(1, rows)
+    def _(i):
+        pl.semaphore_signal(
+            barrier, 1, device_id={"seq": target(i), "ch": here.y_hi}, device_id_type=MESH
+        )
 
     @pl.loop(0, rows)
     def _(i):
         at = pl.ds(pl.multiple_of(i * width, width), width)
         lines[at, :] = late_ref[i].astype(F32)
 
-    @pl.loop(0, width // 2)
-    def _(c):
-        pair = jnp.concatenate(
-            [lines[pl.ds(2 * c + k, rows, stride=width), :] for k in range(2)], 1
-        ).astype(BF16)
-        for k, part in enumerate(outer_stage(pair, first_ref[...], twists_ref[...])):
-            high, low = split(part)
-            there = pl.ds(pl.multiple_of((2 * c + k) * rows, rows), rows)
-            zh[there, :] = high
-            zl[there, :] = low
-
     many = 4
     step = many * rows
-
-    @pl.loop(0, width // many)
-    def _(b):
-        at = pl.ds(pl.multiple_of(b * step, step), step)
-        grad = dot3(zh[at, :], zl[at, :], forward_ref[...])
-        grad_real, grad_imag = grad[:, :LANES], grad[:, LANES:]
-        cosine = jnp.concatenate([twists_ref[:, :LANES]] * many, 0)
-        sine = jnp.concatenate([twists_ref[:, LANES:]] * many, 0)
-        reals, imags = [], []
-        for k in range(2):
-            source = 1 - k
-            other = spec_ref[
-                pl.ds(pl.multiple_of(source * rows * width + b * step, step), step), :
-            ]
-            real, imag = other[:, :LANES], other[:, LANES:]
-            term = jnp.concatenate(
-                [real * grad_real + imag * grad_imag, real * grad_imag - imag * grad_real], 1
-            )
-            back = dot3(*split(term), inverse_ref[...])
-            real, imag = back[:, :LANES], back[:, LANES:]
-            reals.append(real * cosine - imag * sine)
-            imags.append(real * sine + imag * cosine)
-        real, imag = jnp.concatenate(reals, 1), jnp.concatenate(imags, 1)
-        for k in range(many):
-            both = jnp.concatenate(
-                [real[k * rows : (k + 1) * rows], imag[k * rows : (k + 1) * rows]], 0
-            )
-            high, low = split(both)
-            there = pl.ds(
-                pl.multiple_of((b * many + k) * 2 * rows, 2 * rows), 2 * rows
-            )
-            ch[there, :] = high
-            cl[there, :] = low
-
     row = lax.broadcasted_iota(jnp.int32, (rows, LANES), 0)
 
     def with_next(x):
         following = jnp.where(row == high_row, 0.0, pltpu.roll(x, high_row, 0))
         return jnp.concatenate([x, following], 1).astype(BF16)
 
-    def diagonals(c, k, both):
-        wide = pl.ds(pl.multiple_of(c * LANES, LANES), LANES)
+    def diagonals(wide, k, both):
         products = dot(turned_ref[k, wide, :], both)
         slid = pltpu.roll(products, 0, 1, stride=1, stride_axis=0)
         return jnp.sum(slid, axis=0, keepdims=True)
 
-    def channel(c):
-        there = pl.ds(pl.multiple_of(c * 2 * rows, 2 * rows), 2 * rows)
+    def channel(c, within):
+        there = pl.ds(pl.multiple_of(within * 2 * rows, 2 * rows), 2 * rows)
         mine = pl.ds(pl.multiple_of(c * rows, rows), rows)
         wide = pl.ds(pl.multiple_of(c * LANES, LANES), LANES)
         high, low = ch[there, :], cl[there, :]
@@ -216,33 +188,108 @@
         short_grad = dot_t(both, bands_ref[0, wide, :]).astype(BF16).astype(F32)
         pair = with_next(short_grad)
         grad_input = dot_t(pair, bands_ref[1, wide, :])
-        pick = pl.ds(c, rows, stride=width)
+        pick = pl.ds(within, rows, stride=chunk)
         results[0, pick, :] = point * gates_ref[1, mine, :]
         results[1, pick, :] = grad_input
         results[2, pick, :] = filt
-        sums[0, pl.ds(c, 1), :] = diagonals(c, 0, both)
-        sums[1, pl.ds(c, 1), :] = diagonals(c, 1, pair)
-
-    unroll = 4
-
-    @pl.loop(0, width // unroll)
-    def _(b):
-        for k in range(unroll):
-            channel(b * unroll + k)
+        sums[0, pl.ds(c, 1), :] = diagonals(wide, 0, both)
+        sums[1, pl.ds(c, 1), :] = diagonals(wide, 1, pair)
+
+    def compute(start):
+        @pl.loop(0, chunk // 2)
+        def _(c):
+            pair = jnp.concatenate(
+                [lines[pl.ds(start + 2 * c + k, rows, stride=width), :] for k in range(2)], 1
+            ).astype(BF16)
+            for k, part in enumerate(outer_stage(pair, first_ref[...], twists_ref[...])):
+                high, low = split(part)
+                there = pl.ds(pl.multiple_of((2 * c + k) * rows, rows), rows)
+                zh[there, :] = high
+                zl[there, :] = low
+
+        @pl.loop(0, chunk // many)
+        def _(b):
+            at = pl.ds(pl.multiple_of(b * step, step), step)
+            grad = dot3(zh[at, :], zl[at, :], forward_ref[...])
+            grad_real, grad_imag = grad[:, :LANES], grad[:, LANES:]
+            cosine = jnp.concatenate([twists_ref[:, :LANES]] * many, 0)
+            sine = jnp.concatenate([twists_ref[:, LANES:]] * many, 0)
+            reals, imags = [], []
+            for k in range(2):
+                place = (1 - k) * rows * width + start * rows + b * step
+                other = spec_ref[pl.ds(pl.multiple_of(place, step), step), :]
+                real, imag = other[:, :LANES], other[:, LANES:]
+                term = jnp.concatenate(
+                    [real * grad_real + imag * grad_imag, real * grad_imag - imag * grad_real], 1
+                )
+                back = dot3(*split(term), inverse_ref[...])
+                real, imag = back[:, :LANES], back[:, LANES:]
+                reals.append(real * cosine - imag * sine)
+                imags.append(real * sine + imag * cosine)
+            real, imag = jnp.concatenate(reals, 1), jnp.concatenate(imags, 1)
+            for k in range(many):
+                both = jnp.concatenate(
+                    [real[k * rows : (k + 1) * rows], imag[k * rows : (k + 1) * rows]], 0
+                )
+                high, low = split(both)
+                there = pl.ds(
+                    pl.multiple_of((b * many + k) * 2 * rows, 2 * rows), 2 * rows
+                )
+                ch[there, :] = high
+                cl[there, :] = low
+
+        @pl.loop(0, chunk // many)
+        def _(b):
+            for k in range(many):
+                within = b * many + k
+                channel(start + within, within)
 
     factor = (rows * LANES) ** -0.5
-    lags = [pltpu.roll(sums[k], LANES + 1, 1)[:, :LANES] * factor for k in range(2)]
-    medium = lags[0].astype(BF16)
-    square = jnp.concatenate([lags[1], jnp.zeros((LANES - width, LANES), F32)], 0)
-    short = square.T[:PAD].astype(BF16)
-
-    @pl.loop(0, rows)
-    def _(i):
-        at = pl.ds(pl.multiple_of(i * width, width), width)
-        for k in range(3):
-            out_ref[i, k * width : (k + 1) * width] = results[k, at, :].astype(BF16)
-        out_ref[i, 3 * width : 4 * width] = medium
-        out_ref[i, 4 * width :] = short
+    parts = back_ref.shape[1]
+
+    def parcel(ref, k):
+        return ref.at[k] if k == parts - 1 else ref.at[k, pl.ds(0, 4)]
+
+    for k in range(parts):
+        compute(k * chunk)
+        lags = pltpu.roll(sums[0, k * chunk : (k + 1) * chunk], LANES + 1, 1)[:, :LANES]
+        medium = (lags * factor).astype(BF16)
+        if k == parts - 1:
+            lags = pltpu.roll(sums[1], LANES + 1, 1)[:, :LANES] * factor
+            square = jnp.concatenate([lags, jnp.zeros((LANES - width, LANES), F32)], 0)
+            short = square.T[:chunk].astype(BF16)
+
+        @pl.loop(0, rows)
+        def _(i):
+            at = pl.ds(pl.multiple_of(i * chunk, chunk), chunk)
+            for a in range(3):
+                parcels[i, k, a] = results[a, at, :].astype(BF16)
+            parcels[i, k, 3] = medium
+            if k == parts - 1:
+                parcels[i, k, 4] = short
+
+        if k == 0:
+            pl.semaphore_wait(barrier, rows - 1)
+
+        @pl.loop(1, rows)
+        def _(i):
+            to = target(i)
+            send(
+                parcel(parcels.at[to], k), parcel(back_ref.at[me], k),
+                sends.at[k, i], recvs.at[k, i], {"seq": to, "ch": here.y_hi},
+            )
+
+        pltpu.make_async_copy(
+            parcel(parcels.at[me], k), parcel(back_ref.at[me], k), local.at[k]
+        ).start()
+
+    for k in range(parts):
+        await_bytes(parcel(back_ref.at[me], k), local.at[k])
+
+        @pl.loop(1, rows)
+        def _(i):
+            await_bytes(parcel(back_ref.at[origin(i)], k), recvs.at[k, i])
+            await_bytes(parcel(parcels.at[me], k), sends.at[k, i])
 
 
 def whole(n):
@@ -276,21 +323,27 @@
 def finish(late, spec, gates, bands, turned, first, twists, forward, inverse, last):
     rows, width, _ = late.shape
     area = rows * width
+    chunk = width // 2
+    dma = pltpu.SemaphoreType.DMA
     return pl.pallas_call(
         finish_kernel,
-        out_shape=jax.ShapeDtypeStruct((rows, 4 * width + PAD, LANES), BF16),
+        out_shape=jax.ShapeDtypeStruct((rows, 2, 5, chunk, LANES), BF16),
         in_specs=whole(10),
-        out_specs=whole(1)[0],
+        out_specs=pl.BlockSpec(memory_space=pl.ANY),
         scratch_shapes=[
             pltpu.VMEM((area, LANES), F32),
+            pltpu.VMEM((area // 2, 2 * LANES), BF16),
+            pltpu.VMEM((area // 2, 2 * LANES), BF16),
             pltpu.VMEM((area, 2 * LANES), BF16),
             pltpu.VMEM((area, 2 * LANES), BF16),
-            pltpu.VMEM((2 * area, 2 * LANES), BF16),
-            pltpu.VMEM((2 * area, 2 * LANES), BF16),
-            pltpu.VMEM((3, area, LANES), F32),
+            pltpu.VMEM((3, area // 2, LANES), F32),
             pltpu.VMEM((2, width, 2 * LANES), F32),
+            pltpu.VMEM((rows, 2, 5, chunk, LANES), BF16),
+            dma((2,)), dma((2, rows)), dma((2, rows)),
         ],
-        compiler_params=pltpu.CompilerParams(vmem_limit_bytes=VMEM_LIMIT),
+        compiler_params=pltpu.CompilerParams(
+            collective_id=1, has_side_effects=True, vmem_limit_bytes=VMEM_LIMIT
+        ),
         cost_estimate=pl.CostEstimate(flops=8 * 10**9, bytes_accessed=20 * 2**20, transcendentals=0),
         name="finish",
     )(late, spec, gates, bands, turned, first, twists, forward, inverse, last)
@@ -329,30 +382,33 @@
 
 
 def unturn_kernel(in_ref, *outs):
-    blocks, height = in_ref.shape[1], in_ref.shape[4]
-    width = outs[0].shape[1] // blocks
+    height = in_ref.shape[6]
     for k, out in enumerate(outs):
-        block = in_ref[0, :, 0, k * width : (k + 1) * width].astype(F32)
-        out[...] = block.reshape(blocks * width, height).T.astype(out.dtype)
-
-
-def from_blocks(block, width, dtypes):
-    devices, lines, height = block.shape
+        block = in_ref[0, :, 0, :, k].astype(F32)
+        out[...] = block.reshape(out.shape[1], height).T.astype(out.dtype)
+
+
+def from_blocks(block, dtypes):
+    devices, parts, items, chunk, height = block.shape
     span = PLANE // 2
     count = len(dtypes)
+    width = parts * chunk
     return pl.pallas_call(
         unturn_kernel,
         grid=(devices // span,),
         out_shape=[jax.ShapeDtypeStruct((height, devices * width), t) for t in dtypes],
         in_specs=[
-            pl.BlockSpec((1, span, 1, lines, height), lambda i: (*block_place(i), 0, 0))
+            pl.BlockSpec(
+                (1, span, 1, parts, items, chunk, height),
+                lambda i: (*block_place(i), 0, 0, 0, 0),
+            )
         ],
         out_specs=[pl.BlockSpec((height, span * width), lambda i: (0, i))] * count,
         cost_estimate=pl.CostEstimate(
             flops=0, bytes_accessed=8 * count * height * devices * width, transcendentals=0
         ),
         name="from_blocks",
-    )(block.reshape(2, PLANE, 2, lines, height))
+    )(block.reshape(2, PLANE, 2, parts, items, chunk, height))
 
 
 def wrap(i):
@@ -362,12 +418,20 @@
 class Here:
     def __init__(self):
         seq = lax.axis_index("seq")
+        self.seq = seq
         self.y_hi = lax.axis_index("ch")
         self.core = seq % 2
         self.z = (seq // 2) % SIDE
         self.x = (seq // (2 * SIDE)) % SIDE
         self.y_lo = seq // (2 * PLANE)
         self.y = self.y_hi * 2 + self.y_lo
+
+    def token_peer(self, i, sign=1):
+        core = (self.core + i) % 2
+        z = wrap(self.z + sign * ((i // 2) % SIDE))
+        x = wrap(self.x + sign * ((i // (2 * SIDE)) % SIDE))
+        y_lo = (self.y_lo + i // (2 * PLANE)) % 2
+        return ((y_lo * SIDE + x) * SIDE + z) * 2 + core
 
     def at(self, x=None, y=None, z=None, core=None):
         x = self.x if x is None else x
@@ -685,11 +749,10 @@
     grad_outer, late = project(out_grad, out_weight, outer_gate, long_out)
     spec, gates, bands, turned = prepare(early, taps, first, twists, forward, flip)
     results = finish(late, spec, gates, bands, turned, first, twists, forward, inverse, last)
-    results = lax.all_to_all(results, "seq", 0, 0, tiled=True)
     grad_inner, grad_input, grad_filter, grad_medium = from_blocks(
-        results, width, (BF16, BF16, F32, F32)
+        results, (BF16, BF16, F32, F32)
     )
-    short = results[:, 4 * width : 4 * width + SHORT, :width]
+    short = results[:, 1, 4, :SHORT, :width]
     short = short.reshape(2, PLANE, 2, SHORT, width).transpose(3, 0, 2, 1, 4)
     grad_short = short.reshape(SHORT, channels).astype(F32)
     return grad_outer, grad_inner, grad_input, grad_filter, grad_short, grad_medium

time: 189 us -> 177 us (0.937)
  waiting for transfers between devices: 31.2 us -> 0.01 us
  Pallas kernels: 133 us -> 160 us
  starting transfers between devices: 17.7 us -> 11.1 us
    all_to_all x1 -> x0, waiting for transfers between devices: 31.2 us -> none  [per_device(): results = lax.all_to_all(results, 'seq', 0, 0, tiled=True)]
    pallas_call x1, Pallas kernels: 26.8 us -> 52.8 us  [finish(): pl.pallas_call(finish_kernel, out_shape=jax.ShapeDtypeStruct((rows, 2, 5,...]
    all_to_all x1 -> x0, starting transfers between devices: 6.56 us -> none  [per_device(): results = lax.all_to_all(results, 'seq', 0, 0, tiled=True)]
  transfers between devices with their start and end apart: 2 -> 1, of which waited for: 1 -> 0; matrix products, arithmetic and copies ran while one was open for 1% -> 1% of each run, Pallas kernels for 39% -> 42%
where the time goes in v3:
time: 177 us
  Pallas kernels  160 us (90%)
  starting transfers between devices  11.1 us (6%)
  local copies, waits for them, and re-layouts  4.41 us (2%)
    pallas_call x1, Pallas kernels, project(): pl.pallas_call(project_kernel, out_shape=(jax.ShapeDtypeStruct((height, h...  74.1 us
    pallas_call x1, Pallas kernels, finish(): pl.pallas_call(finish_kernel, out_shape=jax.ShapeDtypeStruct((rows, 2, 5,...  52.8 us
    pallas_call x1, Pallas kernels, prepare(): pl.pallas_call(prepare_kernel, out_shape=(jax.ShapeDtypeStruct((2 * area,...  20 us
    all_to_all x1, starting transfers between devices, per_device(): early = lax.all_to_all(early, 'seq', 0, 0, tiled=True)  11.1 us
    pallas_call x1, Pallas kernels, to_blocks(): pl.pallas_call(turn_kernel, grid=(devices // span,), out_shape=jax.ShapeD...  6.59 us
    pallas_call x1, Pallas kernels, from_blocks(): pl.pallas_call(unturn_kernel, grid=(devices // span,), out_shape=[jax.Sha...  6.31 us
  transfers between devices with their start and end apart: 1, of which 0 were waited for; matrix products, arithmetic and copies ran while one was open for 1% of the time, Pallas kernels for 42%

profile of v3, /device:TPU:1, one launch (start us, length us, event | category | flops | bytes accessed | tf_op | source)
XLA Modules:
  0.0 176.7 jit_solution(6107951285342806215)
XLA Ops:
  0.6 0.0 copy-start
  0.6 6.6 %to_blocks.1 = bf16[2,16,2,5,32,128]{5,4,3,2,1,0:T(8,128)(2,1)} custom-call(bf16[128,2048]{1,0:T(8,128)(2,1)} %refs_0_.1, bf16[128,2048]{1,0:T(8,128)(2,1)} %refs_1_.1, bf16[128,2048]{1,0:T(8,128)(2,1)} %refs_2_.1, bf16[128,2048]{1,0:T(8,128)(2,1)} %refs_3_.1, bf16[128,2048]{1,0:T(8,128)(2,1)} %refs_4_.1), custom_call_target="tpu_custom_call" | custom-call | bytes 5242880 | tf_op jit(solution)/shard_map/to_blocks/pallas_call | solution.py:368
  7.2 0.0 copy-start.1
  7.2 0.0 copy-start.2
  7.2 0.0 copy-start.3
  7.2 0.0 copy-start.4
  7.3 11.1 %all-to-all-start = ((bf16[64,5,32,128]{3,2,1,0:T(8,128)(2,1)}), bf16[64,5,32,128]{3,2,1,0:T(8,128)(2,1)}, u32[]{:S(2)}, u32[]{:S(2)}) async-start(bf16[64,5,32,128]{3,2,1,0:T(8,128)(2,1)} %bitcast.17), calls=%async_computation | async-start | bytes 5242880 | tf_op jit(solution)/shard_map/all_to_all | solution.py:743
  18.5 0.0 copy-done
  18.5 0.1 constant_dynamic-slice_fusion.1
  18.6 0.1 copy.26
  18.7 0.8 constant_dynamic-slice_fusion
  19.4 0.1 copy.27
  19.5 0.0 copy-done.1
  19.5 0.0 copy-done.2
  19.5 0.0 copy-done.3
  19.5 0.0 copy-done.4
  19.6 74.1 %project.1 = (bf16[128,2048]{1,0:T(8,128)(2,1)S(1)}, bf16[2,16,2,32,128]{4,3,2,1,0:T(8,128)(2,1)S(1)}) custom-call(bf16[128,2048]{1,0:T(8,128)(2,1)S(1)} %copy-done.1, bf16[32,4096]{1,0:T(8,128)(2,1)S(1)} %copy-done.4, bf16[128,2048]{1,0:T(8,128)(2,1)S(1)} %copy-done.2, bf16[128,2048]{1,0:T(8,128)(2,1)S(1)} %copy-done.3), custom_call_target="tpu_custom_call" | custom-call | flops 2147483648 | bytes 16777216 | tf_op jit(solution)/shard_map/project/pallas_call | solution.py:702
  93.6 0.0 copy-start.5
  93.6 0.8 copy-done.5
  94.4 0.6 maximum_convert_fusion.taps_ref
  95.0 0.0 all-to-all-done.early_ref
  95.0 20.0 %prepare.1 = (f32[4096,256]{1,0:T(8,128)}, f32[2,2048,128]{2,1,0:T(8,128)}, bf16[2,4096,256]{2,1,0:T(8,128)(2,1)}, bf16[2,4096,64]{2,1,0:T(8,128)(2,1)}) custom-call(bf16[64,5,32,128]{3,2,1,0:T(8,128)(2,1)} %all-to-all-done.early_ref, f32[2,32,128]{2,1,0:T(8,128)} %maximum_convert_fusion.taps_ref, bf16[128,128]{1,0:T(8,128)(2,1)} %constant.83.clone.first_ref, ...), custom_call_target="tpu_custom_call" | custom-call | flops 4000000000 | bytes 20971520 | tf_op jit(solution)/shard_map/prepare/pallas_call | solution.py:302
  115.0 52.8 %finish.1 = bf16[64,2,5,16,128]{4,3,2,1,0:T(8,128)(2,1)} custom-call(bf16[64,32,128]{2,1,0:T(8,128)(2,1)} %bitcast.16, f32[4096,256]{1,0:T(8,128)} %get-tuple-element.18.spec_ref, f32[2,2048,128]{2,1,0:T(8,128)} %get-tuple-element.19.gates_ref, bf16[2,4096,256]{2,1,0:T(8,128)(2,1)} %get-tuple-element.20.bands_ref, ...), custom_call_target="tpu_custom_call" | custom-call | flops 8000000000 | bytes 20971520 | tf_op jit(solution)/shard_map/finish/pallas_call | solution.py:328
  167.8 0.9 slice.3
  168.8 6.3 %from_blocks.1 = (bf16[128,2048]{1,0:T(8,128)(2,1)}, bf16[128,2048]{1,0:T(8,128)(2,1)}, f32[128,2048]{1,0:T(8,128)}, f32[128,2048]{1,0:T(8,128)}) custom-call(bf16[2,16,2,2,5,16,128]{6,5,4,3,2,1,0:T(8,128)(2,1)} %bitcast.18), custom_call_target="tpu_custom_call" | custom-call | bytes 8388608 | tf_op jit(solution)/shard_map/from_blocks/pallas_call | solution.py:396
  175.1 0.1 copy.25
  175.2 0.8 reshape.29
  175.9 0.8 copy.29
  (2 shorter events, 0.0 us)
Async XLA Ops:
  0.6 17.9 %copy-start = (bf16[128,2048]{1,0:T(8,128)(2,1)S(1)}, bf16[128,2048]{1,0:T(8,128)(2,1)}, u32[]{:S(2)}) copy-start(bf16[128,2048]{1,0:T(8,128)(2,1)} %param.27) | copy-start | bytes 1572868
  7.2 12.3 %copy-start.1 = (bf16[128,2048]{1,0:T(8,128)(2,1)S(1)}, bf16[128,2048]{1,0:T(8,128)(2,1)}, u32[]{:S(2)}) copy-start(bf16[128,2048]{1,0:T(8,128)(2,1)} %grad_ref.1) | copy-start | bytes 1572868
  7.2 12.3 %copy-start.2 = (bf16[128,2048]{1,0:T(8,128)(2,1)S(1)}, bf16[128,2048]{1,0:T(8,128)(2,1)}, u32[]{:S(2)}) copy-start(bf16[128,2048]{1,0:T(8,128)(2,1)} %gate_ref.1) | copy-start | bytes 1572868
  7.2 12.3 %copy-start.3 = (bf16[128,2048]{1,0:T(8,128)(2,1)S(1)}, bf16[128,2048]{1,0:T(8,128)(2,1)}, u32[]{:S(2)}) copy-start(bf16[128,2048]{1,0:T(8,128)(2,1)} %long_ref.1) | copy-start | bytes 1572868
  7.2 12.3 %copy-start.4 = (bf16[32,4096]{1,0:T(8,128)(2,1)S(1)}, bf16[32,4096]{1,0:T(8,128)(2,1)}, u32[]{:S(2)}) copy-start(bf16[32,4096]{1,0:T(8,128)(2,1)} %weight_ref.1) | copy-start | bytes 786436
  7.3 87.8 %all-to-all-start = ((bf16[64,5,32,128]{3,2,1,0:T(8,128)(2,1)}), bf16[64,5,32,128]{3,2,1,0:T(8,128)(2,1)}, u32[]{:S(2)}, u32[]{:S(2)}) async-start(bf16[64,5,32,128]{3,2,1,0:T(8,128)(2,1)} %bitcast.17), calls=%async_computation | async-start | bytes 5242880 | tf_op jit(solution)/shard_map/all_to_all | solution.py:743
  93.6 0.8 copy-start.5

commit v4 on v2

v4 whole, which is shorter than its diff:
```python
import math

import jax
import jax.numpy as jnp
import numpy as np
from jax import lax
from jax.experimental import pallas as pl
from jax.experimental.pallas import tpu as pltpu
from jax.sharding import PartitionSpec as P

SHORT = 7
MEDIUM = 128
LANES = 128
F32 = jnp.float32
BF16 = jnp.bfloat16
VMEM_LIMIT = 60 * 1024 * 1024
PAD = 16
SIDE = 4
PLANE = SIDE * SIDE
MESH = pl.DeviceIdType.MESH


def split_np(table):
    high = table.astype(np.float32).astype(jnp.bfloat16)
    low = (table - high.astype(np.float64)).astype(np.float32).astype(jnp.bfloat16)
    return high, low


def tables(rows):
    total = 2 * rows * LANES
    freq = np.arange(rows)[:, None] + 0.5
    place = np.arange(rows)[None, :]
    angle = 2.0 * np.pi * freq * place / (2 * rows)
    first = np.concatenate([np.cos(angle), -np.sin(angle)], 0)
    first = np.concatenate(split_np(first), 1)
    twist = 2.0 * np.pi * freq * np.arange(LANES)[None, :] / total
    inner = 2.0 * np.pi * np.outer(np.arange(LANES), np.arange(LANES)) / LANES
    cosine, sine = np.cos(inner), np.sin(inner)
    forward = np.block([[cosine, -sine], [sine, cosine]])
    inverse = np.block([[cosine, sine], [-sine, cosine]])
    scale = (rows * LANES) ** -0.5 * 2.0 / total
    last = np.concatenate([np.cos(angle.T), -np.sin(angle.T)], 1) * scale
    twists = np.concatenate([np.cos(twist), np.sin(twist)], 1).astype(np.float32)
    flip = np.eye(LANES)[::-1].astype(jnp.bfloat16)
    return (
        first,
        twists,
        np.concatenate(split_np(forward), 0),
        np.concatenate(split_np(inverse), 0),
        np.concatenate(split_np(last), 0),
        flip,
    )


def dot(a, b):
    return jnp.dot(a, b, preferred_element_type=F32)


def dot_t(a, b):
    return lax.dot_general(a, b, (((1,), (1,)), ((), ())), preferred_element_type=F32)


def split(x):
    high = x.astype(BF16)
    return high, (x - high.astype(F32)).astype(BF16)


def dot3(high, low, table):
    size = table.shape[0] // 2
    return dot(high, table[:size]) + dot(high, table[size:]) + dot(low, table[:size])


def outer_stage(pair, first, twists):
    rows = pair.shape[0]
    spread = dot(first, jnp.concatenate([pair, pair], 0))
    cosine = jnp.concatenate([twists[:, :LANES]] * 2, 1)
    sine = jnp.concatenate([twists[:, LANES:]] * 2, 1)
    real, imag = spread[:rows], spread[rows:]
    new_real = real * cosine + imag * sine
    new_imag = imag * cosine - real * sine
    return (
        jnp.concatenate([new_real[:, :LANES], new_imag[:, :LANES]], 1),
        jnp.concatenate([new_real[:, LANES:], new_imag[:, LANES:]], 1),
    )


def toeplitz(line):
    row = jnp.concatenate([line, jnp.zeros_like(line)], 1)
    block = jnp.broadcast_to(row, (LANES, 2 * LANES))
    return pltpu.roll(block, 0, 1, stride=1, stride_axis=0)


def wrap(i):
    return lax.rem(i + SIDE, SIDE)


class Here:
    def __init__(self):
        seq = lax.axis_index("seq")
        self.seq = seq
        self.y_hi = lax.axis_index("ch")
        self.core = seq % 2
        self.z = (seq // 2) % SIDE
        self.x = (seq // (2 * SIDE)) % SIDE
        self.y_lo = seq // (2 * PLANE)
        self.y = self.y_hi * 2 + self.y_lo

    def token_peers(self):
        xs = [wrap(self.x + d) for d in range(SIDE)]
        zs = [wrap(self.z + d) for d in range(SIDE)]
        cores, ys = [self.core, 1 - self.core], [self.y_lo, 1 - self.y_lo]
        for dx in range(SIDE):
            for dz in range(SIDE):
                for dy in range(2):
                    for dc in range(2):
                        if dx or dz or dy or dc:
                            cell = xs[dx] * SIDE + zs[dz]
                            yield (
                                (ys[dy] * PLANE + cell) * 2 + cores[dc],
                                (ys[dy] * 2 + cores[dc]) * PLANE + cell,
                            )

    def at(self, x=None, y=None, z=None, core=None):
        x = self.x if x is None else x
        y = self.y if y is None else y
        z = self.z if z is None else z
        core = self.core if core is None else core
        seq = (((y % 2) * SIDE + x) * SIDE + z) * 2 + core
        return {"seq": seq, "ch": y // 2}


def send(source, target, sends, recvs, device):
    copy = pltpu.make_async_remote_copy(
        src_ref=source,
        dst_ref=target,
        send_sem=sends,
        recv_sem=recvs,
        device_id=device,
        device_id_type=MESH,
    )
    copy.start()


def await_bytes(ref, sem):
    pltpu.make_async_copy(ref, ref, sem).wait()


class Ring:
    def __init__(self, here, axis, item, half, sends, recvs, source=None):
        self.at = lambda p: here.at(**{axis: p})
        self.place = getattr(here, axis)
        self.item, self.half = item, half
        self.sends, self.recvs = sends, recvs
        self.source = item(self.place) if source is None else source

    def step(self, i, source, target, to):
        send(source, target, self.sends.at[i], self.recvs.at[i], self.at(wrap(self.place + to)))

    def start(self):
        self.step(0, self.source, self.item(self.place), 1)
        self.step(1, self.source, self.item(self.place), -1)

    def relay(self):
        for i, to in ((0, 1), (1, -1)):
            other = wrap(self.place - to)
            await_bytes(self.item(other), self.recvs.at[i])
            half = self.half(self.item(other), i)
            self.step(2 + i, half, half, to)

    def finish(self):
        opposite = self.item(wrap(self.place + 2))
        for i in range(2):
            await_bytes(self.half(opposite, i), self.recvs.at[2 + i])

    def drain(self):
        opposite = self.item(wrap(self.place + 2))
        for i in range(2):
            await_bytes(self.item(self.place), self.sends.at[i])
            await_bytes(self.half(opposite, i), self.sends.at[2 + i])


def block_kernel(
    grad_ref, weight_ref, gate_ref, long_ref,
    inner_ref, medium_ref, short_ref, conv_ref, filter_ref, taps_ref,
    first_ref, twists_ref, forward_ref, inverse_ref, last_ref, flip_ref,
    outer_ref, back_ref, lags_ref,
    feats, weights, gates, total, turned, hidden, arrived,
    one_out, one_in, two_out, two_in, late,
    lines, zh, zl, gh, gl, spec, bands, saved, points, results, sums, parcels,
    local, spread_s, spread_r, gate_s, gate_r, feat_s, feat_r, pass_s, pass_r,
    ring_s, ring_r, late_sem, hidden_s, hidden_r, batch_s, batch_r, lag_s, lag_r,
):
    here = Here()
    me = here.y_lo * 2 + here.core
    cell = here.x * SIDE + here.z
    block = me * PLANE + cell
    columns = gates.shape[2]
    height = grad_ref.shape[0]
    rows, width = one_in.shape[0], one_in.shape[2]
    area = rows * width
    chunk = width // 2
    partner = here.at(core=1 - here.core)
    peers = list(here.token_peers())

    def column_peers():
        for dy in range(SIDE):
            for dc in range(2):
                if dy or dc:
                    yield dy * 2 + dc - 1, wrap(here.y + dy), (here.core + dc) % 2

    def plane_peers():
        for dx in range(SIDE):
            for dz in range(SIDE):
                if dx or dz:
                    yield wrap(here.x + dx), wrap(here.z + dz)

    barrier = pltpu.get_barrier_semaphore()
    for seq, _ in peers:
        pl.semaphore_signal(
            barrier, 1, device_id={"seq": seq, "ch": here.y_hi}, device_id_type=MESH
        )
    for y_lo in range(2):
        for core in range(2):
            there = here.at(y=(1 - here.y_hi) * 2 + y_lo, core=core)
            pl.semaphore_signal(barrier, 1, device_id=there, device_id_type=MESH)
    pl.semaphore_wait(barrier, len(peers) + 4)

    def weight_columns(y, core):
        return weight_ref.at[:, pl.ds(pl.multiple_of((y * 2 + core) * columns, columns), columns)]

    def gate_columns(index):
        return gate_ref.at[:, pl.ds(pl.multiple_of(index * columns, columns), columns)]

    own_rows = weights.at[here.y_lo, here.x, here.z, here.core * 2 + here.y_hi]
    for i, y, core in column_peers():
        send(
            weight_columns(y, core), own_rows, spread_s.at[i], spread_r.at[i],
            here.at(y=y, core=core),
        )
    copies = [
        pltpu.make_async_copy(weight_columns(here.y, here.core), own_rows, local.at[0]),
        pltpu.make_async_copy(grad_ref, feats.at[here.y_hi, me], local.at[1]),
        pltpu.make_async_copy(gate_columns(me), gates.at[me], local.at[2]),
    ]
    for copy in copies:
        copy.start()

    def half_tokens(ref, i):
        return ref.at[pl.ds(i * (height // 2), height // 2)]

    def feat(y, core):
        return feats.at[y // 2, (y % 2) * 2 + core]

    features = Ring(
        here, "y", lambda y: feat(y, here.core), half_tokens, feat_s, feat_r, source=grad_ref
    )
    features.start()

    def pass_on(i, y):
        source = grad_ref if i == 0 else feat(y, here.core)
        send(source, feat(y, here.core), pass_s.at[i], pass_r.at[i], partner)

    pass_on(0, here.y)
    share = [(0, 1), (1, 0), (1, 1)]

    def sharer(dy, dc):
        y_lo, core = (here.y_lo + dy) % 2, (here.core + dc) % 2
        return y_lo * 2 + core, here.at(y=here.y_hi * 2 + y_lo, core=core)

    for i, (dy, dc) in enumerate(share):
        index, device = sharer(dy, dc)
        send(gate_columns(index), gates.at[me], gate_s.at[i], gate_r.at[i], device)

    def exchange(batch, piece, arrive):
        for seq, other in peers:
            send(
                piece(seq, other), arrive, batch_s.at[batch], batch_r.at[batch],
                {"seq": seq, "ch": here.y_hi},
            )
        pltpu.make_async_copy(piece(here.seq, block), arrive, batch_r.at[batch]).start()

    span = 8

    def turn(value, out, k):
        @pl.loop(0, rows // span)
        def _(b):
            part = pl.ds(pl.multiple_of(b * span * width, span * width), span * width)
            lined = value(part).T.astype(BF16).reshape(span, width, height)
            out[pl.ds(b * span, span), k] = lined

    def plain(ref):
        return lambda part: ref[:, part].astype(F32)

    def half_block(ref, i):
        return ref.at[pl.ds(i * 2, 2)]

    def block_ring(k, axis, item):
        return Ring(here, axis, item, half_block, ring_s.at[k], ring_r.at[k])

    first = [
        block_ring(0, "x", lambda x: weights.at[0, x, here.z]),
        block_ring(1, "z", lambda z: weights.at[1, here.x, z]),
    ]
    second = []
    for j, d in enumerate((0, 3, 1, 2)):
        second.append((
            block_ring(2 + 2 * j, "z", lambda z, d=d: weights.at[0, wrap(here.x + d), z]),
            block_ring(3 + 2 * j, "x", lambda x, d=d: weights.at[1, x, wrap(here.z + d)]),
        ))

    turn(lambda part: inner_ref[:, part].astype(F32) * medium_ref[:, part].astype(F32), one_out, 0)
    turn(plain(filter_ref), one_out, 1)

    for i, y, core in column_peers():
        source_y = wrap(2 * here.y - y + SIDE)
        await_bytes(
            weights.at[source_y % 2, here.x, here.z, core * 2 + source_y // 2], spread_r.at[i]
        )
    copies[0].wait()
    for ring in first:
        ring.start()
    for ring in second[0]:
        ring.start()
    exchange(0, lambda seq, other: one_out.at[other], one_in.at[here.seq])

    turn(plain(inner_ref), two_out, 0)
    for ring in first:
        ring.relay()
    for pair in second[1:3]:
        for ring in pair:
            ring.start()
    turn(plain(short_ref), two_out, 1)
    for ring in second[0]:
        ring.relay()
    for ring in first:
        ring.finish()
    for ring in second[3]:
        ring.start()
    turn(plain(conv_ref), two_out, 2)
    features.relay()
    pass_on(1, wrap(here.y - 1))
    pass_on(2, wrap(here.y + 1))

    def make_bands(k):
        @pl.loop(0, width)
        def _(c):
            wide = pl.ds(pl.multiple_of(c * LANES, LANES), LANES)
            bands[k, wide, :] = toeplitz(taps_ref[k, pl.ds(c, 1), :]).astype(BF16)

    make_bands(0)
    for ring in second[1]:
        ring.relay()
    make_bands(1)
    for ring in second[2]:
        ring.relay()

    def unpack(source, planes):
        @pl.loop(0, rows)
        def _(i):
            at = pl.ds(pl.multiple_of(i * width, width), width)
            for k, plane in planes:
                value = source[i] if k is None else source[i, k]
                lines[plane, at, :] = value.astype(F32)

    def keep(parts, places):
        for part, place in zip(parts, places):
            high, low = split(part)
            there = pl.ds(pl.multiple_of(place, rows), rows)
            yield there, high, low

    await_bytes(one_in, batch_r.at[0])
    unpack(one_in, ((0, 0), (1, 1)))
    for ring in second[3]:
        ring.relay()

    def spread_pairs(begin, end):
        @pl.loop(begin, end)
        def _(c):
            pick = pl.ds(c, rows, stride=width)
            pair = jnp.concatenate([lines[0, pick, :], lines[1, pick, :]], 1).astype(BF16)
            parts = outer_stage(pair, first_ref[...], twists_ref[...])
            for there, high, low in keep(parts, (c * rows, area + c * rows)):
                zh[there, :] = high
                zl[there, :] = low

    spread_pairs(0, width // 2)
    features.finish()
    pass_on(3, wrap(here.y + 2))
    spread_pairs(width // 2, width)
    step = 512

    @pl.loop(0, 2 * area // step)
    def _(b):
        at = pl.ds(pl.multiple_of(b * step, step), step)
        spec[at, :] = dot3(zh[at, :], zl[at, :], forward_ref[...])

    for pair in second:
        for ring in pair:
            ring.finish()
    for i, d in enumerate((0, -1, 1, 2)):
        await_bytes(feat(wrap(here.y + d), 1 - here.core), pass_r.at[i])
    copies[1].wait()
    depth = SIDE * weights.shape[3] * weights.shape[4]
    for h in range(2):
        @pl.loop(0, SIDE)
        def _(x):
            part = pl.ds(pl.multiple_of(x * depth, depth), depth)
            left = feats[h, :, :, part].reshape(4 * height, depth)
            term = dot(left, weights[h, x].reshape(depth, columns))
            if h == 0:
                @pl.when(x == 0)
                def _():
                    total[...] = term

                @pl.when(x > 0)
                def _():
                    total[...] += term
            else:
                total[...] += term

    copies[2].wait()
    for i, (dy, dc) in enumerate(share):
        await_bytes(gates.at[sharer(dy, dc)[0]], gate_r.at[i])
    for g in range(4):
        part = total[g * height : (g + 1) * height]
        long_grad = (part * gates[g].astype(F32)).astype(BF16).astype(F32)
        turned[:, g // 2, g % 2] = long_grad.T.astype(BF16).reshape(PLANE, width, height)
        hidden[g] = part.astype(BF16)
    pltpu.make_async_copy(turned.at[cell], late.at[:, cell], late_sem.at[1]).start()
    for x, z in plane_peers():
        send(
            turned.at[x * SIDE + z], late.at[:, cell], late_sem.at[0], late_sem.at[1],
            here.at(x=x, z=z),
        )
    exchange(1, lambda seq, other: two_out.at[other], two_in.at[here.seq])
    for i, (dy, dc) in enumerate(share):
        index, device = sharer(dy, dc)
        send(hidden.at[index], arrived.at[me], hidden_s.at[i], hidden_r.at[i], device)
    own = pltpu.make_async_copy(hidden.at[me], arrived.at[me], local.at[1])
    own.start()

    await_bytes(late, late_sem.at[1])
    for y_lo in range(2):
        @pl.loop(0, PLANE)
        def _(i):
            for core in range(2):
                place = ((y_lo * PLANE + i) * 2 + core) * width
                at = pl.ds(pl.multiple_of(place, width), width)
                lines[2, at, :] = late[y_lo, i, core].astype(F32)

    many = 4
    wide_step = many * rows
    row = lax.broadcasted_iota(jnp.int32, (rows, LANES), 0)

    def transform(start):
        @pl.loop(0, chunk // 2)
        def _(c):
            pair = jnp.concatenate(
                [lines[2, pl.ds(start + 2 * c + k, rows, stride=width), :] for k in range(2)], 1
            ).astype(BF16)
            parts = outer_stage(pair, first_ref[...], twists_ref[...])
            for there, high, low in keep(parts, (2 * c * rows, (2 * c + 1) * rows)):
                gh[there, :] = high
                gl[there, :] = low

        @pl.loop(0, chunk // many)
        def _(b):
            at = pl.ds(pl.multiple_of(b * wide_step, wide_step), wide_step)
            grad = dot3(gh[at, :], gl[at, :], forward_ref[...])
            grad_real, grad_imag = grad[:, :LANES], grad[:, LANES:]
            cosine = jnp.concatenate([twists_ref[:, :LANES]] * many, 0)
            sine = jnp.concatenate([twists_ref[:, LANES:]] * many, 0)
            reals, imags = [], []
            for k in range(2):
                place = (1 - k) * area + start * rows + b * wide_step
                other = spec[pl.ds(pl.multiple_of(place, wide_step), wide_step), :]
                real, imag = other[:, :LANES], other[:, LANES:]
                term = jnp.concatenate(
                    [real * grad_real + imag * grad_imag, real * grad_imag - imag * grad_real], 1
                )
                back = dot3(*split(term), inverse_ref[...])
                real, imag = back[:, :LANES], back[:, LANES:]
                reals.append(real * cosine - imag * sine)
                imags.append(real * sine + imag * cosine)
            real, imag = jnp.concatenate(reals, 1), jnp.concatenate(imags, 1)
            for k in range(many):
                both = jnp.concatenate(
                    [real[k * rows : (k + 1) * rows], imag[k * rows : (k + 1) * rows]], 0
                )
                high, low = split(both)
                there = pl.ds(pl.multiple_of((b * many + k) * 2 * rows, 2 * rows), 2 * rows)
                zh[there, :] = high
                zl[there, :] = low

        @pl.loop(0, chunk // many)
        def _(b):
            for k in range(many):
                within = b * many + k
                c = start + within
                there = pl.ds(pl.multiple_of(within * 2 * rows, 2 * rows), 2 * rows)
                high, low = zh[there, :], zl[there, :]
                both = (
                    dot(last_ref[:rows], high) + dot(last_ref[:rows], low)
                    + dot(last_ref[rows:], high)
                )
                pick = pl.ds(within, rows, stride=chunk)
                points[pl.ds(pl.multiple_of(c * rows, rows), rows), :] = both[:, :LANES]
                results[0, pick, :] = both[:, :LANES]
                results[1, pick, :] = both[:, LANES:]

    def pack(k, source, to):
        @pl.loop(0, rows)
        def _(i):
            at = pl.ds(pl.multiple_of(i * chunk, chunk), chunk)
            for a, b in zip(source, to):
                parcels[i, k, b] = results[a, at, :].astype(BF16)

    def pair_of(ref, k):
        return ref.at[k, pl.ds(0, 2)]

    for k in range(2):
        transform(k * chunk)
        pack(k, (0, 1), (0, 1))
        exchange(2 + k, lambda seq, other: pair_of(parcels.at[seq], k), pair_of(back_ref.at[block], k))

    own.wait()
    for i, (dy, dc) in enumerate(share):
        await_bytes(arrived.at[sharer(dy, dc)[0]], hidden_r.at[i])
    for g in range(4):
        part = slice(g * columns, (g + 1) * columns)
        outer_ref[:, part] = (arrived[g].astype(F32) * long_ref[:, part].astype(F32)).astype(BF16)

    await_bytes(two_in, batch_r.at[1])
    unpack(two_in, ((0, 0), (1, 1), (2, 2)))

    @pl.loop(0, width)
    def _(c):
        wide = pl.ds(pl.multiple_of(c * LANES, LANES), LANES)
        for k in range(2):
            value = lines[1 + k, pl.ds(c, rows, stride=width), :].astype(BF16)
            saved[k, wide, :] = dot_t(flip_ref[...], value).astype(BF16)

    def with_next(x):
        following = jnp.where(row == rows - 1, 0.0, pltpu.roll(x, rows - 1, 0))
        return jnp.concatenate([x, following], 1).astype(BF16)

    def diagonals(wide, k, both):
        products = dot(saved[k, wide, :], both)
        slid = pltpu.roll(products, 0, 1, stride=1, stride_axis=0)
        return jnp.sum(slid, axis=0, keepdims=True)

    def convolve(start):
        @pl.loop(0, chunk // many)
        def _(b):
            for k in range(many):
                within = b * many + k
                c = start + within
                wide = pl.ds(pl.multiple_of(c * LANES, LANES), LANES)
                point = points[pl.ds(pl.multiple_of(c * rows, rows), rows), :]
                gate = lines[0, pl.ds(c, rows, stride=width), :]
                both = with_next((point * gate).astype(BF16).astype(F32))
                short_grad = dot_t(both, bands[0, wide, :]).astype(BF16).astype(F32)
                pair = with_next(short_grad)
                pick = pl.ds(within, rows, stride=chunk)
                results[0, pick, :] = dot_t(pair, bands[1, wide, :])
                sums[0, pl.ds(c, 1), :] = diagonals(wide, 0, both)
                sums[1, pl.ds(c, 1), :] = diagonals(wide, 1, pair)

    for k in range(2):
        convolve(k * chunk)
        pack(k, (0,), (2,))
        exchange(4 + k, lambda seq, other: parcels.at[seq, k, 2], back_ref.at[block, k, 2])

    factor = (rows * LANES) ** -0.5
    lags = [pltpu.roll(sums[k], LANES + 1, 1)[:, :LANES] * factor for k in range(2)]
    square = jnp.concatenate([lags[1], jnp.zeros((LANES - width, LANES), F32)], 0)
    mine = lags_ref.at[here.y_lo, here.core]
    lags_ref[here.y_lo, here.core, here.x, here.z, :width] = lags[0].astype(BF16)
    lags_ref[here.y_lo, here.core, here.x, here.z, width:] = square.T[:PAD].astype(BF16)

    def lag_send(i, ref, device):
        send(ref, ref, lag_s.at[i], lag_r.at[i], device)

    for d in range(1, SIDE):
        lag_send(d - 1, mine.at[here.x, here.z], here.at(x=wrap(here.x + d)))
    for d in range(1, SIDE):
        await_bytes(mine.at[wrap(here.x - d), here.z], lag_r.at[d - 1])
    for d in range(1, SIDE):
        lag_send(2 + d, mine.at[:, here.z], here.at(z=wrap(here.z + d)))
    for d in range(1, SIDE):
        await_bytes(mine.at[:, wrap(here.z - d)], lag_r.at[2 + d])
    across = here.at(y=here.y_hi * 2 + 1 - here.y_lo)
    lag_send(6, mine, across)
    lag_send(7, mine, partner)
    await_bytes(lags_ref.at[1 - here.y_lo, here.core], lag_r.at[6])
    lag_send(8, lags_ref.at[1 - here.y_lo, here.core], partner)
    await_bytes(lags_ref.at[here.y_lo, 1 - here.core], lag_r.at[7])
    await_bytes(lags_ref.at[1 - here.y_lo, 1 - here.core], lag_r.at[8])

    for k in range(2):
        await_bytes(back_ref.at[:, k, pl.ds(0, 2)], batch_r.at[2 + k])
        await_bytes(back_ref.at[:, k, 2], batch_r.at[4 + k])
    most = pl.ds(0, rows - 1)
    await_bytes(one_out.at[most], batch_s.at[0])
    await_bytes(two_out.at[most], batch_s.at[1])
    for k in range(2):
        await_bytes(parcels.at[most, k, pl.ds(0, 2)], batch_s.at[2 + k])
        await_bytes(parcels.at[most, k, 2], batch_s.at[4 + k])
    await_bytes(turned.at[pl.ds(0, PLANE - 1)], late_sem.at[0])
    for i in range(7):
        await_bytes(own_rows, spread_s.at[i])
    for i in range(3):
        await_bytes(gates.at[me], gate_s.at[i])
        await_bytes(hidden.at[me], hidden_s.at[i])
        await_bytes(mine.at[here.x, here.z], lag_s.at[i])
        await_bytes(mine.at[:, here.z], lag_s.at[3 + i])
        await_bytes(mine, lag_s.at[6 + i])
    for i in range(4):
        await_bytes(feats.at[0, 0], pass_s.at[i])
    features.drain()
    for ring in first:
        ring.drain()
    for pair in second:
        for ring in pair:
            ring.drain()


def block_call(grad, weight, gate, long, channelwise, taps, constants):
    height, half = grad.shape
    depth, model = weight.shape
    columns = model // 8
    width = columns // PLANE
    rows = half // width
    area = rows * width
    chunk = width // 2
    anywhere = pl.BlockSpec(memory_space=pl.ANY)
    near = pl.BlockSpec(memory_space=pltpu.VMEM)
    dma = pltpu.SemaphoreType.DMA
    vmem = pltpu.VMEM
    return pl.pallas_call(
        block_kernel,
        out_shape=(
            jax.ShapeDtypeStruct((height, half), BF16),
            jax.ShapeDtypeStruct((rows, 2, 3, chunk, height), BF16),
            jax.ShapeDtypeStruct((2, 2, SIDE, SIDE, width + PAD, height), BF16),
        ),
        in_specs=[anywhere] * 3 + [near] * (7 + len(constants)),
        out_specs=(near, anywhere, near),
        scratch_shapes=[
            vmem((2, 4, height, half), BF16),
            vmem((2, SIDE, SIDE, 4, depth, columns), BF16),
            vmem((4, height, columns), BF16),
            vmem((4 * height, columns), F32),
            vmem((PLANE, 2, 2, width, height), BF16),
            vmem((4, height, columns), BF16),
            vmem((4, height, columns), BF16),
            vmem((rows, 2, width, height), BF16),
            vmem((rows, 2, width, height), BF16),
            vmem((rows, 3, width, height), BF16),
            vmem((rows, 3, width, height), BF16),
            vmem((2, PLANE, 2, width, height), BF16),
            vmem((3, area, height), F32),
            vmem((2 * area, 2 * height), BF16),
            vmem((2 * area, 2 * height), BF16),
            vmem((area // 2, 2 * height), BF16),
            vmem((area // 2, 2 * height), BF16),
            vmem((2 * area, 2 * height), F32),
            vmem((2, width * LANES, 2 * LANES), BF16),
            vmem((2, width * LANES, rows), BF16),
            vmem((area, height), F32),
            vmem((2, area // 2, height), F32),
            vmem((2, width, 2 * LANES), F32),
            vmem((rows, 2, 3, chunk, height), BF16),
            dma((3,)), dma((7,)), dma((7,)), dma((3,)), dma((3,)), dma((4,)), dma((4,)),
            dma((4,)), dma((4,)), dma((10, 4)), dma((10, 4)), dma((2,)), dma((3,)), dma((3,)),
            dma((6,)), dma((6,)), dma((9,)), dma((9,)),
        ],
        compiler_params=pltpu.CompilerParams(
            collective_id=0, has_side_effects=True, vmem_limit_bytes=VMEM_LIMIT
        ),
        cost_estimate=pl.CostEstimate(
            flops=16 * 10**9, bytes_accessed=32 * 2**20, transcendentals=0
        ),
        name="block",
    )(grad, weight, gate, long, *channelwise, taps, *constants)


def unturn_kernel(in_ref, lags_ref, medium_ref, inner_out, input_out, filter_out, lags_out):
    size, height = inner_out.shape[1], in_ref.shape[4]

    def lined(value):
        return value.astype(F32).reshape(size, height).T

    inner_out[...] = (lined(in_ref[:, :, 0]) * medium_ref[...].astype(F32)).astype(BF16)
    filter_out[...] = lined(in_ref[:, :, 1])
    input_out[...] = lined(in_ref[:, :, 2]).astype(BF16)
    lags_out[...] = lined(lags_ref[:, : size // in_ref.shape[0]])


def from_blocks(block, lags, medium_out):
    devices, parts, items, chunk, height = block.shape
    span = 8
    size = span * parts * chunk
    channels = devices * parts * chunk
    rows = pl.BlockSpec((height, size), lambda i: (0, i))
    return pl.pallas_call(
        unturn_kernel,
        grid=(devices // span,),
        out_shape=[
            jax.ShapeDtypeStruct((height, channels), t) for t in (BF16, BF16, F32, F32)
        ],
        in_specs=[
            pl.BlockSpec((span, parts, items, chunk, height), lambda i: (i, 0, 0, 0, 0)),
            pl.BlockSpec((span, lags.shape[1], height), lambda i: (i, 0, 0)),
            rows,
        ],
        out_specs=[rows] * 4,
        cost_estimate=pl.CostEstimate(
            flops=0, bytes_accessed=24 * height * channels, transcendentals=0
        ),
        name="from_blocks",
    )(block, lags, medium_out)


def per_device(
    out_grad, out_weight, outer_gate, long_out, inner_gate, conv_input,
    short_out, medium_out, long_filter, taps_short, taps_medium,
):
    channels = outer_gate.shape[1]
    devices = lax.axis_size("seq")
    width = channels // devices
    here = Here()
    at = (((here.y_lo * 2 + here.core) * SIDE + here.x) * SIDE + here.z) * width
    own = [lax.dynamic_slice_in_dim(t, at, width, 1) for t in (taps_medium, taps_short)]
    own[1] = jnp.pad(own[1], ((0, MEDIUM - SHORT), (0, 0)))
    taps = jnp.stack([t.astype(F32).T for t in own])
    grad_outer, results, lags = block_call(
        out_grad, out_weight, outer_gate, long_out,
        (inner_gate, medium_out, short_out, conv_input, long_filter), taps, tables(devices),
    )
    lags = lags.reshape(devices, width + PAD, LANES)
    grad_inner, grad_input, grad_filter, grad_medium = from_blocks(results, lags, medium_out)
    short = lags[:, width : width + SHORT, :width].transpose(1, 0, 2)
    grad_short = short.reshape(SHORT, channels).astype(F32)
    return grad_outer, grad_inner, grad_input, grad_filter, grad_short, grad_medium


def solution(mesh):
    rows = P("seq", "ch")
    return jax.shard_map(
        per_device,
        mesh=mesh,
        in_specs=(rows, P(("seq", "ch"), None)) + (rows,) * 7 + (P(None, "ch"),) * 2,
        out_specs=(rows,) * 4 + (P(None, "ch"),) * 2,
        check_vma=False,
    )
```

time: 189 us -> 140 us (0.74)
  waiting for transfers between devices: 31.2 us -> 0 us
  starting transfers between devices: 17.7 us -> 0 us
    all_to_all x2 -> x0, waiting for transfers between devices: 31.2 us -> none  [the longest x1 31.2 us: per_device(): results = lax.all_to_all(results, 'seq', 0, 0, tiled=True)]
    all_to_all x2 -> x0, starting transfers between devices: 17.7 us -> none  [the longest x1 11.1 us: per_device(): early = lax.all_to_all(early, 'seq', 0, 0, tiled=True)]
    pallas_call x4 -> x1, Pallas kernels: 127 us -> 127 us  [block_call(): pl.pallas_call(block_kernel, out_shape=(jax.ShapeDtypeStruct((height, hal...]
  transfers between devices with their start and end apart: 2 -> 0, of which waited for: 1 -> 0; matrix products, arithmetic and copies ran while one was open for 1% -> 0% of each run, Pallas kernels for 39% -> 0%
where the time goes in v4:
time: 140 us; the launch traced here: 139 us
  Pallas kernels  134 us (96%)
  local copies, waits for them, and re-layouts  2.74 us (2%)
  other arithmetic  1.57 us (1%)
    pallas_call x1, Pallas kernels, block_call(): pl.pallas_call(block_kernel, out_shape=(jax.ShapeDtypeStruct((height, hal...  127 us
    pallas_call x1, Pallas kernels, from_blocks(): pl.pallas_call(unturn_kernel, grid=(devices // span,), out_shape=[jax.Sha...  6.48 us

profile of v4, /device:TPU:1, one launch (start us, length us, event | category | flops | bytes accessed | tf_op | source)
XLA Modules:
  0.0 138.9 jit_solution(9659980799489846180)
XLA Ops:
  0.6 0.0 copy-start
  0.7 0.8 constant_dynamic-slice_fusion
  1.5 0.1 copy.29
  1.6 0.1 copy-done
  1.7 0.1 constant_dynamic-slice_fusion.1
  1.8 0.1 copy.28
  1.8 0.6 maximum_convert_fusion.taps_ref
  2.5 127.4 %block.1 = (bf16[128,2048]{1,0:T(8,128)(2,1)}, bf16[64,2,3,16,128]{4,3,2,1,0:T(8,128)(2,1)}, bf16[2,2,4,4,48,128]{5,4,3,2,1,0:T(8,128)(2,1)}) custom-call(bf16[128,2048]{1,0:T(8,128)(2,1)} %grad_ref.1, bf16[32,4096]{1,0:T(8,128)(2,1)} %weight_ref.1, bf16[128,2048]{1,0:T(8,128)(2,1)} %gate_ref.1, bf16[128,2048]{1,0:T(8,128)(2,1)} %long_ref.1, ...), custom_call_target="tpu_custom_call" | custom-call | flops 16000000000 | bytes 33554432 | tf_op jit(solution)/shard_map/block/pallas_call | solution.py:640
  129.9 0.0 copy-start.1
  129.9 6.5 %from_blocks.1 = (bf16[128,2048]{1,0:T(8,128)(2,1)}, bf16[128,2048]{1,0:T(8,128)(2,1)}, f32[128,2048]{1,0:T(8,128)}, f32[128,2048]{1,0:T(8,128)}) custom-call(bf16[64,2,3,16,128]{4,3,2,1,0:T(8,128)(2,1)} %get-tuple-element.14.in_ref, bf16[64,48,128]{2,1,0:T(8,128)(2,1)} %bitcast.10, bf16[128,2048]{1,0:T(8,128)(2,1)} %medium_ref.3), custom_call_target="tpu_custom_call" | custom-call | bytes 6291456 | tf_op jit(solution)/shard_map/from_blocks/pallas_call | solution.py:706
  136.3 0.9 convert_bitcast_fusion
  137.3 0.8 reshape.19
  138.1 0.0 copy-done.1
  138.1 0.8 copy.31
  (2 shorter events, 0.1 us)
Async XLA Ops:
  0.6 1.1 copy-start
  129.9 8.2 %copy-start.1 = (bf16[128,2048]{1,0:T(8,128)(2,1)S(1)}, bf16[128,2048]{1,0:T(8,128)(2,1)}, u32[]{:S(2)}) copy-start(bf16[128,2048]{1,0:T(8,128)(2,1)} %get-tuple-element.26) | copy-start | bytes 1572868

commit v5 on v4

--- a/solution.py
+++ b/solution.py
@@ -17,6 +17,7 @@
 PAD = 16
 SIDE = 4
 PLANE = SIDE * SIDE
+ORDER = (0, 3, 1, 2)
 MESH = pl.DeviceIdType.MESH
 
 
@@ -49,6 +50,7 @@
         np.concatenate(split_np(inverse), 0),
         np.concatenate(split_np(last), 0),
         flip,
+        np.eye(2 * LANES).astype(jnp.bfloat16),
     )
 
 
@@ -181,12 +183,12 @@
 
 def block_kernel(
     grad_ref, weight_ref, gate_ref, long_ref,
-    inner_ref, medium_ref, short_ref, conv_ref, filter_ref, taps_ref,
-    first_ref, twists_ref, forward_ref, inverse_ref, last_ref, flip_ref,
+    inner_ref, medium_ref, short_ref, conv_ref, filter_ref, taps_short_ref, taps_medium_ref,
+    first_ref, twists_ref, forward_ref, inverse_ref, last_ref, flip_ref, eye_ref,
     outer_ref, back_ref, lags_ref,
     feats, weights, gates, total, turned, hidden, arrived,
-    one_out, one_in, two_out, two_in, late,
-    lines, zh, zl, gh, gl, spec, bands, saved, points, results, sums, parcels,
+    one_out, one_in, two_out, two_in, three_out, three_in, late,
+    lines, zh, zl, gh, gl, spec, bands, taps, points, pairs, results, sums, parcels,
     local, spread_s, spread_r, gate_s, gate_r, feat_s, feat_r, pass_s, pass_r,
     ring_s, ring_r, late_sem, hidden_s, hidden_r, batch_s, batch_r, lag_s, lag_r,
 ):
@@ -245,22 +247,33 @@
     for copy in copies:
         copy.start()
 
+    def feat(y, core):
+        return feats.at[y // 2, (y % 2) * 2 + core]
+
     def half_tokens(ref, i):
         return ref.at[pl.ds(i * (height // 2), height // 2)]
 
-    def feat(y, core):
-        return feats.at[y // 2, (y % 2) * 2 + core]
-
-    features = Ring(
-        here, "y", lambda y: feat(y, here.core), half_tokens, feat_s, feat_r, source=grad_ref
-    )
-    features.start()
-
-    def pass_on(i, y):
-        source = grad_ref if i == 0 else feat(y, here.core)
-        send(source, feat(y, here.core), pass_s.at[i], pass_r.at[i], partner)
-
-    pass_on(0, here.y)
+    near_y = here.y_hi * 2 + 1 - here.y_lo
+    far_y = wrap(here.y + 2 * here.y_lo - 1)
+    opposite_y = wrap(here.y + 2)
+
+    def feat_send(k, source, target, y):
+        send(source, target, feat_s.at[k], feat_r.at[k], here.at(y=y))
+
+    own_feat = feat(here.y, here.core)
+    for i in range(2):
+        feat_send(i, half_tokens(grad_ref, i), half_tokens(own_feat, i), near_y)
+    feat_send(2, grad_ref, own_feat, far_y)
+
+    def feat_relay(i):
+        half = half_tokens(feat(near_y, here.core), i)
+        await_bytes(half, feat_r.at[i])
+        feat_send(3 + i, half, half, far_y)
+
+    def pass_on(k, source, target):
+        send(source, target, pass_s.at[k], pass_r.at[k], partner)
+
+    pass_on(0, grad_ref, own_feat)
     share = [(0, 1), (1, 0), (1, 1)]
 
     def sharer(dy, dc):
@@ -281,15 +294,27 @@
 
     span = 8
 
-    def turn(value, out, k):
+    def turn(value, put):
         @pl.loop(0, rows // span)
         def _(b):
             part = pl.ds(pl.multiple_of(b * span * width, span * width), span * width)
-            lined = value(part).T.astype(BF16).reshape(span, width, height)
-            out[pl.ds(b * span, span), k] = lined
+            lined = dot_t(eye_ref[...], value(part)).astype(BF16)
+            put(pl.ds(b * span, span), lined.reshape(span, width, height))
+
+    def into(out, k):
+        def put(at, value):
+            out[at, k] = value
+
+        return put
+
+    def into_two(at, value):
+        two_out[at] = value
 
     def plain(ref):
-        return lambda part: ref[:, part].astype(F32)
+        return lambda part: ref[:, part]
+
+    def product(part):
+        return (inner_ref[:, part].astype(F32) * medium_ref[:, part].astype(F32)).astype(BF16)
 
     def half_block(ref, i):
         return ref.at[pl.ds(i * 2, 2)]
@@ -302,14 +327,15 @@
         block_ring(1, "z", lambda z: weights.at[1, here.x, z]),
     ]
     second = []
-    for j, d in enumerate((0, 3, 1, 2)):
+    for j, d in enumerate(ORDER):
         second.append((
             block_ring(2 + 2 * j, "z", lambda z, d=d: weights.at[0, wrap(here.x + d), z]),
             block_ring(3 + 2 * j, "x", lambda x, d=d: weights.at[1, x, wrap(here.z + d)]),
         ))
 
-    turn(lambda part: inner_ref[:, part].astype(F32) * medium_ref[:, part].astype(F32), one_out, 0)
-    turn(plain(filter_ref), one_out, 1)
+    turn(product, into(one_out, 0))
+    turn(plain(filter_ref), into(one_out, 1))
+    exchange(0, lambda seq, other: one_out.at[other], one_in.at[here.seq])
 
     for i, y, core in column_peers():
         source_y = wrap(2 * here.y - y + SIDE)
@@ -321,38 +347,23 @@
         ring.start()
     for ring in second[0]:
         ring.start()
-    exchange(0, lambda seq, other: one_out.at[other], one_in.at[here.seq])
-
-    turn(plain(inner_ref), two_out, 0)
+    turn(plain(inner_ref), into_two)
     for ring in first:
         ring.relay()
     for pair in second[1:3]:
         for ring in pair:
             ring.start()
-    turn(plain(short_ref), two_out, 1)
+    turn(plain(short_ref), into(three_out, 0))
     for ring in second[0]:
         ring.relay()
     for ring in first:
         ring.finish()
     for ring in second[3]:
         ring.start()
-    turn(plain(conv_ref), two_out, 2)
-    features.relay()
-    pass_on(1, wrap(here.y - 1))
-    pass_on(2, wrap(here.y + 1))
-
-    def make_bands(k):
-        @pl.loop(0, width)
-        def _(c):
-            wide = pl.ds(pl.multiple_of(c * LANES, LANES), LANES)
-            bands[k, wide, :] = toeplitz(taps_ref[k, pl.ds(c, 1), :]).astype(BF16)
-
-    make_bands(0)
-    for ring in second[1]:
-        ring.relay()
-    make_bands(1)
-    for ring in second[2]:
-        ring.relay()
+    feat_relay(0)
+    turn(plain(conv_ref), into(three_out, 1))
+    feat_relay(1)
+    pass_on(1, feat(near_y, here.core), feat(near_y, here.core))
 
     def unpack(source, planes):
         @pl.loop(0, rows)
@@ -370,61 +381,91 @@
 
     await_bytes(one_in, batch_r.at[0])
     unpack(one_in, ((0, 0), (1, 1)))
+    for ring in second[1]:
+        ring.relay()
+
+    def spread_pairs(part):
+        size = width // 4
+
+        @pl.loop(part * size // 2, (part + 1) * size // 2)
+        def _(b):
+            for j in range(2):
+                c = 2 * b + j
+                pick = pl.ds(c, rows, stride=width)
+                pair = jnp.concatenate([lines[0, pick, :], lines[1, pick, :]], 1).astype(BF16)
+                parts = outer_stage(pair, first_ref[...], twists_ref[...])
+                for there, high, low in keep(parts, (c * rows, area + c * rows)):
+                    zh[there, :] = high
+                    zl[there, :] = low
+
+    spread_pairs(0)
+    await_bytes(feat(far_y, here.core), feat_r.at[2])
+    pass_on(2, feat(far_y, here.core), feat(far_y, here.core))
+    for ring in second[2]:
+        ring.relay()
+    spread_pairs(1)
     for ring in second[3]:
         ring.relay()
-
-    def spread_pairs(begin, end):
+    spread_pairs(2)
+    for i in range(2):
+        half = half_tokens(feat(opposite_y, here.core), i)
+        await_bytes(half, feat_r.at[3 + i])
+        pass_on(3 + i, half, half)
+    spread_pairs(3)
+    step = 512
+
+    def transform_pairs(begin, end):
         @pl.loop(begin, end)
-        def _(c):
-            pick = pl.ds(c, rows, stride=width)
-            pair = jnp.concatenate([lines[0, pick, :], lines[1, pick, :]], 1).astype(BF16)
-            parts = outer_stage(pair, first_ref[...], twists_ref[...])
-            for there, high, low in keep(parts, (c * rows, area + c * rows)):
-                zh[there, :] = high
-                zl[there, :] = low
-
-    spread_pairs(0, width // 2)
-    features.finish()
-    pass_on(3, wrap(here.y + 2))
-    spread_pairs(width // 2, width)
-    step = 512
-
-    @pl.loop(0, 2 * area // step)
-    def _(b):
-        at = pl.ds(pl.multiple_of(b * step, step), step)
-        spec[at, :] = dot3(zh[at, :], zl[at, :], forward_ref[...])
-
-    for pair in second:
-        for ring in pair:
+        def _(b):
+            at = pl.ds(pl.multiple_of(b * step, step), step)
+            spec[at, :] = dot3(zh[at, :], zl[at, :], forward_ref[...])
+
+    halves = area // step
+    transform_pairs(0, halves)
+
+    other_core = 1 - here.core
+    copies[1].wait()
+    for k, y in ((0, here.y), (1, near_y), (2, far_y)):
+        await_bytes(feat(y, other_core), pass_r.at[k])
+    for i in range(2):
+        await_bytes(half_tokens(feat(opposite_y, other_core), i), pass_r.at[3 + i])
+    exchange(1, lambda seq, other: two_out.at[other], two_in.at[here.seq])
+    rows_of = weights.shape[3] * weights.shape[4]
+    depth = SIDE * rows_of
+    for j, d in enumerate(ORDER):
+        for ring in second[j]:
             ring.finish()
-    for i, d in enumerate((0, -1, 1, 2)):
-        await_bytes(feat(wrap(here.y + d), 1 - here.core), pass_r.at[i])
-    copies[1].wait()
-    depth = SIDE * weights.shape[3] * weights.shape[4]
-    for h in range(2):
-        @pl.loop(0, SIDE)
-        def _(x):
-            part = pl.ds(pl.multiple_of(x * depth, depth), depth)
-            left = feats[h, :, :, part].reshape(4 * height, depth)
-            term = dot(left, weights[h, x].reshape(depth, columns))
-            if h == 0:
-                @pl.when(x == 0)
-                def _():
-                    total[...] = term
-
-                @pl.when(x > 0)
-                def _():
-                    total[...] += term
-            else:
-                total[...] += term
+        x, z = wrap(here.x + d), wrap(here.z + d)
+        left = feats[0, :, :, pl.ds(pl.multiple_of(x * depth, depth), depth)]
+        term = dot(left.reshape(4 * height, depth), weights[0, x].reshape(depth, columns))
+        if j == 0:
+            total[...] = term
+        else:
+            total[...] += term
+        left = jnp.concatenate(
+            [
+                feats[1, :, :, pl.ds(pl.multiple_of(k * depth + z * rows_of, rows_of), rows_of)]
+                for k in range(SIDE)
+            ],
+            2,
+        )
+        total[...] += dot(
+            left.reshape(4 * height, depth), weights[1, :, z].reshape(depth, columns)
+        )
 
     copies[2].wait()
     for i, (dy, dc) in enumerate(share):
         await_bytes(gates.at[sharer(dy, dc)[0]], gate_r.at[i])
+    block_size = eye_ref.shape[0]
+    cells = block_size // width
     for g in range(4):
         part = total[g * height : (g + 1) * height]
-        long_grad = (part * gates[g].astype(F32)).astype(BF16).astype(F32)
-        turned[:, g // 2, g % 2] = long_grad.T.astype(BF16).reshape(PLANE, width, height)
+        long_grad = (part * gates[g].astype(F32)).astype(BF16)
+        for k in range(columns // block_size):
+            lined = dot_t(eye_ref[...], long_grad[:, k * block_size : (k + 1) * block_size])
+            turned[k * cells : (k + 1) * cells, g // 2, g % 2] = lined.astype(BF16).reshape(
+                cells, width, height
+            )
         hidden[g] = part.astype(BF16)
     pltpu.make_async_copy(turned.at[cell], late.at[:, cell], late_sem.at[1]).start()
     for x, z in plane_peers():
@@ -432,13 +473,32 @@
             turned.at[x * SIDE + z], late.at[:, cell], late_sem.at[0], late_sem.at[1],
             here.at(x=x, z=z),
         )
-    exchange(1, lambda seq, other: two_out.at[other], two_in.at[here.seq])
+    exchange(2, lambda seq, other: three_out.at[other], three_in.at[here.seq])
     for i, (dy, dc) in enumerate(share):
         index, device = sharer(dy, dc)
         send(hidden.at[index], arrived.at[me], hidden_s.at[i], hidden_r.at[i], device)
     own = pltpu.make_async_copy(hidden.at[me], arrived.at[me], local.at[1])
     own.start()
 
+    place = pl.multiple_of((me * PLANE + here.x * SIDE) * width, LANES)
+    chosen = lax.broadcasted_iota(jnp.int32, (width, LANES), 1)
+    chosen = chosen == lax.broadcasted_iota(jnp.int32, (width, LANES), 0) + here.z * width
+    chosen = chosen.astype(F32).astype(BF16)
+    taps[0] = dot_t(chosen, taps_medium_ref[:, pl.ds(place, LANES)])
+    sums[0, : width // 4, :LANES] = jnp.zeros((width // 4, LANES), F32)
+    sums[0, :SHORT, :LANES] = taps_short_ref[:, pl.ds(place, LANES)].astype(F32)
+    padded = jnp.concatenate(
+        [sums[0, : width // 4, :LANES], jnp.zeros((LANES - width // 4, LANES), F32)], 0
+    )
+    taps[1] = dot_t(chosen, padded.astype(BF16))
+
+    @pl.loop(0, width)
+    def _(c):
+        wide = pl.ds(pl.multiple_of(c * LANES, LANES), LANES)
+        for k in range(2):
+            bands[k, wide, :] = toeplitz(taps[k, pl.ds(c, 1), :]).astype(BF16)
+
+    transform_pairs(halves, 2 * halves)
     await_bytes(late, late_sem.at[1])
     for y_lo in range(2):
         @pl.loop(0, PLANE)
@@ -521,33 +581,54 @@
     for k in range(2):
         transform(k * chunk)
         pack(k, (0, 1), (0, 1))
-        exchange(2 + k, lambda seq, other: pair_of(parcels.at[seq], k), pair_of(back_ref.at[block], k))
-
-    own.wait()
-    for i, (dy, dc) in enumerate(share):
-        await_bytes(arrived.at[sharer(dy, dc)[0]], hidden_r.at[i])
-    for g in range(4):
-        part = slice(g * columns, (g + 1) * columns)
-        outer_ref[:, part] = (arrived[g].astype(F32) * long_ref[:, part].astype(F32)).astype(BF16)
+        exchange(3 + k, lambda seq, other: pair_of(parcels.at[seq], k), pair_of(back_ref.at[block], k))
 
     await_bytes(two_in, batch_r.at[1])
-    unpack(two_in, ((0, 0), (1, 1), (2, 2)))
-
-    @pl.loop(0, width)
-    def _(c):
-        wide = pl.ds(pl.multiple_of(c * LANES, LANES), LANES)
+    await_bytes(three_in, batch_r.at[2])
+
+    @pl.loop(0, rows)
+    def _(i):
+        at = pl.ds(pl.multiple_of(i * width, width), width)
+        lines[0, at, :] = two_in[i].astype(F32)
         for k in range(2):
-            value = lines[1 + k, pl.ds(c, rows, stride=width), :].astype(BF16)
-            saved[k, wide, :] = dot_t(flip_ref[...], value).astype(BF16)
+            lines[1 + k, at, :] = three_in[i, k].astype(F32)
 
     def with_next(x):
         following = jnp.where(row == rows - 1, 0.0, pltpu.roll(x, rows - 1, 0))
         return jnp.concatenate([x, following], 1).astype(BF16)
 
-    def diagonals(wide, k, both):
-        products = dot(saved[k, wide, :], both)
+    def diagonals(c, k, both):
+        value = lines[1 + k, pl.ds(c, rows, stride=width), :].astype(BF16)
+        products = dot(dot_t(flip_ref[...], value).astype(BF16), both)
         slid = pltpu.roll(products, 0, 1, stride=1, stride_axis=0)
-        return jnp.sum(slid, axis=0, keepdims=True)
+        sums[k, pl.ds(c, 1), :] = jnp.sum(slid, axis=0, keepdims=True)
+
+    @pl.loop(0, width // many)
+    def _(b):
+        for k in range(many):
+            c = b * many + k
+            wide = pl.ds(pl.multiple_of(c * LANES, LANES), LANES)
+            there = pl.ds(pl.multiple_of(c * rows, rows), rows)
+            gate = lines[0, pl.ds(c, rows, stride=width), :]
+            both = with_next((points[there, :] * gate).astype(BF16).astype(F32))
+            short_grad = dot_t(both, bands[0, wide, :]).astype(BF16).astype(F32)
+            pair = with_next(short_grad)
+            pairs[there, :] = pair
+            diagonals(c, 0, both)
+            diagonals(c, 1, pair)
+
+    factor = (rows * LANES) ** -0.5
+    lags = [pltpu.roll(sums[k], LANES + 1, 1)[:, :LANES] * factor for k in range(2)]
+    square = jnp.concatenate([lags[1], jnp.zeros((LANES - width, LANES), F32)], 0)
+    mine = lags_ref.at[here.y_lo, here.core]
+    lags_ref[here.y_lo, here.core, here.x, here.z, :width] = lags[0].astype(BF16)
+    lags_ref[here.y_lo, here.core, here.x, here.z, width:] = square.T[:PAD].astype(BF16)
+
+    def lag_send(i, ref, device):
+        send(ref, ref, lag_s.at[i], lag_r.at[i], device)
+
+    for d in range(1, SIDE):
+        lag_send(d - 1, mine.at[here.x, here.z], here.at(x=wrap(here.x + d)))
 
     def convolve(start):
         @pl.loop(0, chunk // many)
@@ -556,56 +637,47 @@
                 within = b * many + k
                 c = start + within
                 wide = pl.ds(pl.multiple_of(c * LANES, LANES), LANES)
-                point = points[pl.ds(pl.multiple_of(c * rows, rows), rows), :]
-                gate = lines[0, pl.ds(c, rows, stride=width), :]
-                both = with_next((point * gate).astype(BF16).astype(F32))
-                short_grad = dot_t(both, bands[0, wide, :]).astype(BF16).astype(F32)
-                pair = with_next(short_grad)
-                pick = pl.ds(within, rows, stride=chunk)
-                results[0, pick, :] = dot_t(pair, bands[1, wide, :])
-                sums[0, pl.ds(c, 1), :] = diagonals(wide, 0, both)
-                sums[1, pl.ds(c, 1), :] = diagonals(wide, 1, pair)
+                there = pl.ds(pl.multiple_of(c * rows, rows), rows)
+                results[0, pl.ds(within, rows, stride=chunk), :] = dot_t(
+                    pairs[there, :], bands[1, wide, :]
+                )
 
     for k in range(2):
         convolve(k * chunk)
         pack(k, (0,), (2,))
-        exchange(4 + k, lambda seq, other: parcels.at[seq, k, 2], back_ref.at[block, k, 2])
-
-    factor = (rows * LANES) ** -0.5
-    lags = [pltpu.roll(sums[k], LANES + 1, 1)[:, :LANES] * factor for k in range(2)]
-    square = jnp.concatenate([lags[1], jnp.zeros((LANES - width, LANES), F32)], 0)
-    mine = lags_ref.at[here.y_lo, here.core]
-    lags_ref[here.y_lo, here.core, here.x, here.z, :width] = lags[0].astype(BF16)
-    lags_ref[here.y_lo, here.core, here.x, here.z, width:] = square.T[:PAD].astype(BF16)
-
-    def lag_send(i, ref, device):
-        send(ref, ref, lag_s.at[i], lag_r.at[i], device)
-
-    for d in range(1, SIDE):
-        lag_send(d - 1, mine.at[here.x, here.z], here.at(x=wrap(here.x + d)))
-    for d in range(1, SIDE):
-        await_bytes(mine.at[wrap(here.x - d), here.z], lag_r.at[d - 1])
-    for d in range(1, SIDE):
-        lag_send(2 + d, mine.at[:, here.z], here.at(z=wrap(here.z + d)))
+        if k == 0:
+            for d in range(1, SIDE):
+                await_bytes(mine.at[wrap(here.x - d), here.z], lag_r.at[d - 1])
+            for d in range(1, SIDE):
+                lag_send(2 + d, mine.at[:, here.z], here.at(z=wrap(here.z + d)))
+        exchange(5 + k, lambda seq, other: parcels.at[seq, k, 2], back_ref.at[block, k, 2])
+
     for d in range(1, SIDE):
         await_bytes(mine.at[:, wrap(here.z - d)], lag_r.at[2 + d])
-    across = here.at(y=here.y_hi * 2 + 1 - here.y_lo)
-    lag_send(6, mine, across)
+    lag_send(6, mine, here.at(y=near_y))
     lag_send(7, mine, partner)
+
+    own.wait()
+    for i, (dy, dc) in enumerate(share):
+        await_bytes(arrived.at[sharer(dy, dc)[0]], hidden_r.at[i])
+    for g in range(4):
+        part = slice(g * columns, (g + 1) * columns)
+        outer_ref[:, part] = (arrived[g].astype(F32) * long_ref[:, part].astype(F32)).astype(BF16)
+
     await_bytes(lags_ref.at[1 - here.y_lo, here.core], lag_r.at[6])
     lag_send(8, lags_ref.at[1 - here.y_lo, here.core], partner)
     await_bytes(lags_ref.at[here.y_lo, 1 - here.core], lag_r.at[7])
     await_bytes(lags_ref.at[1 - here.y_lo, 1 - here.core], lag_r.at[8])
 
     for k in range(2):
-        await_bytes(back_ref.at[:, k, pl.ds(0, 2)], batch_r.at[2 + k])
-        await_bytes(back_ref.at[:, k, 2], batch_r.at[4 + k])
+        await_bytes(back_ref.at[:, k, pl.ds(0, 2)], batch_r.at[3 + k])
+        await_bytes(back_ref.at[:, k, 2], batch_r.at[5 + k])
     most = pl.ds(0, rows - 1)
-    await_bytes(one_out.at[most], batch_s.at[0])
-    await_bytes(two_out.at[most], batch_s.at[1])
+    for k, ref in enumerate((one_out, two_out, three_out)):
+        await_bytes(ref.at[most], batch_s.at[k])
     for k in range(2):
-        await_bytes(parcels.at[most, k, pl.ds(0, 2)], batch_s.at[2 + k])
-        await_bytes(parcels.at[most, k, 2], batch_s.at[4 + k])
+        await_bytes(parcels.at[most, k, pl.ds(0, 2)], batch_s.at[3 + k])
+        await_bytes(parcels.at[most, k, 2], batch_s.at[5 + k])
     await_bytes(turned.at[pl.ds(0, PLANE - 1)], late_sem.at[0])
     for i in range(7):
         await_bytes(own_rows, spread_s.at[i])
@@ -615,9 +687,14 @@
         await_bytes(mine.at[here.x, here.z], lag_s.at[i])
         await_bytes(mine.at[:, here.z], lag_s.at[3 + i])
         await_bytes(mine, lag_s.at[6 + i])
-    for i in range(4):
-        await_bytes(feats.at[0, 0], pass_s.at[i])
-    features.drain()
+    for i in range(3):
+        await_bytes(own_feat, pass_s.at[i])
+    await_bytes(own_feat, feat_s.at[2])
+    for i in range(2):
+        half = half_tokens(own_feat, i)
+        await_bytes(half, pass_s.at[3 + i])
+        await_bytes(half, feat_s.at[i])
+        await_bytes(half, feat_s.at[3 + i])
     for ring in first:
         ring.drain()
     for pair in second:
@@ -625,7 +702,7 @@
             ring.drain()
 
 
-def block_call(grad, weight, gate, long, channelwise, taps, constants):
+def block_call(grad, weight, gate, long, channelwise, constants):
     height, half = grad.shape
     depth, model = weight.shape
     columns = model // 8
@@ -644,7 +721,7 @@
             jax.ShapeDtypeStruct((rows, 2, 3, chunk, height), BF16),
             jax.ShapeDtypeStruct((2, 2, SIDE, SIDE, width + PAD, height), BF16),
         ),
-        in_specs=[anywhere] * 3 + [near] * (7 + len(constants)),
+        in_specs=[anywhere] * 3 + [near] * (1 + len(channelwise) + len(constants)),
         out_specs=(near, anywhere, near),
         scratch_shapes=[
             vmem((2, 4, height, half), BF16),
@@ -656,8 +733,10 @@
             vmem((4, height, columns), BF16),
             vmem((rows, 2, width, height), BF16),
             vmem((rows, 2, width, height), BF16),
-            vmem((rows, 3, width, height), BF16),
-            vmem((rows, 3, width, height), BF16),
+            vmem((rows, width, height), BF16),
+            vmem((rows, width, height), BF16),
+            vmem((rows, 2, width, height), BF16),
+            vmem((rows, 2, width, height), BF16),
             vmem((2, PLANE, 2, width, height), BF16),
             vmem((3, area, height), F32),
             vmem((2 * area, 2 * height), BF16),
@@ -666,14 +745,15 @@
             vmem((area // 2, 2 * height), BF16),
             vmem((2 * area, 2 * height), F32),
             vmem((2, width * LANES, 2 * LANES), BF16),
-            vmem((2, width * LANES, rows), BF16),
+            vmem((2, width, LANES), F32),
             vmem((area, height), F32),
+            vmem((area, 2 * height), BF16),
             vmem((2, area // 2, height), F32),
             vmem((2, width, 2 * LANES), F32),
             vmem((rows, 2, 3, chunk, height), BF16),
-            dma((3,)), dma((7,)), dma((7,)), dma((3,)), dma((3,)), dma((4,)), dma((4,)),
-            dma((4,)), dma((4,)), dma((10, 4)), dma((10, 4)), dma((2,)), dma((3,)), dma((3,)),
-            dma((6,)), dma((6,)), dma((9,)), dma((9,)),
+            dma((3,)), dma((7,)), dma((7,)), dma((3,)), dma((3,)), dma((5,)), dma((5,)),
+            dma((5,)), dma((5,)), dma((10, 4)), dma((10, 4)), dma((2,)), dma((3,)), dma((3,)),
+            dma((7,)), dma((7,)), dma((9,)), dma((9,)),
         ],
         compiler_params=pltpu.CompilerParams(
             collective_id=0, has_side_effects=True, vmem_limit_bytes=VMEM_LIMIT
@@ -682,19 +762,31 @@
             flops=16 * 10**9, bytes_accessed=32 * 2**20, transcendentals=0
         ),
         name="block",
-    )(grad, weight, gate, long, *channelwise, taps, *constants)
-
-
-def unturn_kernel(in_ref, lags_ref, medium_ref, inner_out, input_out, filter_out, lags_out):
+    )(grad, weight, gate, long, *channelwise, *constants)
+
+
+def unturn_kernel(
+    in_ref, lags_ref, medium_ref, eye_ref,
+    inner_out, input_out, filter_out, lags_out, short_out,
+):
     size, height = inner_out.shape[1], in_ref.shape[4]
+    blocks = in_ref.shape[0]
+    width = size // blocks
 
     def lined(value):
-        return value.astype(F32).reshape(size, height).T
+        return dot_t(eye_ref[...], value.reshape(size, height))
 
     inner_out[...] = (lined(in_ref[:, :, 0]) * medium_ref[...].astype(F32)).astype(BF16)
     filter_out[...] = lined(in_ref[:, :, 1])
     input_out[...] = lined(in_ref[:, :, 2]).astype(BF16)
-    lags_out[...] = lined(lags_ref[:, : size // in_ref.shape[0]])
+    lags_out[...] = lined(lags_ref[:, :width])
+    lane = lax.broadcasted_iota(jnp.int32, (height, size), 0)
+    column = lax.broadcasted_iota(jnp.int32, (height, size), 1)
+    short = jnp.zeros((PAD, size), F32)
+    for b in range(blocks):
+        place = (column == lane + b * width) & (lane < width)
+        short += dot(lags_ref[b, width:], place.astype(F32).astype(BF16))
+    short_out[...] = short[:SHORT]
 
 
 def from_blocks(block, lags, medium_out):
@@ -703,23 +795,25 @@
     size = span * parts * chunk
     channels = devices * parts * chunk
     rows = pl.BlockSpec((height, size), lambda i: (0, i))
+    eye = np.eye(height).astype(jnp.bfloat16)
     return pl.pallas_call(
         unturn_kernel,
         grid=(devices // span,),
         out_shape=[
             jax.ShapeDtypeStruct((height, channels), t) for t in (BF16, BF16, F32, F32)
-        ],
+        ] + [jax.ShapeDtypeStruct((SHORT, channels), F32)],
         in_specs=[
             pl.BlockSpec((span, parts, items, chunk, height), lambda i: (i, 0, 0, 0, 0)),
             pl.BlockSpec((span, lags.shape[1], height), lambda i: (i, 0, 0)),
             rows,
+            pl.BlockSpec((height, height), lambda i: (0, 0)),
         ],
-        out_specs=[rows] * 4,
+        out_specs=[rows] * 4 + [pl.BlockSpec((SHORT, size), lambda i: (0, i))],
         cost_estimate=pl.CostEstimate(
             flops=0, bytes_accessed=24 * height * channels, transcendentals=0
         ),
         name="from_blocks",
-    )(block, lags, medium_out)
+    )(block, lags, medium_out, eye)
 
 
 def per_device(
@@ -729,19 +823,15 @@
     channels = outer_gate.shape[1]
     devices = lax.axis_size("seq")
     width = channels // devices
-    here = Here()
-    at = (((here.y_lo * 2 + here.core) * SIDE + here.x) * SIDE + here.z) * width
-    own = [lax.dynamic_slice_in_dim(t, at, width, 1) for t in (taps_medium, taps_short)]
-    own[1] = jnp.pad(own[1], ((0, MEDIUM - SHORT), (0, 0)))
-    taps = jnp.stack([t.astype(F32).T for t in own])
     grad_outer, results, lags = block_call(
         out_grad, out_weight, outer_gate, long_out,
-        (inner_gate, medium_out, short_out, conv_input, long_filter), taps, tables(devices),
+        (inner_gate, medium_out, short_out, conv_input, long_filter, taps_short, taps_medium),
+        tables(devices),
     )
     lags = lags.reshape(devices, width + PAD, LANES)
-    grad_inner, grad_input, grad_filter, grad_medium = from_blocks(results, lags, medium_out)
-    short = lags[:, width : width + SHORT, :width].transpose(1, 0, 2)
-    grad_short = short.reshape(SHORT, channels).astype(F32)
+    grad_inner, grad_input, grad_filter, grad_medium, grad_short = from_blocks(
+        results, lags, medium_out
+    )
     return grad_outer, grad_inner, grad_input, grad_filter, grad_short, grad_medium
 
 

time: 140 us -> 122 us (0.87)
  Pallas kernels: 134 us -> 120 us
  local copies, waits for them, and re-layouts: 2.74 us -> 0.8 us
  other arithmetic: 1.57 us -> 0 us
    pallas_call x1, Pallas kernels: 127 us -> 113 us  [block_call(): pl.pallas_call(block_kernel, out_shape=(jax.ShapeDtypeStruct((height, hal...]
where the time goes in v5:
time: 122 us; the launch traced here: 121 us
  Pallas kernels  120 us (98%)
    pallas_call x1, Pallas kernels, block_call(): pl.pallas_call(block_kernel, out_shape=(jax.ShapeDtypeStruct((height, hal...  113 us
    pallas_call x1, Pallas kernels, from_blocks(): pl.pallas_call(unturn_kernel, grid=(devices // span,), out_shape=[jax.Sha...  6.86 us

profile of v5, /device:TPU:1, one launch (start us, length us, event | category | flops | bytes accessed | tf_op | source)
XLA Modules:
  0.0 121.2 jit_solution(18307618260809110149)
XLA Ops:
  0.6 112.9 %block.1 = (bf16[128,2048]{1,0:T(8,128)(2,1)}, bf16[64,2,3,16,128]{4,3,2,1,0:T(8,128)(2,1)}, bf16[2,2,4,4,48,128]{5,4,3,2,1,0:T(8,128)(2,1)}) custom-call(bf16[128,2048]{1,0:T(8,128)(2,1)} %grad_ref.1, bf16[32,4096]{1,0:T(8,128)(2,1)} %weight_ref.1, bf16[128,2048]{1,0:T(8,128)(2,1)} %gate_ref.1, bf16[128,2048]{1,0:T(8,128)(2,1)} %long_ref.1, ...), custom_call_target="tpu_custom_call" | custom-call | flops 16000000000 | bytes 33554432 | tf_op jit(solution)/shard_map/block/pallas_call | solution.py:717
  113.6 0.0 copy-start
  113.6 6.9 %from_blocks.1 = (bf16[128,2048]{1,0:T(8,128)(2,1)}, bf16[128,2048]{1,0:T(8,128)(2,1)}, f32[128,2048]{1,0:T(8,128)}, f32[128,2048]{1,0:T(8,128)}, f32[7,2048]{1,0:T(8,128)}) custom-call(bf16[64,2,3,16,128]{4,3,2,1,0:T(8,128)(2,1)} %get-tuple-element.15.in_ref, bf16[64,48,128]{2,1,0:T(8,128)(2,1)} %bitcast.1, bf16[128,2048]{1,0:T(8,128)(2,1)} %medium_ref.3, ...), custom_call_target="tpu_custom_call" | custom-call | bytes 6291456 | tf_op jit(solution)/shard_map/from_blocks/pallas_call | solution.py:799
  120.4 0.0 copy-done
  120.4 0.8 copy.26
Async XLA Ops:
  113.6 6.9 %copy-start = (bf16[128,2048]{1,0:T(8,128)(2,1)S(1)}, bf16[128,2048]{1,0:T(8,128)(2,1)}, u32[]{:S(2)}) copy-start(bf16[128,2048]{1,0:T(8,128)(2,1)} %get-tuple-element.28) | copy-start | bytes 1572868

commit v6 on v5

--- a/solution.py
+++ b/solution.py
@@ -182,11 +182,11 @@
 
 
 def block_kernel(
-    grad_ref, weight_ref, gate_ref, long_ref,
+    grad_ref, weight_ref, gate_ref,
     inner_ref, medium_ref, short_ref, conv_ref, filter_ref, taps_short_ref, taps_medium_ref,
     first_ref, twists_ref, forward_ref, inverse_ref, last_ref, flip_ref, eye_ref,
-    outer_ref, back_ref, lags_ref,
-    feats, weights, gates, total, turned, hidden, arrived,
+    arrived, back_ref, lags_ref,
+    feats, weights, gates, total, turned, hidden,
     one_out, one_in, two_out, two_in, three_out, three_in, late,
     lines, zh, zl, gh, gl, spec, bands, taps, points, pairs, results, sums, parcels,
     local, spread_s, spread_r, gate_s, gate_r, feat_s, feat_r, pass_s, pass_r,
@@ -294,12 +294,15 @@
 
     span = 8
 
-    def turn(value, put):
-        @pl.loop(0, rows // span)
-        def _(b):
-            part = pl.ds(pl.multiple_of(b * span * width, span * width), span * width)
-            lined = dot_t(eye_ref[...], value(part)).astype(BF16)
-            put(pl.ds(b * span, span), lined.reshape(span, width, height))
+    def turn(*jobs):
+        @pl.loop(0, rows // (2 * span))
+        def _(pair):
+            for j in range(2):
+                b = 2 * pair + j
+                part = pl.ds(pl.multiple_of(b * span * width, span * width), span * width)
+                for value, put in jobs:
+                    lined = dot_t(eye_ref[...], value(part)).astype(BF16)
+                    put(pl.ds(b * span, span), lined.reshape(span, width, height))
 
     def into(out, k):
         def put(at, value):
@@ -333,8 +336,7 @@
             block_ring(3 + 2 * j, "x", lambda x, d=d: weights.at[1, x, wrap(here.z + d)]),
         ))
 
-    turn(product, into(one_out, 0))
-    turn(plain(filter_ref), into(one_out, 1))
+    turn((product, into(one_out, 0)), (plain(filter_ref), into(one_out, 1)))
     exchange(0, lambda seq, other: one_out.at[other], one_in.at[here.seq])
 
     for i, y, core in column_peers():
@@ -347,13 +349,13 @@
         ring.start()
     for ring in second[0]:
         ring.start()
-    turn(plain(inner_ref), into_two)
+    turn((plain(inner_ref), into_two))
     for ring in first:
         ring.relay()
     for pair in second[1:3]:
         for ring in pair:
             ring.start()
-    turn(plain(short_ref), into(three_out, 0))
+    turn((plain(short_ref), into(three_out, 0)))
     for ring in second[0]:
         ring.relay()
     for ring in first:
@@ -361,17 +363,18 @@
     for ring in second[3]:
         ring.start()
     feat_relay(0)
-    turn(plain(conv_ref), into(three_out, 1))
+    turn((plain(conv_ref), into(three_out, 1)))
     feat_relay(1)
     pass_on(1, feat(near_y, here.core), feat(near_y, here.core))
 
     def unpack(source, planes):
-        @pl.loop(0, rows)
-        def _(i):
-            at = pl.ds(pl.multiple_of(i * width, width), width)
-            for k, plane in planes:
-                value = source[i] if k is None else source[i, k]
-                lines[plane, at, :] = value.astype(F32)
+        @pl.loop(0, rows // 4)
+        def _(b):
+            for j in range(4):
+                i = 4 * b + j
+                at = pl.ds(pl.multiple_of(i * width, width), width)
+                for k, plane in planes:
+                    lines[plane, at, :] = source[i, k].astype(F32)
 
     def keep(parts, places):
         for part, place in zip(parts, places):
@@ -501,27 +504,31 @@
     transform_pairs(halves, 2 * halves)
     await_bytes(late, late_sem.at[1])
     for y_lo in range(2):
-        @pl.loop(0, PLANE)
-        def _(i):
-            for core in range(2):
-                place = ((y_lo * PLANE + i) * 2 + core) * width
-                at = pl.ds(pl.multiple_of(place, width), width)
-                lines[2, at, :] = late[y_lo, i, core].astype(F32)
+        @pl.loop(0, PLANE // 2)
+        def _(b):
+            for j in range(2):
+                for core in range(2):
+                    i = 2 * b + j
+                    place = ((y_lo * PLANE + i) * 2 + core) * width
+                    at = pl.ds(pl.multiple_of(place, width), width)
+                    lines[2, at, :] = late[y_lo, i, core].astype(F32)
 
     many = 4
     wide_step = many * rows
     row = lax.broadcasted_iota(jnp.int32, (rows, LANES), 0)
 
     def transform(start):
-        @pl.loop(0, chunk // 2)
-        def _(c):
-            pair = jnp.concatenate(
-                [lines[2, pl.ds(start + 2 * c + k, rows, stride=width), :] for k in range(2)], 1
-            ).astype(BF16)
-            parts = outer_stage(pair, first_ref[...], twists_ref[...])
-            for there, high, low in keep(parts, (2 * c * rows, (2 * c + 1) * rows)):
-                gh[there, :] = high
-                gl[there, :] = low
+        @pl.loop(0, chunk // 8)
+        def _(b):
+            for j in range(4):
+                c = 4 * b + j
+                pair = jnp.concatenate(
+                    [lines[2, pl.ds(start + 2 * c + k, rows, stride=width), :] for k in range(2)], 1
+                ).astype(BF16)
+                parts = outer_stage(pair, first_ref[...], twists_ref[...])
+                for there, high, low in keep(parts, (2 * c * rows, (2 * c + 1) * rows)):
+                    gh[there, :] = high
+                    gl[there, :] = low
 
         @pl.loop(0, chunk // many)
         def _(b):
@@ -569,11 +576,13 @@
                 results[1, pick, :] = both[:, LANES:]
 
     def pack(k, source, to):
-        @pl.loop(0, rows)
-        def _(i):
-            at = pl.ds(pl.multiple_of(i * chunk, chunk), chunk)
-            for a, b in zip(source, to):
-                parcels[i, k, b] = results[a, at, :].astype(BF16)
+        @pl.loop(0, rows // 8)
+        def _(group):
+            for j in range(8):
+                i = 8 * group + j
+                at = pl.ds(pl.multiple_of(i * chunk, chunk), chunk)
+                for a, b in zip(source, to):
+                    parcels[i, k, b] = results[a, at, :].astype(BF16)
 
     def pair_of(ref, k):
         return ref.at[k, pl.ds(0, 2)]
@@ -586,12 +595,14 @@
     await_bytes(two_in, batch_r.at[1])
     await_bytes(three_in, batch_r.at[2])
 
-    @pl.loop(0, rows)
-    def _(i):
-        at = pl.ds(pl.multiple_of(i * width, width), width)
-        lines[0, at, :] = two_in[i].astype(F32)
-        for k in range(2):
-            lines[1 + k, at, :] = three_in[i, k].astype(F32)
+    @pl.loop(0, rows // 4)
+    def _(b):
+        for j in range(4):
+            i = 4 * b + j
+            at = pl.ds(pl.multiple_of(i * width, width), width)
+            lines[0, at, :] = two_in[i].astype(F32)
+            for k in range(2):
+                lines[1 + k, at, :] = three_in[i, k].astype(F32)
 
     def with_next(x):
         following = jnp.where(row == rows - 1, 0.0, pltpu.roll(x, rows - 1, 0))
@@ -650,20 +661,16 @@
                 await_bytes(mine.at[wrap(here.x - d), here.z], lag_r.at[d - 1])
             for d in range(1, SIDE):
                 lag_send(2 + d, mine.at[:, here.z], here.at(z=wrap(here.z + d)))
+        else:
+            for d in range(1, SIDE):
+                await_bytes(mine.at[:, wrap(here.z - d)], lag_r.at[2 + d])
+            lag_send(6, mine, here.at(y=near_y))
+            lag_send(7, mine, partner)
         exchange(5 + k, lambda seq, other: parcels.at[seq, k, 2], back_ref.at[block, k, 2])
-
-    for d in range(1, SIDE):
-        await_bytes(mine.at[:, wrap(here.z - d)], lag_r.at[2 + d])
-    lag_send(6, mine, here.at(y=near_y))
-    lag_send(7, mine, partner)
 
     own.wait()
     for i, (dy, dc) in enumerate(share):
         await_bytes(arrived.at[sharer(dy, dc)[0]], hidden_r.at[i])
-    for g in range(4):
-        part = slice(g * columns, (g + 1) * columns)
-        outer_ref[:, part] = (arrived[g].astype(F32) * long_ref[:, part].astype(F32)).astype(BF16)
-
     await_bytes(lags_ref.at[1 - here.y_lo, here.core], lag_r.at[6])
     lag_send(8, lags_ref.at[1 - here.y_lo, here.core], partner)
     await_bytes(lags_ref.at[here.y_lo, 1 - here.core], lag_r.at[7])
@@ -702,7 +709,7 @@
             ring.drain()
 
 
-def block_call(grad, weight, gate, long, channelwise, constants):
+def block_call(grad, weight, gate, channelwise, constants):
     height, half = grad.shape
     depth, model = weight.shape
     columns = model // 8
@@ -717,19 +724,18 @@
     return pl.pallas_call(
         block_kernel,
         out_shape=(
-            jax.ShapeDtypeStruct((height, half), BF16),
+            jax.ShapeDtypeStruct((4, height, columns), BF16),
             jax.ShapeDtypeStruct((rows, 2, 3, chunk, height), BF16),
             jax.ShapeDtypeStruct((2, 2, SIDE, SIDE, width + PAD, height), BF16),
         ),
-        in_specs=[anywhere] * 3 + [near] * (1 + len(channelwise) + len(constants)),
-        out_specs=(near, anywhere, near),
+        in_specs=[anywhere] * 3 + [near] * (len(channelwise) + len(constants)),
+        out_specs=(anywhere, anywhere, near),
         scratch_shapes=[
             vmem((2, 4, height, half), BF16),
             vmem((2, SIDE, SIDE, 4, depth, columns), BF16),
             vmem((4, height, columns), BF16),
             vmem((4 * height, columns), F32),
             vmem((PLANE, 2, 2, width, height), BF16),
-            vmem((4, height, columns), BF16),
             vmem((4, height, columns), BF16),
             vmem((rows, 2, width, height), BF16),
             vmem((rows, 2, width, height), BF16),
@@ -762,12 +768,12 @@
             flops=16 * 10**9, bytes_accessed=32 * 2**20, transcendentals=0
         ),
         name="block",
-    )(grad, weight, gate, long, *channelwise, *constants)
+    )(grad, weight, gate, *channelwise, *constants)
 
 
 def unturn_kernel(
-    in_ref, lags_ref, medium_ref, eye_ref,
-    inner_out, input_out, filter_out, lags_out, short_out,
+    in_ref, lags_ref, medium_ref, hidden_ref, long_ref, eye_ref,
+    outer_out, inner_out, input_out, filter_out, lags_out, short_out,
 ):
     size, height = inner_out.shape[1], in_ref.shape[4]
     blocks = in_ref.shape[0]
@@ -776,6 +782,7 @@
     def lined(value):
         return dot_t(eye_ref[...], value.reshape(size, height))
 
+    outer_out[...] = (hidden_ref[0].astype(F32) * long_ref[...].astype(F32)).astype(BF16)
     inner_out[...] = (lined(in_ref[:, :, 0]) * medium_ref[...].astype(F32)).astype(BF16)
     filter_out[...] = lined(in_ref[:, :, 1])
     input_out[...] = lined(in_ref[:, :, 2]).astype(BF16)
@@ -789,9 +796,9 @@
     short_out[...] = short[:SHORT]
 
 
-def from_blocks(block, lags, medium_out):
+def from_blocks(block, lags, medium_out, hidden, long_out):
     devices, parts, items, chunk, height = block.shape
-    span = 8
+    span = devices // 4
     size = span * parts * chunk
     channels = devices * parts * chunk
     rows = pl.BlockSpec((height, size), lambda i: (0, i))
@@ -800,20 +807,22 @@
         unturn_kernel,
         grid=(devices // span,),
         out_shape=[
-            jax.ShapeDtypeStruct((height, channels), t) for t in (BF16, BF16, F32, F32)
+            jax.ShapeDtypeStruct((height, channels), t) for t in (BF16, BF16, BF16, F32, F32)
         ] + [jax.ShapeDtypeStruct((SHORT, channels), F32)],
         in_specs=[
             pl.BlockSpec((span, parts, items, chunk, height), lambda i: (i, 0, 0, 0, 0)),
             pl.BlockSpec((span, lags.shape[1], height), lambda i: (i, 0, 0)),
             rows,
+            pl.BlockSpec((1, height, size), lambda i: (i, 0, 0)),
+            rows,
             pl.BlockSpec((height, height), lambda i: (0, 0)),
         ],
-        out_specs=[rows] * 4 + [pl.BlockSpec((SHORT, size), lambda i: (0, i))],
+        out_specs=[rows] * 5 + [pl.BlockSpec((SHORT, size), lambda i: (0, i))],
         cost_estimate=pl.CostEstimate(
             flops=0, bytes_accessed=24 * height * channels, transcendentals=0
         ),
         name="from_blocks",
-    )(block, lags, medium_out, eye)
+    )(block, lags, medium_out, hidden, long_out, eye)
 
 
 def per_device(
@@ -823,16 +832,16 @@
     channels = outer_gate.shape[1]
     devices = lax.axis_size("seq")
     width = channels // devices
-    grad_outer, results, lags = block_call(
-        out_grad, out_weight, outer_gate, long_out,
+    hidden, results, lags = block_call(
+        out_grad, out_weight, outer_gate,
         (inner_gate, medium_out, short_out, conv_input, long_filter, taps_short, taps_medium),
         tables(devices),
     )
     lags = lags.reshape(devices, width + PAD, LANES)
-    grad_inner, grad_input, grad_filter, grad_medium, grad_short = from_blocks(
-        results, lags, medium_out
+    outer, inner, short, filt, medium_taps, short_taps = from_blocks(
+        results, lags, medium_out, hidden, long_out
     )
-    return grad_outer, grad_inner, grad_input, grad_filter, grad_short, grad_medium
+    return outer, inner, short, filt, short_taps, medium_taps
 
 
 def solution(mesh):

time: 122 us -> 116 us (0.951)
  Pallas kernels: 120 us -> 115 us
    pallas_call x1, Pallas kernels: 113 us -> 110 us  [block_call(): pl.pallas_call(block_kernel, out_shape=(jax.ShapeDtypeStruct((4, height,...]
    pallas_call x1, Pallas kernels: 6.86 us -> 5.01 us  [from_blocks(): pl.pallas_call(unturn_kernel, grid=(devices // span,), out_shape=[jax.Sha...]
where the time goes in v6:
time: 116 us
  Pallas kernels  115 us (99%)
    pallas_call x1, Pallas kernels, block_call(): pl.pallas_call(block_kernel, out_shape=(jax.ShapeDtypeStruct((4, height,...  110 us
    pallas_call x1, Pallas kernels, from_blocks(): pl.pallas_call(unturn_kernel, grid=(devices // span,), out_shape=[jax.Sha...  5.01 us

profile of v6, /device:TPU:1, one launch (start us, length us, event | category | flops | bytes accessed | tf_op | source)
XLA Modules:
  0.0 116.0 jit_solution(14647639187614301039)
XLA Ops:
  0.6 110.4 %block.1 = (bf16[4,128,512]{2,1,0:T(8,128)(2,1)}, bf16[64,2,3,16,128]{4,3,2,1,0:T(8,128)(2,1)}, bf16[2,2,4,4,48,128]{5,4,3,2,1,0:T(8,128)(2,1)}) custom-call(bf16[128,2048]{1,0:T(8,128)(2,1)} %grad_ref.1, bf16[32,4096]{1,0:T(8,128)(2,1)} %weight_ref.1, bf16[128,2048]{1,0:T(8,128)(2,1)} %gate_ref.1, bf16[128,2048]{1,0:T(8,128)(2,1)} %inner_ref.1, ...), custom_call_target="tpu_custom_call" | custom-call | flops 16000000000 | bytes 33554432 | tf_op jit(solution)/shard_map/block/pallas_call | solution.py:724
  111.0 5.0 %from_blocks.1 = (bf16[128,2048]{1,0:T(8,128)(2,1)}, bf16[128,2048]{1,0:T(8,128)(2,1)}, bf16[128,2048]{1,0:T(8,128)(2,1)}, f32[128,2048]{1,0:T(8,128)}, f32[128,2048]{1,0:T(8,128)}, /*index=5*/f32[7,2048]{1,0:T(8,128)}) custom-call(bf16[64,2,3,16,128]{4,3,2,1,0:T(8,128)(2,1)} %get-tuple-element.15.in_ref, bf16[64,48,128]{2,1,0:T(8,128)(2,1)} %bitcast.1, ...), custom_call_target="tpu_custom_call" | custom-call | bytes 6291456 | tf_op jit(solution)/shard_map/from_blocks/pallas_call | solution.py:806

commit v7 on v6

--- a/solution.py
+++ b/solution.py
@@ -188,7 +188,7 @@
     arrived, back_ref, lags_ref,
     feats, weights, gates, total, turned, hidden,
     one_out, one_in, two_out, two_in, three_out, three_in, late,
-    lines, zh, zl, gh, gl, spec, bands, taps, points, pairs, results, sums, parcels,
+    lines, zh, zl, gh, gl, spec, bands, taps, points, boths, pairs, results, sums, parcels,
     local, spread_s, spread_r, gate_s, gate_r, feat_s, feat_r, pass_s, pass_r,
     ring_s, ring_r, late_sem, hidden_s, hidden_r, batch_s, batch_r, lag_s, lag_r,
 ):
@@ -593,16 +593,13 @@
         exchange(3 + k, lambda seq, other: pair_of(parcels.at[seq], k), pair_of(back_ref.at[block], k))
 
     await_bytes(two_in, batch_r.at[1])
-    await_bytes(three_in, batch_r.at[2])
-
-    @pl.loop(0, rows // 4)
+
+    @pl.loop(0, rows // 8)
     def _(b):
-        for j in range(4):
-            i = 4 * b + j
+        for j in range(8):
+            i = 8 * b + j
             at = pl.ds(pl.multiple_of(i * width, width), width)
             lines[0, at, :] = two_in[i].astype(F32)
-            for k in range(2):
-                lines[1 + k, at, :] = three_in[i, k].astype(F32)
 
     def with_next(x):
         following = jnp.where(row == rows - 1, 0.0, pltpu.roll(x, rows - 1, 0))
@@ -624,9 +621,19 @@
             both = with_next((points[there, :] * gate).astype(BF16).astype(F32))
             short_grad = dot_t(both, bands[0, wide, :]).astype(BF16).astype(F32)
             pair = with_next(short_grad)
+            boths[there, :] = both
             pairs[there, :] = pair
-            diagonals(c, 0, both)
-            diagonals(c, 1, pair)
+
+    await_bytes(three_in, batch_r.at[2])
+    unpack(three_in, ((0, 1), (1, 2)))
+
+    @pl.loop(0, width // many)
+    def _(b):
+        for k in range(many):
+            c = b * many + k
+            there = pl.ds(pl.multiple_of(c * rows, rows), rows)
+            diagonals(c, 0, boths[there, :])
+            diagonals(c, 1, pairs[there, :])
 
     factor = (rows * LANES) ** -0.5
     lags = [pltpu.roll(sums[k], LANES + 1, 1)[:, :LANES] * factor for k in range(2)]
@@ -638,8 +645,13 @@
     def lag_send(i, ref, device):
         send(ref, ref, lag_s.at[i], lag_r.at[i], device)
 
-    for d in range(1, SIDE):
-        lag_send(d - 1, mine.at[here.x, here.z], here.at(x=wrap(here.x + d)))
+    own_lags = mine.at[here.x, here.z]
+    for dx in range(SIDE):
+        for dz in range(SIDE):
+            x, z = wrap(here.x + dx), wrap(here.z + dz)
+            lag_send(7, own_lags, here.at(y=near_y, x=x, z=z))
+            if dx or dz:
+                lag_send(dx - 1 if dx else 2 + dz, own_lags, here.at(x=x, z=z))
 
     def convolve(start):
         @pl.loop(0, chunk // many)
@@ -656,24 +668,19 @@
     for k in range(2):
         convolve(k * chunk)
         pack(k, (0,), (2,))
-        if k == 0:
-            for d in range(1, SIDE):
-                await_bytes(mine.at[wrap(here.x - d), here.z], lag_r.at[d - 1])
-            for d in range(1, SIDE):
-                lag_send(2 + d, mine.at[:, here.z], here.at(z=wrap(here.z + d)))
-        else:
-            for d in range(1, SIDE):
-                await_bytes(mine.at[:, wrap(here.z - d)], lag_r.at[2 + d])
-            lag_send(6, mine, here.at(y=near_y))
-            lag_send(7, mine, partner)
         exchange(5 + k, lambda seq, other: parcels.at[seq, k, 2], back_ref.at[block, k, 2])
 
     own.wait()
     for i, (dy, dc) in enumerate(share):
         await_bytes(arrived.at[sharer(dy, dc)[0]], hidden_r.at[i])
-    await_bytes(lags_ref.at[1 - here.y_lo, here.core], lag_r.at[6])
-    lag_send(8, lags_ref.at[1 - here.y_lo, here.core], partner)
-    await_bytes(lags_ref.at[here.y_lo, 1 - here.core], lag_r.at[7])
+    for d in range(1, SIDE):
+        await_bytes(mine.at[wrap(here.x - d)], lag_r.at[d - 1])
+        await_bytes(mine.at[here.x, wrap(here.z - d)], lag_r.at[2 + d])
+    lag_send(6, mine, partner)
+    across = lags_ref.at[1 - here.y_lo, here.core]
+    await_bytes(across, lag_r.at[7])
+    lag_send(8, across, partner)
+    await_bytes(lags_ref.at[here.y_lo, 1 - here.core], lag_r.at[6])
     await_bytes(lags_ref.at[1 - here.y_lo, 1 - here.core], lag_r.at[8])
 
     for k in range(2):
@@ -691,8 +698,8 @@
     for i in range(3):
         await_bytes(gates.at[me], gate_s.at[i])
         await_bytes(hidden.at[me], hidden_s.at[i])
-        await_bytes(mine.at[here.x, here.z], lag_s.at[i])
-        await_bytes(mine.at[:, here.z], lag_s.at[3 + i])
+        await_bytes(mine.at[here.x], lag_s.at[i])
+        await_bytes(own_lags, lag_s.at[3 + i])
         await_bytes(mine, lag_s.at[6 + i])
     for i in range(3):
         await_bytes(own_feat, pass_s.at[i])
@@ -754,6 +761,7 @@
             vmem((2, width, LANES), F32),
             vmem((area, height), F32),
             vmem((area, 2 * height), BF16),
+            vmem((area, 2 * height), BF16),
             vmem((2, area // 2, height), F32),
             vmem((2, width, 2 * LANES), F32),
             vmem((rows, 2, 3, chunk, height), BF16),

time: 116 us -> 111 us (0.957)
  Pallas kernels: 115 us -> 110 us
    pallas_call x1, Pallas kernels: 110 us -> 105 us  [block_call(): pl.pallas_call(block_kernel, out_shape=(jax.ShapeDtypeStruct((4, height,...]
where the time goes in v7:
time: 111 us
  Pallas kernels  110 us (99%)
    pallas_call x1, Pallas kernels, block_call(): pl.pallas_call(block_kernel, out_shape=(jax.ShapeDtypeStruct((4, height,...  105 us
    pallas_call x1, Pallas kernels, from_blocks(): pl.pallas_call(unturn_kernel, grid=(devices // span,), out_shape=[jax.Sha...  5.01 us

profile of v7, /device:TPU:1, one launch (start us, length us, event | category | flops | bytes accessed | tf_op | source)
XLA Modules:
  0.0 111.1 jit_solution(15888878916241325213)
XLA Ops:
  0.6 105.4 %block.1 = (bf16[4,128,512]{2,1,0:T(8,128)(2,1)}, bf16[64,2,3,16,128]{4,3,2,1,0:T(8,128)(2,1)}, bf16[2,2,4,4,48,128]{5,4,3,2,1,0:T(8,128)(2,1)}) custom-call(bf16[128,2048]{1,0:T(8,128)(2,1)} %grad_ref.1, bf16[32,4096]{1,0:T(8,128)(2,1)} %weight_ref.1, bf16[128,2048]{1,0:T(8,128)(2,1)} %gate_ref.1, bf16[128,2048]{1,0:T(8,128)(2,1)} %inner_ref.1, ...), custom_call_target="tpu_custom_call" | custom-call | flops 16000000000 | bytes 33554432 | tf_op jit(solution)/shard_map/block/pallas_call | solution.py:731
  106.1 5.0 %from_blocks.1 = (bf16[128,2048]{1,0:T(8,128)(2,1)}, bf16[128,2048]{1,0:T(8,128)(2,1)}, bf16[128,2048]{1,0:T(8,128)(2,1)}, f32[128,2048]{1,0:T(8,128)}, f32[128,2048]{1,0:T(8,128)}, /*index=5*/f32[7,2048]{1,0:T(8,128)}) custom-call(bf16[64,2,3,16,128]{4,3,2,1,0:T(8,128)(2,1)} %get-tuple-element.15.in_ref, bf16[64,48,128]{2,1,0:T(8,128)(2,1)} %bitcast.1, ...), custom_call_target="tpu_custom_call" | custom-call | bytes 6291456 | tf_op jit(solution)/shard_map/from_blocks/pallas_call | solution.py:814

commit v8 on v7

--- a/solution.py
+++ b/solution.py
@@ -355,7 +355,6 @@
     for pair in second[1:3]:
         for ring in pair:
             ring.start()
-    turn((plain(short_ref), into(three_out, 0)))
     for ring in second[0]:
         ring.relay()
     for ring in first:
@@ -363,7 +362,6 @@
     for ring in second[3]:
         ring.start()
     feat_relay(0)
-    turn((plain(conv_ref), into(three_out, 1)))
     feat_relay(1)
     pass_on(1, feat(near_y, here.core), feat(near_y, here.core))
 
@@ -424,7 +422,6 @@
             spec[at, :] = dot3(zh[at, :], zl[at, :], forward_ref[...])
 
     halves = area // step
-    transform_pairs(0, halves)
 
     other_core = 1 - here.core
     copies[1].wait()
@@ -476,6 +473,7 @@
             turned.at[x * SIDE + z], late.at[:, cell], late_sem.at[0], late_sem.at[1],
             here.at(x=x, z=z),
         )
+    turn((plain(short_ref), into(three_out, 0)), (plain(conv_ref), into(three_out, 1)))
     exchange(2, lambda seq, other: three_out.at[other], three_in.at[here.seq])
     for i, (dy, dc) in enumerate(share):
         index, device = sharer(dy, dc)
@@ -501,7 +499,7 @@
         for k in range(2):
             bands[k, wide, :] = toeplitz(taps[k, pl.ds(c, 1), :]).astype(BF16)
 
-    transform_pairs(halves, 2 * halves)
+    transform_pairs(0, 2 * halves)
     await_bytes(late, late_sem.at[1])
     for y_lo in range(2):
         @pl.loop(0, PLANE // 2)

time: 111 us -> 112 us (level)
  no operation moved by 1% of the time
where the time goes in v8:
time: 112 us
  Pallas kernels  111 us (99%)
    pallas_call x1, Pallas kernels, block_call(): pl.pallas_call(block_kernel, out_shape=(jax.ShapeDtypeStruct((4, height,...  106 us
    pallas_call x1, Pallas kernels, from_blocks(): pl.pallas_call(unturn_kernel, grid=(devices // span,), out_shape=[jax.Sha...  5.01 us

profile of v8, /device:TPU:1, one launch (start us, length us, event | category | flops | bytes accessed | tf_op | source)
XLA Modules:
  0.0 111.6 jit_solution(12988778726842183785)
XLA Ops:
  0.6 106.0 %block.1 = (bf16[4,128,512]{2,1,0:T(8,128)(2,1)}, bf16[64,2,3,16,128]{4,3,2,1,0:T(8,128)(2,1)}, bf16[2,2,4,4,48,128]{5,4,3,2,1,0:T(8,128)(2,1)}) custom-call(bf16[128,2048]{1,0:T(8,128)(2,1)} %grad_ref.1, bf16[32,4096]{1,0:T(8,128)(2,1)} %weight_ref.1, bf16[128,2048]{1,0:T(8,128)(2,1)} %gate_ref.1, bf16[128,2048]{1,0:T(8,128)(2,1)} %inner_ref.1, ...), custom_call_target="tpu_custom_call" | custom-call | flops 16000000000 | bytes 33554432 | tf_op jit(solution)/shard_map/block/pallas_call | solution.py:729
  106.6 5.0 %from_blocks.1 = (bf16[128,2048]{1,0:T(8,128)(2,1)}, bf16[128,2048]{1,0:T(8,128)(2,1)}, bf16[128,2048]{1,0:T(8,128)(2,1)}, f32[128,2048]{1,0:T(8,128)}, f32[128,2048]{1,0:T(8,128)}, /*index=5*/f32[7,2048]{1,0:T(8,128)}) custom-call(bf16[64,2,3,16,128]{4,3,2,1,0:T(8,128)(2,1)} %get-tuple-element.15.in_ref, bf16[64,48,128]{2,1,0:T(8,128)(2,1)} %bitcast.1, ...), custom_call_target="tpu_custom_call" | custom-call | bytes 6291456 | tf_op jit(solution)/shard_map/from_blocks/pallas_call | solution.py:812

commit v9 on v8

--- a/solution.py
+++ b/solution.py
@@ -355,6 +355,7 @@
     for pair in second[1:3]:
         for ring in pair:
             ring.start()
+    turn((plain(short_ref), into(three_out, 0)))
     for ring in second[0]:
         ring.relay()
     for ring in first:
@@ -362,6 +363,7 @@
     for ring in second[3]:
         ring.start()
     feat_relay(0)
+    turn((plain(conv_ref), into(three_out, 1)))
     feat_relay(1)
     pass_on(1, feat(near_y, here.core), feat(near_y, here.core))
 
@@ -473,7 +475,6 @@
             turned.at[x * SIDE + z], late.at[:, cell], late_sem.at[0], late_sem.at[1],
             here.at(x=x, z=z),
         )
-    turn((plain(short_ref), into(three_out, 0)), (plain(conv_ref), into(three_out, 1)))
     exchange(2, lambda seq, other: three_out.at[other], three_in.at[here.seq])
     for i, (dy, dc) in enumerate(share):
         index, device = sharer(dy, dc)

time: 112 us -> 113 us (level)
    pallas_call x1, Pallas kernels: 106 us -> 107 us  [block_call(): pl.pallas_call(block_kernel, out_shape=(jax.ShapeDtypeStruct((4, height,...]
where the time goes in v9:
time: 113 us
  Pallas kernels  112 us (99%)
    pallas_call x1, Pallas kernels, block_call(): pl.pallas_call(block_kernel, out_shape=(jax.ShapeDtypeStruct((4, height,...  107 us
    pallas_call x1, Pallas kernels, from_blocks(): pl.pallas_call(unturn_kernel, grid=(devices // span,), out_shape=[jax.Sha...  5.01 us

profile of v9, /device:TPU:1, one launch (start us, length us, event | category | flops | bytes accessed | tf_op | source)
XLA Modules:
  0.0 112.8 jit_solution(12569037933889605211)
XLA Ops:
  0.6 107.1 %block.1 = (bf16[4,128,512]{2,1,0:T(8,128)(2,1)}, bf16[64,2,3,16,128]{4,3,2,1,0:T(8,128)(2,1)}, bf16[2,2,4,4,48,128]{5,4,3,2,1,0:T(8,128)(2,1)}) custom-call(bf16[128,2048]{1,0:T(8,128)(2,1)} %grad_ref.1, bf16[32,4096]{1,0:T(8,128)(2,1)} %weight_ref.1, bf16[128,2048]{1,0:T(8,128)(2,1)} %gate_ref.1, bf16[128,2048]{1,0:T(8,128)(2,1)} %inner_ref.1, ...), custom_call_target="tpu_custom_call" | custom-call | flops 16000000000 | bytes 33554432 | tf_op jit(solution)/shard_map/block/pallas_call | solution.py:730
  107.8 5.0 %from_blocks.1 = (bf16[128,2048]{1,0:T(8,128)(2,1)}, bf16[128,2048]{1,0:T(8,128)(2,1)}, bf16[128,2048]{1,0:T(8,128)(2,1)}, f32[128,2048]{1,0:T(8,128)}, f32[128,2048]{1,0:T(8,128)}, /*index=5*/f32[7,2048]{1,0:T(8,128)}) custom-call(bf16[64,2,3,16,128]{4,3,2,1,0:T(8,128)(2,1)} %get-tuple-element.15.in_ref, bf16[64,48,128]{2,1,0:T(8,128)(2,1)} %bitcast.1, ...), custom_call_target="tpu_custom_call" | custom-call | bytes 6291456 | tf_op jit(solution)/shard_map/from_blocks/pallas_call | solution.py:813
